TPU v7x, 256 devices: a whole 4x4x8 slice. The times are simulated.
256 devices in a mesh: section: 16 (over x_hi, y, core), tm: 16 (over z, x_lo).
Axes of the slice: x: 4 (x_hi: 2, x_lo: 2; x = x_hi * 2 + x_lo), y: 4, z: 8, core: 2. Of those that a mesh axis runs over, the one named last changes fastest.
Arguments:
- fwd_input: bfloat16 [16, 2048, 1536], P('section', 'tm'), may hold values from -6 to 6
- saved_input: bfloat16 [16, 2048, 1536], P('section', 'tm'), may hold values from -6 to 6
- grad_in: bfloat16 [16, 2048, 1536], P('section', 'tm'), may hold values from -6 to 6
- gain: float32 [16, 1536], P('section'), may hold values from 0.25 to 1.75
- kernel: float32 [16, 31, 1536], P('section'), may hold values from -1 to 1
- w_out: bfloat16 [16, 1536, 1536], P('section', 'tm'), may hold values from -0.15625 to 0.15625
- lengths: int32 [32], replicated, may hold values from 1 to 2048, 49152 in all
- plan: int32 [16, 2], P('section'), may hold values from 0 to 31
Outputs:
- passed_activation: bfloat16 [16, 2048, 1536], P('section', 'tm')
- passed_gradient: bfloat16 [16, 2048, 1536], P('section', 'tm')
- weight_grad: float32 [16, 1536, 1536], P('section', 'tm')
- kernel_grad: float32 [16, 31, 1536], P('section')
- gain_grad: float32 [16, 1536], P('section')
Inputs may be any that keep to these rules, and one draw needn't show every extreme that they name: `lengths`: 32 valid counts summing to 49152, the largest exactly 2048. `plan`: indices into lengths.
All inputs are finite; a program needn't handle non-finite values.
Results may differ from a plain program's by a relative error of at most 0.017.
Values may be sent and summed in bfloat16 or wider, within the bound.
No kernel may reach another device: no remote copies, remote signals or barrier semaphores. Data moves between devices by JAX's collectives and lax.ppermute only.
A program may use at most 64 MiB of HBM per device.

v0:
```python
import functools

import jax
import jax.numpy as jnp
from jax import lax
from jax.experimental import pallas as pl
from jax.experimental.pallas import tpu as pltpu
from jax.sharding import Mesh
from jax.sharding import PartitionSpec as P


KW = 31
HALO = 16
LANES = 128
ROWS = 16


VMEM = pl.BlockSpec(memory_space=pltpu.VMEM)
SMEM = pl.BlockSpec(memory_space=pltpu.SMEM)
HBM = pl.BlockSpec(memory_space=pl.ANY)


def call(body, outs, in_specs, scratch=(), flops=0, size=0):
    return pl.pallas_call(
        body,
        out_shape=[jax.ShapeDtypeStruct(shape, kind) for shape, kind in outs],
        in_specs=in_specs,
        out_specs=[VMEM] * len(outs),
        scratch_shapes=list(scratch),
        compiler_params=pltpu.CompilerParams(vmem_limit_bytes=40 << 20),
        cost_estimate=pl.CostEstimate(flops=flops, bytes_accessed=size, transcendentals=0),
    )


def partner(array):
    return lax.ppermute(array, "x", [(0, 1), (1, 0)])


def from_behind(array, by):
    length = lax.axis_size("section")
    pairs = [(i, i + by) for i in range(length) if 0 <= i + by < length]
    return lax.ppermute(array, "section", pairs)


def divide(array, block):
    count = array.shape[1] // block
    pieces = [array[:, k * block : (k + 1) * block] for k in range(count)]
    return jnp.concatenate(pieces[0::2], axis=1), jnp.concatenate(pieces[1::2], axis=1)


def unite(even, odd, block):
    pieces = []
    for k in range(even.shape[1] // block):
        pieces += [even[:, k * block : (k + 1) * block], odd[:, k * block : (k + 1) * block]]
    return jnp.concatenate(pieces, axis=1)


def normalize(values):
    center = values - jnp.mean(values, axis=-1, keepdims=True)
    inverse = lax.rsqrt(jnp.mean(center * center, axis=-1, keepdims=True) + 1e-05)
    return (center * inverse, inverse)


def mask_of(start, length):
    return ((start + lax.broadcasted_iota(jnp.int32, (ROWS, 1), 0)) < length).astype(jnp.float32)


def conv_input(rows, gain_row, start, length):
    hat, _ = normalize(rows.astype(jnp.float32))
    return (hat * gain_row * mask_of(start, length)).astype(jnp.bfloat16)


def both(array, block, first):
    even, odd = divide(array, block)
    return jnp.where(first, even, odd), jnp.where(first, odd, even)


def enter_kernel(
    block, plan, lengths, where, saved_hbm, fwd_hbm, grad_hbm, gain, kernel,
    own, other, taps, edges, saved, fwd, sems,
):
    frames = saved.shape[0]
    side = where[0]
    first = side == 0
    wide = pl.ds(pl.multiple_of(side * (frames - 2 * HALO), HALO), 2 * HALO)
    thin = pl.ds(pl.multiple_of(side * (frames - HALO), HALO), HALO)
    copies = [
        pltpu.make_async_copy(saved_hbm, saved, sems.at[0]),
        pltpu.make_async_copy(fwd_hbm, fwd, sems.at[1]),
        pltpu.make_async_copy(grad_hbm.at[thin, :], edges.at[3 * HALO : 4 * HALO, :], sems.at[2]),
    ]
    for copy in copies:
        copy.start()
    taps[0:KW, :] = both(kernel[:, 0, :], block, first)[0]
    taps[KW : KW + 1, :] = jnp.zeros((1, taps.shape[1]), jnp.float32)
    origin = where[1] * 2 * frames
    fwd_len = lengths[plan[0, 0]]
    bwd_len = lengths[plan[0, 1]]
    gain_row = gain[...]

    def pass_over(source, offset, length):
        def body(i, carry):
            at = pl.multiple_of(i * ROWS, ROWS)
            start = origin + side * frames + at
            value = conv_input(source[pl.ds(at, ROWS), :], gain_row, start, length)
            mine, theirs = both(value, block, first)
            own[pl.ds(pl.multiple_of(at + offset, ROWS), ROWS), :] = mine
            other[pl.ds(pl.multiple_of(at + offset, ROWS), ROWS), :] = theirs
            return carry

        lax.fori_loop(0, frames // ROWS, body, 0)

    copies[0].wait()
    pass_over(saved, 0, bwd_len)
    copies[1].wait()
    pass_over(fwd, frames, fwd_len)
    edges[0 : 2 * HALO, :] = saved[wide, :]
    edges[2 * HALO : 3 * HALO, :] = fwd[thin, :]
    copies[2].wait()


def slide(buffer, chunk, start, count, weight):
    total = jnp.zeros((count, LANES), jnp.float32)
    for shift in range(8):
        tile = buffer[chunk, pl.ds(start + shift, count + 24), :]
        for step in range(4):
            offset = 8 * step + shift
            if 1 <= offset <= KW:
                total = total + weight(offset) * tile[8 * step : 8 * step + count]
    return total


def conv_kernel(
    block, plan, lengths, where, own, got, taps, grad, grad_got, near, far, gain,
    hidden_saved, hidden_own, hidden_other, slope, window, grad_window, fwd_window, halo,
):
    side = where[0]
    frames = grad.shape[0]
    mine = side * frames
    theirs = frames - mine
    chunks = own.shape[1] // LANES
    first = side == 0
    origin = where[1] * 2 * frames
    fwd_len = lengths[plan[0, 0]]
    bwd_len = lengths[plan[0, 1]]
    gain_row = gain[...]
    spots = (
        (0, 0, -2 * HALO, bwd_len, True),
        (HALO, HALO, -HALO, bwd_len, True),
        (2 * HALO, 4 * HALO, -HALO, fwd_len, True),
        (0, 2 * HALO, 2 * frames, bwd_len, False),
        (HALO, 3 * HALO, 2 * frames + HALO, bwd_len, False),
        (2 * HALO, 5 * HALO, 2 * frames, fwd_len, False),
    )
    for row, out_row, start, length, ahead in spots:
        pieces = near[row : row + ROWS, :], far[row : row + ROWS, :]
        rows = jnp.where(first == ahead, *pieces)
        value = conv_input(rows, gain_row, origin + start, length)
        halo[out_row : out_row + ROWS, :] = both(value, block, first)[0]

    grad_window[pl.ds(pl.multiple_of(HALO + mine, HALO), frames), :] = grad[...]
    grad_window[pl.ds(pl.multiple_of(HALO + theirs, HALO), frames), :] = grad_got[...]
    grad_window[0:HALO, :] = jnp.where(first, near[3 * HALO :, :], far[3 * HALO :, :])
    grad_window[HALO + 2 * frames :, :] = jnp.where(first, far[3 * HALO :, :], near[3 * HALO :, :])

    def body(chunk, carry):
        lanes = pl.ds(pl.multiple_of(chunk * LANES, LANES), LANES)

        def put(buffer, row, values):
            size = values.shape[0]
            if not isinstance(row, int):
                row = pl.multiple_of(row, 8)
            buffer[chunk, pl.ds(row, size), :] = values.astype(jnp.float32)

        put(window, 0, halo[0 : 2 * HALO, lanes])
        put(window, 2 * HALO + mine, own[0:frames, lanes])
        put(window, 2 * HALO + theirs, got[0:frames, lanes])
        put(window, 2 * HALO + 2 * frames, halo[2 * HALO : 4 * HALO, lanes])
        put(window, 4 * HALO + 2 * frames, jnp.zeros((8, LANES), jnp.float32))
        put(fwd_window, 0, halo[4 * HALO : 5 * HALO, lanes])
        put(fwd_window, HALO + mine, own[frames:, lanes])
        put(fwd_window, HALO + theirs, got[frames:, lanes])
        put(fwd_window, HALO + 2 * frames, halo[5 * HALO :, lanes])
        put(fwd_window, 2 * HALO + 2 * frames, jnp.zeros((8, LANES), jnp.float32))

        def weight(offset):
            return taps[offset - 1 : offset, lanes]

        span = frames + HALO
        for half in range(2):
            mixed = slide(window, chunk, half * span, span, weight)
            gate = jax.nn.sigmoid(mixed)
            hidden = mixed * gate
            slope[pl.ds(half * span, span), lanes] = gate + hidden * (1.0 - gate)
            keep = hidden[HALO:] if half == 0 else hidden[:frames]
            hidden_saved[pl.ds(half * frames, frames), lanes] = keep.astype(jnp.bfloat16)
        for half in range(2):
            mixed = slide(fwd_window, chunk, half * frames, frames, weight)
            hidden = (mixed * jax.nn.sigmoid(mixed)).astype(jnp.bfloat16)

            @pl.when(side == half)
            def _():
                hidden_own[:, lanes] = hidden

            @pl.when(side != half)
            def _():
                hidden_other[:, lanes] = hidden

        return carry

    lax.fori_loop(0, chunks, body, 0)


def back_kernel(
    factor, plan, lengths, where, hidden_grad, slope, window, taps,
    grad_own, grad_other, kernel_grad, conv_grad,
):
    side = where[0]
    frames = grad_own.shape[0]
    chunks = taps.shape[1] // LANES
    origin = where[1] * 2 * frames
    bwd_len = lengths[plan[0, 1]]

    def body(chunk, carry):
        lanes = pl.ds(pl.multiple_of(chunk * LANES, LANES), LANES)
        value = (hidden_grad[:, lanes] * slope[:, lanes]).astype(jnp.bfloat16).astype(jnp.float32)
        conv_grad[chunk, 0 : 2 * frames + 2 * HALO, :] = value
        conv_grad[chunk, 2 * frames + 2 * HALO :, :] = jnp.zeros((8, LANES), jnp.float32)

        def weight(offset):
            return taps[KW - offset : KW - offset + 1, lanes]

        for half in range(2):
            total = slide(conv_grad, chunk, half * frames, frames, weight)
            frame = origin + half * frames + lax.broadcasted_iota(jnp.int32, (frames, 1), 0)
            total = (total * (frame < bwd_len).astype(jnp.float32)).astype(jnp.bfloat16)

            @pl.when(side == half)
            def _():
                grad_own[:, lanes] = total

            @pl.when(side != half)
            def _():
                grad_other[:, lanes] = total

        for shift in range(8):
            sums = [jnp.zeros((8, LANES), jnp.float32) for _ in range(4)]
            for half in range(2):
                left = conv_grad[chunk, pl.ds(HALO + half * frames, frames), :]
                right = window[chunk, pl.ds(HALO + half * frames + shift, frames + 24), :]
                for step in range(4):
                    if 1 <= 8 * step + shift <= KW:
                        term = left * right[8 * step : 8 * step + frames]
                        sums[step] = sums[step] + jnp.sum(term.reshape(frames // 8, 8, LANES), axis=0)
            for step in range(4):
                tap = 8 * step + shift - 1
                if 0 <= tap < KW:
                    row = jnp.sum(sums[step], axis=0, keepdims=True) * factor
                    kernel_grad[tap : tap + 1, lanes] = row
        kernel_grad[KW : KW + 1, lanes] = jnp.zeros((1, LANES), jnp.float32)
        return carry

    lax.fori_loop(0, chunks, body, 0)


def leave_kernel(block, where, own, got, saved, grad, gain, out):
    first = where[0] == 0
    gain_row = gain[...]

    def body(i, carry):
        at = pl.ds(pl.multiple_of(i * ROWS, ROWS), ROWS)
        mine, theirs = own[at, :], got[at, :]
        even, odd = jnp.where(first, mine, theirs), jnp.where(first, theirs, mine)
        hat_grad = unite(even, odd, block).astype(jnp.float32) * gain_row
        hat, inverse = normalize(saved[at, :].astype(jnp.float32))
        back = grad[at, :].astype(jnp.float32) + inverse * (
            hat_grad
            - jnp.mean(hat_grad, axis=-1, keepdims=True)
            - hat * jnp.mean(hat_grad * hat, axis=-1, keepdims=True)
        )
        out[at, :] = back.astype(jnp.bfloat16)
        return carry

    lax.fori_loop(0, saved.shape[0] // ROWS, body, 0)


def totals_kernel(block, where, own, got, kernel, gain, kernel_out, gain_out):
    first = where[0] == 0
    mine, theirs = own[...], got[...]
    even, odd = jnp.where(first, mine, theirs), jnp.where(first, theirs, mine)
    total = unite(even.astype(jnp.float32), odd.astype(jnp.float32), block)[:KW]
    kernel_out[:, 0, :] = total
    gain_out[...] = jnp.sum(kernel[:, 0, :] * total, axis=0, keepdims=True) / gain[...]


def per_device(fwd_input, saved_input, grad_in, gain, kernel, w_out, lengths, plan):
    frames, width = fwd_input.shape[1:]
    depth = lax.axis_size("z")
    side = lax.axis_index("x")
    rows = w_out.shape[1]
    half = rows * depth
    pair = 2 * frames
    factor = float(pair * depth) ** (-0.5)
    fwd_rows = fwd_input[0]
    saved_rows = saved_input[0]
    upstream = grad_in[0]
    bf16, f32 = jnp.bfloat16, jnp.float32
    here = lax.axis_index("z")
    where = jnp.stack([side, here]).astype(jnp.int32)

    barrier = lax.optimization_barrier

    up = [(i, (i + 1) % depth) for i in range(depth)]
    down = [(j, i) for i, j in up]
    cut = rows // 2

    def ring(pair_of):
        return lax.ppermute(pair_of[0], "z", up), lax.ppermute(pair_of[1], "z", down)

    def spot(k):
        return jnp.where(here + k % depth < depth, here + k % depth, here + k % depth - depth) * rows

    def take(array, k):
        return lax.dynamic_slice_in_dim(array, spot(k), rows, axis=0)

    def put(array, piece, k, offset=0):
        return lax.dynamic_update_slice_in_dim(array, piece, spot(k) + offset, axis=0)

    grad_got = partner(upstream)
    block = w_out[0]
    round_1 = ring((block, block))
    tap_rows = jnp.transpose(kernel, (1, 0, 2))

    own, other, taps, edges = call(
        functools.partial(enter_kernel, rows),
        [((pair, half), bf16), ((pair, half), bf16), ((KW + 1, half), f32), ((4 * HALO, width), bf16)],
        [SMEM, SMEM, SMEM, HBM, HBM, HBM, VMEM, VMEM],
        [
            pltpu.VMEM((frames, width), bf16),
            pltpu.VMEM((frames, width), bf16),
            pltpu.SemaphoreType.DMA((3,)),
        ],
        flops=12 * 2 * frames * width,
        size=10 * frames * width,
    )(plan, lengths, where, saved_rows, fwd_rows, upstream, gain, tap_rows)
    got = partner(other)
    count = 2 * depth
    tm = ("z", "x")
    hops = [(t, t + 1 if t % 2 else t - 1) for t in range(count)]
    near = lax.ppermute(edges, tm, [(a, b) for a, b in hops if 0 <= b < count])
    hops = [(t, t + 2 if t % 2 else t - 2) for t in range(count)]
    far = lax.ppermute(edges, tm, [(a, b) for a, b in hops if 0 <= b < count])

    round_2 = ring(round_1)
    got, near, far, grad_got, round_2 = barrier((got, near, far, grad_got, round_2))
    round_3 = ring(round_2)
    hidden_saved, hidden_own, hidden_other, slope, window, grad_window = call(
        functools.partial(conv_kernel, rows),
        [
            ((pair, half), bf16),
            ((frames, half), bf16),
            ((frames, half), bf16),
            ((pair + 2 * HALO, half), f32),
            ((half // LANES, pair + 4 * HALO + 8, LANES), f32),
            ((pair + 2 * HALO, width), bf16),
        ],
        [SMEM, SMEM, SMEM] + [VMEM] * 8,
        [
            pltpu.VMEM((half // LANES, pair + 2 * HALO + 8, LANES), f32),
            pltpu.VMEM((6 * HALO, half), bf16),
        ],
        flops=2 * KW * 2 * pair * half,
        size=16 * pair * half,
    )(plan, lengths, where, own, got, taps, upstream, grad_got, near, far, gain)

    hidden_saved, round_3 = barrier((hidden_saved, round_3))
    round_4 = ring((round_3[0][:cut], round_3[1][cut:]))
    partial = (
        lax.dot_general(
            hidden_saved,
            grad_window[HALO : HALO + pair],
            (((0,), (0,)), ((), ())),
            preferred_element_type=f32,
        )
        * factor
    ).astype(bf16)
    partial = barrier(partial)

    def plus(arrived, own_part):
        return (arrived.astype(f32) + own_part.astype(f32)).astype(bf16)

    back_1 = ring((take(partial, depth // 2)[:cut], take(partial, depth // 2)[cut:]))

    w_half = jnp.zeros((half, width), bf16)
    w_half = put(w_half, block, 0)
    for k, (behind, ahead) in enumerate((round_1, round_2, round_3), 1):
        w_half = put(put(w_half, behind, -k), ahead, k)
    w_half = put(put(w_half, round_4[0], depth // 2), round_4[1], depth // 2, cut)

    hidden_grad = lax.dot_general(
        grad_window, w_half, (((1,), (1,)), ((), ())), preferred_element_type=f32
    )
    hidden_grad, back_1 = barrier((hidden_grad, back_1))
    ahead, behind = take(partial, depth // 2 - 1), take(partial, depth // 2 + 1)
    back_2 = ring(
        (
            jnp.concatenate([plus(back_1[0], ahead[:cut]), ahead[cut:]]),
            jnp.concatenate([behind[:cut], plus(back_1[1], behind[cut:])]),
        )
    )
    norm_own, norm_other, kernel_local = call(
        functools.partial(back_kernel, factor),
        [((frames, half), bf16), ((frames, half), bf16), ((KW + 1, half), f32)],
        [SMEM, SMEM, SMEM] + [VMEM] * 4,
        [pltpu.VMEM((half // LANES, pair + 2 * HALO + 8, LANES), f32)],
        flops=4 * KW * pair * half,
        size=12 * pair * half,
    )(plan, lengths, where, hidden_grad, slope, window, taps)
    norm_got = partner(norm_other)
    total = kernel_local.astype(bf16)
    step = 1
    while step < depth:
        arrived = lax.ppermute(total, "z", [(i, i ^ step) for i in range(depth)])
        total = (total.astype(f32) + arrived.astype(f32)).astype(bf16)
        step *= 2
    total_got = partner(total)

    back_3 = ring((plus(back_2[0], take(partial, 2)), plus(back_2[1], take(partial, -2))))
    back_4 = ring((plus(back_3[0], take(partial, 1)), plus(back_3[1], take(partial, -1))))
    weight_grad = back_4[0].astype(f32) + back_4[1].astype(f32) + take(partial, 0).astype(f32)

    product_got = partner(jnp.dot(hidden_other, w_half, preferred_element_type=f32).astype(bf16))
    output = (
        fwd_rows.astype(f32)
        + (jnp.dot(hidden_own, w_half, preferred_element_type=f32) + product_got.astype(f32))
    ).astype(bf16)
    passed_activation = from_behind(output[None], 1)

    (input_back,) = call(
        functools.partial(leave_kernel, rows),
        [((frames, width), bf16)],
        [SMEM] + [VMEM] * 5,
        flops=20 * frames * width,
        size=8 * frames * width,
    )(where, norm_own, norm_got, saved_rows, upstream, gain)
    passed_gradient = from_behind(input_back[None], -1)
    kernel_grad, gain_grad = call(
        functools.partial(totals_kernel, rows),
        [((KW, 1, width), f32), ((1, width), f32)],
        [SMEM] + [VMEM] * 4,
        flops=4 * KW * width,
        size=12 * KW * width,
    )(where, total, total_got, tap_rows, gain)
    return (
        passed_activation,
        passed_gradient,
        weight_grad[None],
        jnp.transpose(kernel_grad, (1, 0, 2)),
        gain_grad,
    )


def solution(mesh):
    sections, pieces = mesh.devices.shape
    folded = Mesh(mesh.devices.reshape(sections, pieces // 2, 2), ("section", "z", "x"))
    split = P("section", ("z", "x"), None)
    placed = (
        split,
        split,
        split,
        P("section", None),
        P("section", None, None),
        split,
        P(),
        P("section", None),
    )

    return jax.shard_map(
        per_device,
        mesh=folded,
        in_specs=placed,
        out_specs=(split, split, split, P("section", None, None), P("section", None)),
        check_vma=False,
    )
```

profile of v0, /device:TPU:1, one launch (start us, length us, event | category | flops | bytes accessed | tf_op | source)
XLA Modules:
  0.0 109.7 jit_solution(5878772114849970838)
XLA Ops:
  0.6 2.5 %collective-permute-start.4 = (bf16[96,1536]{1,0:T(8,128)(2,1)}, bf16[96,1536]{1,0:T(8,128)(2,1)S(1)}, u32[]{:S(2)}, u32[]{:S(2)}) collective-permute-start(bf16[96,1536]{1,0:T(8,128)(2,1)} %bitcast.32), channel_id=1, source_target_pairs={{0,2},{2,4},{4,6},{6,8},{8,10},{10,12},{12,14},{14,0},{1,3},{3,5},... | collective-permute-start | bytes 884744 | tf_op jit(solution)/shard_map/ppermute | solution.py:318
  3.2 4.0 %collective-permute-start.6 = (bf16[96,1536]{1,0:T(8,128)(2,1)}, bf16[96,1536]{1,0:T(8,128)(2,1)S(1)}, u32[]{:S(2)}, u32[]{:S(2)}) collective-permute-start(bf16[96,1536]{1,0:T(8,128)(2,1)} %bitcast.33), channel_id=1, source_target_pairs={{2,0},{4,2},{6,4},{8,6},{10,8},{12,10},{14,12},{0,14},{3,1},{5,3},... | collective-permute-start | bytes 884744 | tf_op jit(solution)/shard_map/ppermute | solution.py:318
  14.4 5.7 %shard_map.119 = (bf16[256,768]{1,0:T(8,128)(2,1)S(1)}, bf16[256,768]{1,0:T(8,128)(2,1)S(1)}, f32[32,768]{1,0:T(8,128)S(1)}, bf16[64,1536]{1,0:T(8,128)(2,1)S(1)}) custom-call(s32[1,2]{1,0:T(1,128)S(1)} %copy-done.10, s32[32]{0:T(128)S(1)} %copy-done.12, s32[2]{0:T(128)S(1)} %pad_add_fusion.where, bf16[128,1536]{1,0:T(8,128)(2,1)S(1)} %bitcast.27, ...), custom_call_target="tpu_custom_call" | custom-call | flops 4718592 | bytes 1966080 | tf_op jit(solution)/shard_map/pallas_call | solution.py:334
  20.7 1.6 %collective-permute-start = (bf16[256,768]{1,0:T(8,128)(2,1)S(1)}, bf16[256,768]{1,0:T(8,128)(2,1)S(1)}, u32[]{:S(2)}, u32[]{:S(2)}) collective-permute-start(bf16[256,768]{1,0:T(8,128)(2,1)S(1)} %get-tuple-element.33), channel_id=1, source_target_pairs={{0,1},{1,0},{2,3},{3,2},{4,5},{5,4},{6,7},{7,6},{8,9},{9,8},{10,11... | collective-permute-start | bytes 1179656 | tf_op jit(solution)/shard_map/ppermute | solution.py:36
  22.6 1.4 %collective-permute-start.5 = (bf16[96,1536]{1,0:T(8,128)(2,1)S(1)}, bf16[96,1536]{1,0:T(8,128)(2,1)S(1)}, u32[]{:S(2)}, u32[]{:S(2)}) collective-permute-start(bf16[96,1536]{1,0:T(8,128)(2,1)S(1)} %collective-permute-done.4), channel_id=1, source_target_pairs={{0,2},{2,4},{4,6},{6,8},{8,10},{10,12},{12,14},{14,0},{1,3},{3,5},... | collective-permute-start | bytes 884744 | tf_op jit(solution)/shard_map/ppermute | solution.py:318
  26.7 11.1 %collective-permute-done.2.far = bf16[64,1536]{1,0:T(8,128)(2,1)S(1)} collective-permute-done((bf16[64,1536]{1,0:T(8,128)(2,1)S(1)}, bf16[64,1536]{1,0:T(8,128)(2,1)S(1)}, u32[]{:S(2)}, u32[]{:S(2)}) %collective-permute-start.2) | collective-permute-done | bytes 196640 | tf_op jit(solution)/shard_map/ppermute | solution.py:352
  37.9 2.7 %collective-permute-start.9 = (bf16[96,1536]{1,0:T(8,128)(2,1)S(1)}, bf16[96,1536]{1,0:T(8,128)(2,1)S(1)}, u32[]{:S(2)}, u32[]{:S(2)}) collective-permute-start(bf16[96,1536]{1,0:T(8,128)(2,1)S(1)} %collective-permute-done.7), channel_id=1, source_target_pairs={{2,0},{4,2},{6,4},{8,6},{10,8},{12,10},{14,12},{0,14},{3,1},{5,3},... | collective-permute-start | bytes 884744 | tf_op jit(solution)/shard_map/ppermute | solution.py:318
  40.6 5.2 %shard_map.120 = (bf16[256,768]{1,0:T(8,128)(2,1)S(1)}, bf16[128,768]{1,0:T(8,128)(2,1)S(1)}, bf16[128,768]{1,0:T(8,128)(2,1)S(1)}, f32[288,768]{1,0:T(8,128)S(1...) custom-call(s32[1,2]{1,0:T(1,128)S(1)} %copy-done.11, s32[32]{0:T(128)S(1)} %copy-done.13, ...), custom_call_target="tpu_custom_call" | custom-call | flops 24379392 | bytes 3145728 | tf_op jit(solution)/shard_map/pallas_call | solution.py:357
  46.0 2.7 %collective-permute-start.11 = (bf16[48,1536]{1,0:T(8,128)(2,1)S(1)}, bf16[48,1536]{1,0:T(8,128)(2,1)S(1)}, u32[]{:S(2)}, u32[]{:S(2)}) collective-permute-start(bf16[48,1536]{1,0:T(8,128)(2,1)S(1)} %slice.28), channel_id=1, source_target_pairs={{2,0},{4,2},{6,4},{8,6},{10,8},{12,10},{14,12},{0,14},{3,1},{5,3},... | collective-permute-start | bytes 442376 | tf_op jit(solution)/shard_map/ppermute | solution.py:318
  49.7 2.7 %collective-permute-start.15 = (bf16[48,1536]{1,0:T(8,128)(2,1)S(1)}, bf16[48,1536]{1,0:T(8,128)(2,1)S(1)}, u32[]{:S(2)}, u32[]{:S(2)}) collective-permute-start(bf16[48,1536]{1,0:T(8,128)(2,1)S(1)} %get-tuple-element.68), channel_id=1, source_target_pairs={{2,0},{4,2},{6,4},{8,6},{10,8},{12,10},{14,12},{0,14},{3,1},{5,3},... | collective-permute-start | bytes 442376 | tf_op jit(solution)/shard_map/ppermute | solution.py:318
  53.4 2.5 %collective-permute-done.14 = bf16[48,1536]{1,0:T(8,128)(2,1)S(1)} collective-permute-done((bf16[48,1536]{1,0:T(8,128)(2,1)S(1)}, bf16[48,1536]{1,0:T(8,128)(2,1)S(1)}, u32[]{:S(2)}, u32[]{:S(2)}) %collective-permute-start.14) | collective-permute-done | bytes 147488 | tf_op jit(solution)/shard_map/ppermute | solution.py:318
  55.9 4.6 %shard_map.121 = (bf16[128,768]{1,0:T(8,128)(2,1)S(1)}, bf16[128,768]{1,0:T(8,128)(2,1)S(1)}, f32[32,768]{1,0:T(8,128)S(1)}) custom-call(s32[1,2]{1,0:T(1,128)S(1)} %copy-done.11, s32[32]{0:T(128)S(1)} %copy-done.13, s32[2]{0:T(128)S(1)} %pad_add_fusion.where, f32[288,768]{1,0:T(8,128)S(1)} %fusion.4.hidden_grad, f32[288,768]{1,0:T(8,128)S(1)} %get-tuple-element.50.slope, ...), custom_call_target="tpu_custom_call" | custom-call | flops 24379392 | bytes 2359296 | tf_op jit(solution)/shard_map/pallas_call | solution.py:411
  60.7 3.2 %collective-permute-start.21 = (bf16[96,1536]{1,0:T(8,128)(2,1)S(1)}, bf16[96,1536]{1,0:T(8,128)(2,1)S(1)}, u32[]{:S(2)}, u32[]{:S(2)}) collective-permute-start(bf16[96,1536]{1,0:T(8,128)(2,1)S(1)} %pad_maximum_fusion.1), channel_id=1, source_target_pairs={{2,0},{4,2},{6,4},{8,6},{10,8},{12,10},{14,12},{0,14},{3,1},{5,3},... | collective-permute-start | bytes 884744 | tf_op jit(solution)/shard_map/ppermute | solution.py:318
  64.6 1.5 %collective-permute-start.12 = (bf16[128,1536]{1,0:T(8,128)(2,1)S(1)}, bf16[128,1536]{1,0:T(8,128)(2,1)S(1)}, u32[]{:S(2)}, u32[]{:S(2)}) collective-permute-start(bf16[128,1536]{1,0:T(8,128)(2,1)S(1)} %convolution_convert_fusion), channel_id=1, source_target_pairs={{0,1},{1,0},{2,3},{3,2},{4,5},{5,4},{6,7},{7,6},{8,9},{9,8},{10,11... | collective-permute-start | bytes 1179656 | tf_op jit(solution)/shard_map/ppermute | solution.py:36
  66.2 4.3 %collective-permute-start.25 = (bf16[32,768]{1,0:T(8,128)(2,1)S(1)}, bf16[32,768]{1,0:T(8,128)(2,1)S(1)}, u32[]{:S(2)}, u32[]{:S(2)}) collective-permute-start(bf16[32,768]{1,0:T(8,128)(2,1)S(1)} %add_convert_fusion.8), channel_id=1, source_target_pairs={{0,4},{2,6},{4,0},{6,2},{8,12},{10,14},{12,8},{14,10},{1,5},{3,7},... | collective-permute-start | bytes 147464 | tf_op jit(solution)/shard_map/ppermute | solution.py:423
  72.0 1.7 %collective-permute-start.22 = (bf16[96,1536]{1,0:T(8,128)(2,1)S(1)}, bf16[96,1536]{1,0:T(8,128)(2,1)S(1)}, u32[]{:S(2)}, u32[]{:S(2)}) collective-permute-start(bf16[96,1536]{1,0:T(8,128)(2,1)S(1)} %get-tuple-element.62), channel_id=1, source_target_pairs={{2,0},{4,2},{6,4},{8,6},{10,8},{12,10},{14,12},{0,14},{3,1},{5,3},... | collective-permute-start | bytes 884744 | tf_op jit(solution)/shard_map/ppermute | solution.py:318
  73.7 2.2 %collective-permute-start.26 = (bf16[32,768]{1,0:T(8,128)(2,1)S(1)}, bf16[32,768]{1,0:T(8,128)(2,1)S(1)}, u32[]{:S(2)}, u32[]{:S(2)}) collective-permute-start(bf16[32,768]{1,0:T(8,128)(2,1)S(1)} %add_convert_fusion.7), channel_id=1, source_target_pairs={{0,8},{2,10},{4,12},{6,14},{8,0},{10,2},{12,4},{14,6},{1,9},{3,11}... | collective-permute-start | bytes 147464 | tf_op jit(solution)/shard_map/ppermute | solution.py:423
  75.9 2.9 %shard_map.122 = bf16[128,1536]{1,0:T(8,128)(2,1)S(1)} custom-call(s32[2]{0:T(128)S(1)} %pad_add_fusion.where, bf16[128,768]{1,0:T(8,128)(2,1)S(1)} %get-tuple-element.52.own, bf16[128,768]{1,0:T(8,128)(2,1)S(1)} %collective-permute-done.16.got, bf16[128,1536]{1,0:T(8,128)(2,1)S(1)} %bitcast.28, bf16[128,1536]{1,0:T(8,128)(2,1)S(1)} %bitcast.25, ...), custom_call_target="tpu_custom_call" | custom-call | flops 3932160 | bytes 1572864 | tf_op jit(solution)/shard_map/pallas_call | solution.py:439
  78.9 14.7 %collective-permute-start.17 = (bf16[1,128,1536]{2,1,0:T(8,128)(2,1)S(1)}, bf16[1,128,1536]{2,1,0:T(8,128)(2,1)S(1)}, u32[]{:S(2)}, u32[]{:S(2)}) collective-permute-start(bf16[1,128,1536]{2,1,0:T(8,128)(2,1)S(1)} %bitcast.31), channel_id=1, source_target_pairs={{16,0},{32,16},{48,32},{64,48},{80,64},{96,80},{112,96},{128,112},... | collective-permute-start | bytes 1179656 | tf_op jit(solution)/shard_map/ppermute | solution.py:42
  94.1 3.1 %collective-permute-start.13 = (bf16[1,128,1536]{2,1,0:T(8,128)(2,1)S(1)}, bf16[1,128,1536]{2,1,0:T(8,128)(2,1)S(1)}, u32[]{:S(2)}, u32[]{:S(2)}) collective-permute-start(bf16[1,128,1536]{2,1,0:T(8,128)(2,1)S(1)} %fusion.2), channel_id=1, source_target_pairs={{0,16},{16,32},{32,48},{48,64},{64,80},{80,96},{96,112},{112,128},... | collective-permute-start | bytes 1179656 | tf_op jit(solution)/shard_map/ppermute | solution.py:42
  97.5 2.7 %collective-permute-start.23 = (bf16[96,1536]{1,0:T(8,128)(2,1)S(1)}, bf16[96,1536]{1,0:T(8,128)(2,1)S(1)}, u32[]{:S(2)}, u32[]{:S(2)}) collective-permute-start(bf16[96,1536]{1,0:T(8,128)(2,1)S(1)} %get-tuple-element.60), channel_id=1, source_target_pairs={{2,0},{4,2},{6,4},{8,6},{10,8},{12,10},{14,12},{0,14},{3,1},{5,3},... | collective-permute-start | bytes 884744 | tf_op jit(solution)/shard_map/ppermute | solution.py:318
  100.2 3.4 %collective-permute-done.27.got = bf16[32,768]{1,0:T(8,128)(2,1)S(1)} collective-permute-done((bf16[32,768]{1,0:T(8,128)(2,1)S(1)}, bf16[32,768]{1,0:T(8,128)(2,1)S(1)}, u32[]{:S(2)}, u32[]{:S(2)}) %collective-permute-start.27) | collective-permute-done | bytes 49184 | tf_op jit(solution)/shard_map/ppermute | solution.py:36
  103.6 1.4 %shard_map.123 = (f32[31,1,1536]{2,1,0:T(1,128)}, f32[1,1536]{1,0:T(1,128)}) custom-call(s32[2]{0:T(128)S(1)} %pad_add_fusion.where, bf16[32,768]{1,0:T(8,128)(2,1)S(1)} %add_convert_fusion.6.own, bf16[32,768]{1,0:T(8,128)(2,1)S(1)} %collective-permute-done.27.got, f32[31,1,1536]{2,1,0:T(1,128)S(1)} %bitcast.30, f32[1,1536]{1,0:T(1,128)S(1)} %copy-done.9), custom_call_target="tpu_custom_call" | custom-call | flops 190464 | bytes 571392 | tf_op jit(solution)/shard_map/pallas_call | solution.py:447
  105.0 2.2 %collective-permute-done.20 = bf16[96,1536]{1,0:T(8,128)(2,1)S(1)} collective-permute-done((bf16[96,1536]{1,0:T(8,128)(2,1)S(1)}, bf16[96,1536]{1,0:T(8,128)(2,1)S(1)}, u32[]{:S(2)}, u32[]{:S(2)}) %collective-permute-start.20) | collective-permute-done | bytes 294944 | tf_op jit(solution)/shard_map/ppermute | solution.py:318
  (97 shorter events, 18.7 us)
Async XLA Ops:
  0.6 21.9 %collective-permute-start.4 = (bf16[96,1536]{1,0:T(8,128)(2,1)}, bf16[96,1536]{1,0:T(8,128)(2,1)S(1)}, u32[]{:S(2)}, u32[]{:S(2)}) collective-permute-start(bf16[96,1536]{1,0:T(8,128)(2,1)} %bitcast.32), channel_id=1, source_target_pairs={{0,2},{2,4},{4,6},{6,8},{8,10},{10,12},{12,14},{14,0},{1,3},{3,5},... | collective-permute-start | bytes 884744 | tf_op jit(solution)/shard_map/ppermute | solution.py:318
  3.2 20.8 %collective-permute-start.6 = (bf16[96,1536]{1,0:T(8,128)(2,1)}, bf16[96,1536]{1,0:T(8,128)(2,1)S(1)}, u32[]{:S(2)}, u32[]{:S(2)}) collective-permute-start(bf16[96,1536]{1,0:T(8,128)(2,1)} %bitcast.33), channel_id=1, source_target_pairs={{2,0},{4,2},{6,4},{8,6},{10,8},{12,10},{14,12},{0,14},{3,1},{5,3},... | collective-permute-start | bytes 884744 | tf_op jit(solution)/shard_map/ppermute | solution.py:318
  7.2 30.6 %collective-permute-start.3 = (bf16[128,1536]{1,0:T(8,128)(2,1)}, bf16[128,1536]{1,0:T(8,128)(2,1)S(1)}, u32[]{:S(2)}, u32[]{:S(2)}) collective-permute-start(bf16[128,1536]{1,0:T(8,128)(2,1)} %bitcast.22), channel_id=1, source_target_pairs={{0,1},{1,0},{2,3},{3,2},{4,5},{5,4},{6,7},{7,6},{8,9},{9,8},{10,11... | collective-permute-start | bytes 1179656 | tf_op jit(solution)/shard_map/ppermute | solution.py:36
  20.7 17.0 %collective-permute-start = (bf16[256,768]{1,0:T(8,128)(2,1)S(1)}, bf16[256,768]{1,0:T(8,128)(2,1)S(1)}, u32[]{:S(2)}, u32[]{:S(2)}) collective-permute-start(bf16[256,768]{1,0:T(8,128)(2,1)S(1)} %get-tuple-element.33), channel_id=1, source_target_pairs={{0,1},{1,0},{2,3},{3,2},{4,5},{5,4},{6,7},{7,6},{8,9},{9,8},{10,11... | collective-permute-start | bytes 1179656 | tf_op jit(solution)/shard_map/ppermute | solution.py:36
  22.6 15.2 %collective-permute-start.5 = (bf16[96,1536]{1,0:T(8,128)(2,1)S(1)}, bf16[96,1536]{1,0:T(8,128)(2,1)S(1)}, u32[]{:S(2)}, u32[]{:S(2)}) collective-permute-start(bf16[96,1536]{1,0:T(8,128)(2,1)S(1)} %collective-permute-done.4), channel_id=1, source_target_pairs={{0,2},{2,4},{4,6},{6,8},{8,10},{10,12},{12,14},{14,0},{1,3},{3,5},... | collective-permute-start | bytes 884744 | tf_op jit(solution)/shard_map/ppermute | solution.py:318
  23.9 13.8 %collective-permute-start.7 = (bf16[96,1536]{1,0:T(8,128)(2,1)S(1)}, bf16[96,1536]{1,0:T(8,128)(2,1)S(1)}, u32[]{:S(2)}, u32[]{:S(2)}) collective-permute-start(bf16[96,1536]{1,0:T(8,128)(2,1)S(1)} %collective-permute-done.6), channel_id=1, source_target_pairs={{2,0},{4,2},{6,4},{8,6},{10,8},{12,10},{14,12},{0,14},{3,1},{5,3},... | collective-permute-start | bytes 884744 | tf_op jit(solution)/shard_map/ppermute | solution.py:318
  25.4 12.4 %collective-permute-start.2 = (bf16[64,1536]{1,0:T(8,128)(2,1)S(1)}, bf16[64,1536]{1,0:T(8,128)(2,1)S(1)}, u32[]{:S(2)}, u32[]{:S(2)}) collective-permute-start(bf16[64,1536]{1,0:T(8,128)(2,1)S(1)} %get-tuple-element.34), channel_id=1, source_target_pairs={{1,3},{2,0},{3,5},{4,2},{5,7},{6,4},{7,9},{8,6},{9,11},{10,8},{11,... | collective-permute-start | bytes 589832 | tf_op jit(solution)/shard_map/ppermute | solution.py:352
  37.8 8.1 %collective-permute-start.8 = (bf16[96,1536]{1,0:T(8,128)(2,1)S(1)}, bf16[96,1536]{1,0:T(8,128)(2,1)S(1)}, u32[]{:S(2)}, u32[]{:S(2)}) collective-permute-start(bf16[96,1536]{1,0:T(8,128)(2,1)S(1)} %collective-permute-done.5), channel_id=1, source_target_pairs={{0,2},{2,4},{4,6},{6,8},{8,10},{10,12},{12,14},{14,0},{1,3},{3,5},... | collective-permute-start | bytes 884744 | tf_op jit(solution)/shard_map/ppermute | solution.py:318
  37.9 8.0 %collective-permute-start.9 = (bf16[96,1536]{1,0:T(8,128)(2,1)S(1)}, bf16[96,1536]{1,0:T(8,128)(2,1)S(1)}, u32[]{:S(2)}, u32[]{:S(2)}) collective-permute-start(bf16[96,1536]{1,0:T(8,128)(2,1)S(1)} %collective-permute-done.7), channel_id=1, source_target_pairs={{2,0},{4,2},{6,4},{8,6},{10,8},{12,10},{14,12},{0,14},{3,1},{5,3},... | collective-permute-start | bytes 884744 | tf_op jit(solution)/shard_map/ppermute | solution.py:318
  45.9 6.5 %collective-permute-start.10 = (bf16[48,1536]{1,0:T(8,128)(2,1)S(1)}, bf16[48,1536]{1,0:T(8,128)(2,1)S(1)}, u32[]{:S(2)}, u32[]{:S(2)}) collective-permute-start(bf16[48,1536]{1,0:T(8,128)(2,1)S(1)} %slice.27), channel_id=1, source_target_pairs={{0,2},{2,4},{4,6},{6,8},{8,10},{10,12},{12,14},{14,0},{1,3},{3,5},... | collective-permute-start | bytes 442376 | tf_op jit(solution)/shard_map/ppermute | solution.py:318
  46.0 6.4 %collective-permute-start.11 = (bf16[48,1536]{1,0:T(8,128)(2,1)S(1)}, bf16[48,1536]{1,0:T(8,128)(2,1)S(1)}, u32[]{:S(2)}, u32[]{:S(2)}) collective-permute-start(bf16[48,1536]{1,0:T(8,128)(2,1)S(1)} %slice.28), channel_id=1, source_target_pairs={{2,0},{4,2},{6,4},{8,6},{10,8},{12,10},{14,12},{0,14},{3,1},{5,3},... | collective-permute-start | bytes 442376 | tf_op jit(solution)/shard_map/ppermute | solution.py:318
  49.6 6.2 %collective-permute-start.14 = (bf16[48,1536]{1,0:T(8,128)(2,1)S(1)}, bf16[48,1536]{1,0:T(8,128)(2,1)S(1)}, u32[]{:S(2)}, u32[]{:S(2)}) collective-permute-start(bf16[48,1536]{1,0:T(8,128)(2,1)S(1)} %get-tuple-element.67), channel_id=1, source_target_pairs={{0,2},{2,4},{4,6},{6,8},{8,10},{10,12},{12,14},{14,0},{1,3},{3,5},... | collective-permute-start | bytes 442376 | tf_op jit(solution)/shard_map/ppermute | solution.py:318
  60.7 9.8 %collective-permute-start.21 = (bf16[96,1536]{1,0:T(8,128)(2,1)S(1)}, bf16[96,1536]{1,0:T(8,128)(2,1)S(1)}, u32[]{:S(2)}, u32[]{:S(2)}) collective-permute-start(bf16[96,1536]{1,0:T(8,128)(2,1)S(1)} %pad_maximum_fusion.1), channel_id=1, source_target_pairs={{2,0},{4,2},{6,4},{8,6},{10,8},{12,10},{14,12},{0,14},{3,1},{5,3},... | collective-permute-start | bytes 884744 | tf_op jit(solution)/shard_map/ppermute | solution.py:318
  63.9 6.9 %collective-permute-start.18 = (bf16[96,1536]{1,0:T(8,128)(2,1)S(1)}, bf16[96,1536]{1,0:T(8,128)(2,1)S(1)}, u32[]{:S(2)}, u32[]{:S(2)}) collective-permute-start(bf16[96,1536]{1,0:T(8,128)(2,1)S(1)} %pad_maximum_fusion), channel_id=1, source_target_pairs={{0,2},{2,4},{4,6},{6,8},{8,10},{10,12},{12,14},{14,0},{1,3},{3,5},... | collective-permute-start | bytes 884744 | tf_op jit(solution)/shard_map/ppermute | solution.py:318
  64.0 11.9 %collective-permute-start.16 = (bf16[128,768]{1,0:T(8,128)(2,1)S(1)}, bf16[128,768]{1,0:T(8,128)(2,1)S(1)}, u32[]{:S(2)}, u32[]{:S(2)}) collective-permute-start(bf16[128,768]{1,0:T(8,128)(2,1)S(1)} %get-tuple-element.53), channel_id=1, source_target_pairs={{0,1},{1,0},{2,3},{3,2},{4,5},{5,4},{6,7},{7,6},{8,9},{9,8},{10,11... | collective-permute-start | bytes 589832 | tf_op jit(solution)/shard_map/ppermute | solution.py:36
  64.6 28.9 %collective-permute-start.12 = (bf16[128,1536]{1,0:T(8,128)(2,1)S(1)}, bf16[128,1536]{1,0:T(8,128)(2,1)S(1)}, u32[]{:S(2)}, u32[]{:S(2)}) collective-permute-start(bf16[128,1536]{1,0:T(8,128)(2,1)S(1)} %convolution_convert_fusion), channel_id=1, source_target_pairs={{0,1},{1,0},{2,3},{3,2},{4,5},{5,4},{6,7},{7,6},{8,9},{9,8},{10,11... | collective-permute-start | bytes 1179656 | tf_op jit(solution)/shard_map/ppermute | solution.py:36
  66.2 7.5 %collective-permute-start.25 = (bf16[32,768]{1,0:T(8,128)(2,1)S(1)}, bf16[32,768]{1,0:T(8,128)(2,1)S(1)}, u32[]{:S(2)}, u32[]{:S(2)}) collective-permute-start(bf16[32,768]{1,0:T(8,128)(2,1)S(1)} %add_convert_fusion.8), channel_id=1, source_target_pairs={{0,4},{2,6},{4,0},{6,2},{8,12},{10,14},{12,8},{14,10},{1,5},{3,7},... | collective-permute-start | bytes 147464 | tf_op jit(solution)/shard_map/ppermute | solution.py:423
  71.0 26.2 %collective-permute-start.19 = (bf16[96,1536]{1,0:T(8,128)(2,1)S(1)}, bf16[96,1536]{1,0:T(8,128)(2,1)S(1)}, u32[]{:S(2)}, u32[]{:S(2)}) collective-permute-start(bf16[96,1536]{1,0:T(8,128)(2,1)S(1)} %get-tuple-element.61), channel_id=1, source_target_pairs={{0,2},{2,4},{4,6},{6,8},{8,10},{10,12},{12,14},{14,0},{1,3},{3,5},... | collective-permute-start | bytes 884744 | tf_op jit(solution)/shard_map/ppermute | solution.py:318
  72.0 25.2 %collective-permute-start.22 = (bf16[96,1536]{1,0:T(8,128)(2,1)S(1)}, bf16[96,1536]{1,0:T(8,128)(2,1)S(1)}, u32[]{:S(2)}, u32[]{:S(2)}) collective-permute-start(bf16[96,1536]{1,0:T(8,128)(2,1)S(1)} %get-tuple-element.62), channel_id=1, source_target_pairs={{2,0},{4,2},{6,4},{8,6},{10,8},{12,10},{14,12},{0,14},{3,1},{5,3},... | collective-permute-start | bytes 884744 | tf_op jit(solution)/shard_map/ppermute | solution.py:318
  73.7 26.4 %collective-permute-start.26 = (bf16[32,768]{1,0:T(8,128)(2,1)S(1)}, bf16[32,768]{1,0:T(8,128)(2,1)S(1)}, u32[]{:S(2)}, u32[]{:S(2)}) collective-permute-start(bf16[32,768]{1,0:T(8,128)(2,1)S(1)} %add_convert_fusion.7), channel_id=1, source_target_pairs={{0,8},{2,10},{4,12},{6,14},{8,0},{10,2},{12,4},{14,6},{1,9},{3,11}... | collective-permute-start | bytes 147464 | tf_op jit(solution)/shard_map/ppermute | solution.py:423
  78.9 26.1 %collective-permute-start.17 = (bf16[1,128,1536]{2,1,0:T(8,128)(2,1)S(1)}, bf16[1,128,1536]{2,1,0:T(8,128)(2,1)S(1)}, u32[]{:S(2)}, u32[]{:S(2)}) collective-permute-start(bf16[1,128,1536]{2,1,0:T(8,128)(2,1)S(1)} %bitcast.31), channel_id=1, source_target_pairs={{16,0},{32,16},{48,32},{64,48},{80,64},{96,80},{112,96},{128,112},... | collective-permute-start | bytes 1179656 | tf_op jit(solution)/shard_map/ppermute | solution.py:42
  94.1 10.9 %collective-permute-start.13 = (bf16[1,128,1536]{2,1,0:T(8,128)(2,1)S(1)}, bf16[1,128,1536]{2,1,0:T(8,128)(2,1)S(1)}, u32[]{:S(2)}, u32[]{:S(2)}) collective-permute-start(bf16[1,128,1536]{2,1,0:T(8,128)(2,1)S(1)} %fusion.2), channel_id=1, source_target_pairs={{0,16},{16,32},{32,48},{48,64},{64,80},{80,96},{96,112},{112,128},... | collective-permute-start | bytes 1179656 | tf_op jit(solution)/shard_map/ppermute | solution.py:42
  97.4 9.9 %collective-permute-start.20 = (bf16[96,1536]{1,0:T(8,128)(2,1)S(1)}, bf16[96,1536]{1,0:T(8,128)(2,1)S(1)}, u32[]{:S(2)}, u32[]{:S(2)}) collective-permute-start(bf16[96,1536]{1,0:T(8,128)(2,1)S(1)} %get-tuple-element.59), channel_id=1, source_target_pairs={{0,2},{2,4},{4,6},{6,8},{8,10},{10,12},{12,14},{14,0},{1,3},{3,5},... | collective-permute-start | bytes 884744 | tf_op jit(solution)/shard_map/ppermute | solution.py:318
  97.5 9.8 %collective-permute-start.23 = (bf16[96,1536]{1,0:T(8,128)(2,1)S(1)}, bf16[96,1536]{1,0:T(8,128)(2,1)S(1)}, u32[]{:S(2)}, u32[]{:S(2)}) collective-permute-start(bf16[96,1536]{1,0:T(8,128)(2,1)S(1)} %get-tuple-element.60), channel_id=1, source_target_pairs={{2,0},{4,2},{6,4},{8,6},{10,8},{12,10},{14,12},{0,14},{3,1},{5,3},... | collective-permute-start | bytes 884744 | tf_op jit(solution)/shard_map/ppermute | solution.py:318
  (19 other events, 158.5 us)
where the time goes:
time: 110 us
  starting transfers between devices  57.2 us (52%)
  Pallas kernels  19.8 us (18%)
  waiting for transfers between devices  19.6 us (18%)
  local copies, waits for them, and re-layouts  7.89 us (7%)
  matrix products  2.66 us (2%)
  other arithmetic  1.48 us (1%)
  between operations  1.1 us (1%)
    ppermute x8, starting transfers between devices, ring(): lax.ppermute(pair_of[1], 'z', down)  21 us
    ppermute x2, starting transfers between devices, from_behind(): return lax.ppermute(array, 'section', pairs)  17.8 us
    ppermute x1, waiting for transfers between devices, per_device(): far = lax.ppermute(edges, tm, [(a, b) for a, b in hops if 0 <= b < count])  11.1 us
    unnamed x32, local copies, waits for them, and re-layouts  7.44 us
    ppermute x3, starting transfers between devices, per_device(): arrived = lax.ppermute(total, 'z', [(i, i ^ step) for i in range(depth)])  6.62 us
    pallas_call x1, Pallas kernels, per_device(): call(functools.partial(enter_kernel, rows), [((pair, half), bf16), ((pair...  5.65 us
    ppermute x8, starting transfers between devices, ring(): lax.ppermute(pair_of[0], 'z', up)  5.38 us
    pallas_call x1, Pallas kernels, per_device(): call(functools.partial(conv_kernel, rows), [((pair, half), bf16), ((frame...  5.19 us
  transfers between devices with their start and end apart: 28, of which 5 were waited for; matrix products, arithmetic and copies ran while one was open for 3% of the time, Pallas kernels for 14%

commit v1 on v0

v1 whole, which is shorter than its diff:
```python
import functools

import jax
import jax.numpy as jnp
from jax import lax
from jax.experimental import pallas as pl
from jax.experimental.pallas import tpu as pltpu
from jax.sharding import Mesh
from jax.sharding import PartitionSpec as P


KW = 31
HALO = 16
LANES = 128
ROWS = 16


VMEM = pl.BlockSpec(memory_space=pltpu.VMEM)
SMEM = pl.BlockSpec(memory_space=pltpu.SMEM)
HBM = pl.BlockSpec(memory_space=pltpu.HBM)


def call(body, outs, in_specs, scratch=(), flops=0, size=0, limit=40 << 20):
    return pl.pallas_call(
        body,
        out_shape=[jax.ShapeDtypeStruct(shape, kind) for shape, kind in outs],
        in_specs=in_specs,
        out_specs=[VMEM] * len(outs),
        scratch_shapes=list(scratch),
        compiler_params=pltpu.CompilerParams(vmem_limit_bytes=limit),
        cost_estimate=pl.CostEstimate(flops=flops, bytes_accessed=size, transcendentals=0),
    )


def partner(array):
    return lax.ppermute(array, "x", [(0, 1), (1, 0)])


def from_behind(array, by):
    length = lax.axis_size("section")
    pairs = [(i, i + by) for i in range(length) if 0 <= i + by < length]
    return lax.ppermute(array, "section", pairs)


def divide(array, block):
    count = array.shape[1] // block
    pieces = [array[:, k * block : (k + 1) * block] for k in range(count)]
    return jnp.concatenate(pieces[0::2], axis=1), jnp.concatenate(pieces[1::2], axis=1)


def unite(even, odd, block):
    pieces = []
    for k in range(even.shape[1] // block):
        pieces += [even[:, k * block : (k + 1) * block], odd[:, k * block : (k + 1) * block]]
    return jnp.concatenate(pieces, axis=1)


def normalize(values):
    center = values - jnp.mean(values, axis=-1, keepdims=True)
    inverse = lax.rsqrt(jnp.mean(center * center, axis=-1, keepdims=True) + 1e-05)
    return (center * inverse, inverse)


def mask_of(start, length):
    return ((start + lax.broadcasted_iota(jnp.int32, (ROWS, 1), 0)) < length).astype(jnp.float32)


def conv_input(rows, gain_row, start, length):
    hat, _ = normalize(rows.astype(jnp.float32))
    return (hat * gain_row * mask_of(start, length)).astype(jnp.bfloat16)


def both(array, block, first):
    even, odd = divide(array, block)
    return jnp.where(first, even, odd), jnp.where(first, odd, even)


def edge_kernel(saved, fwd, grad, edges, sems):
    frames = saved.shape[0]
    side = lax.axis_index("x")
    wide = pl.ds(pl.multiple_of(side * (frames - 2 * HALO), HALO), 2 * HALO)
    thin = pl.ds(pl.multiple_of(side * (frames - HALO), HALO), HALO)
    copies = [
        pltpu.make_async_copy(saved.at[wide, :], edges.at[0 : 2 * HALO, :], sems.at[0]),
        pltpu.make_async_copy(fwd.at[thin, :], edges.at[2 * HALO : 3 * HALO, :], sems.at[1]),
        pltpu.make_async_copy(grad.at[thin, :], edges.at[3 * HALO : 4 * HALO, :], sems.at[2]),
    ]
    for copy in copies:
        copy.start()
    for copy in copies:
        copy.wait()


def enter_kernel(
    block, plan_hbm, lengths_hbm, saved_hbm, fwd_hbm, gain_hbm, kernel_hbm,
    own, own_fwd, other, other_fwd, taps, plan, lengths, saved, fwd, gain, kernel, sems,
):
    frames = saved.shape[0]
    side = lax.axis_index("x")
    first = side == 0
    pairs = (
        (saved_hbm, saved),
        (kernel_hbm, kernel),
        (plan_hbm, plan),
        (lengths_hbm, lengths),
        (gain_hbm, gain),
        (fwd_hbm, fwd),
    )
    copies = [pltpu.make_async_copy(a, b, sems.at[i]) for i, (a, b) in enumerate(pairs)]
    for copy in copies:
        copy.start()
    for copy in copies[1:5]:
        copy.wait()
    taps[0:KW, :] = both(kernel[:, 0, :], block, first)[0]
    taps[KW : KW + 1, :] = jnp.zeros((1, taps.shape[1]), jnp.float32)
    origin = lax.axis_index("z") * 2 * frames
    fwd_len = lengths[plan[0, 0]]
    bwd_len = lengths[plan[0, 1]]
    gain_row = gain[...]

    def pass_over(source, mine_out, theirs_out, length):
        def body(i, carry):
            at = pl.multiple_of(i * ROWS, ROWS)
            start = origin + side * frames + at
            value = conv_input(source[pl.ds(at, ROWS), :], gain_row, start, length)
            mine, theirs = both(value, block, first)
            mine_out[pl.ds(at, ROWS), :] = mine
            theirs_out[pl.ds(at, ROWS), :] = theirs
            return carry

        lax.fori_loop(0, frames // ROWS, body, 0)

    copies[0].wait()
    pass_over(saved, own, other, bwd_len)
    copies[5].wait()
    pass_over(fwd, own_fwd, other_fwd, fwd_len)


def slide(buffer, chunk, start, count, weight):
    total = jnp.zeros((count, LANES), jnp.float32)
    for shift in range(8):
        tile = buffer[chunk, pl.ds(start + shift, count + 24), :]
        for step in range(4):
            offset = 8 * step + shift
            if 1 <= offset <= KW:
                total = total + weight(offset) * tile[8 * step : 8 * step + count]
    return total


def fill_halo(block, halo, near, far, gain, spots, origin, length):
    first = lax.axis_index("x") == 0
    gain_row = gain[...]
    for row, out_row, start, ahead in spots:
        rows = jnp.where(first == ahead, near[row : row + ROWS, :], far[row : row + ROWS, :])
        value = conv_input(rows, gain_row, origin + start, length)
        halo[out_row : out_row + ROWS, :] = both(value, block, first)[0]


def store_rows(buffer, chunk, row, values):
    if not isinstance(row, int):
        row = pl.multiple_of(row, 8)
    buffer[chunk, pl.ds(row, values.shape[0]), :] = values.astype(jnp.float32)


def fwd_kernel(block, plan, lengths, own, got, taps, near, far, gain, hidden_own, hidden_other, window, halo):
    side = lax.axis_index("x")
    frames = own.shape[0]
    mine = side * frames
    theirs = frames - mine
    spots = ((2 * HALO, 0, -HALO, True), (2 * HALO, HALO, 2 * frames, False))
    origin = lax.axis_index("z") * 2 * frames
    fill_halo(block, halo, near, far, gain, spots, origin, lengths[plan[0, 0]])

    def body(chunk, carry):
        lanes = pl.ds(pl.multiple_of(chunk * LANES, LANES), LANES)
        put = functools.partial(store_rows, window, 0)
        put(0, halo[0:HALO, lanes])
        put(HALO + mine, own[:, lanes])
        put(HALO + theirs, got[:, lanes])
        put(HALO + 2 * frames, halo[HALO:, lanes])
        put(2 * HALO + 2 * frames, jnp.zeros((8, LANES), jnp.float32))

        def weight(offset):
            return taps[offset - 1 : offset, lanes]

        for half in range(2):
            mixed = slide(window, 0, half * frames, frames, weight)
            hidden = (mixed * jax.nn.sigmoid(mixed)).astype(jnp.bfloat16)

            @pl.when(side == half)
            def _():
                hidden_own[:, lanes] = hidden

            @pl.when(side != half)
            def _():
                hidden_other[:, lanes] = hidden

        return carry

    lax.fori_loop(0, own.shape[1] // LANES, body, 0)


def conv_kernel(
    block, factor, plan, lengths, own, got, taps, grad_hbm, grad_got, near, far, gain,
    *refs,
):
    blocks = refs[:-8]
    slope, keep_window, grad_window, hidden_saved, window, halo, product, sem = refs[-8:]
    side = lax.axis_index("x")
    frames = grad_got.shape[0]
    mine = side * frames
    spot = pl.ds(pl.multiple_of(HALO + mine, HALO), frames)
    copy = pltpu.make_async_copy(grad_hbm, grad_window.at[spot, :], sem)
    copy.start()
    theirs = frames - mine
    chunks = own.shape[1] // LANES
    first = side == 0
    origin = lax.axis_index("z") * 2 * frames
    spots = (
        (0, 0, -2 * HALO, True),
        (HALO, HALO, -HALO, True),
        (0, 2 * HALO, 2 * frames, False),
        (HALO, 3 * HALO, 2 * frames + HALO, False),
    )
    fill_halo(block, halo, near, far, gain, spots, origin, lengths[plan[0, 1]])

    grad_window[pl.ds(pl.multiple_of(HALO + theirs, HALO), frames), :] = grad_got[...]
    grad_window[0:HALO, :] = jnp.where(first, near[3 * HALO :, :], far[3 * HALO :, :])
    grad_window[HALO + 2 * frames :, :] = jnp.where(first, far[3 * HALO :, :], near[3 * HALO :, :])

    def body(chunk, carry):
        lanes = pl.ds(pl.multiple_of(chunk * LANES, LANES), LANES)

        put = functools.partial(store_rows, window, 0)
        put(0, halo[0 : 2 * HALO, lanes])
        put(2 * HALO + mine, own[:, lanes])
        put(2 * HALO + theirs, got[:, lanes])
        put(2 * HALO + 2 * frames, halo[2 * HALO :, lanes])
        put(4 * HALO + 2 * frames, jnp.zeros((8, LANES), jnp.float32))

        def weight(offset):
            return taps[offset - 1 : offset, lanes]

        keep_window[:, lanes] = window[0, 0 : keep_window.shape[0], :].astype(jnp.bfloat16)
        span = frames + HALO
        for half in range(2):
            mixed = slide(window, 0, half * span, span, weight)
            gate = jax.nn.sigmoid(mixed)
            hidden = mixed * gate
            value = gate + hidden * (1.0 - gate)
            slope[pl.ds(half * span, span), lanes] = value.astype(jnp.bfloat16)
            keep = hidden[HALO:] if half == 0 else hidden[:frames]
            hidden_saved[pl.ds(half * frames, frames), lanes] = keep.astype(jnp.bfloat16)
        return carry

    lax.fori_loop(0, chunks, body, 0)
    copy.wait()
    depth = len(blocks)
    here = lax.axis_index("z")

    def outer(index, carry):
        lanes = pl.ds(pl.multiple_of(index * 2 * LANES, 2 * LANES), 2 * LANES)
        value = lax.dot_general(
            hidden_saved[...],
            grad_window[HALO : HALO + 2 * frames, lanes],
            (((0,), (0,)), ((), ())),
            preferred_element_type=jnp.float32,
        )
        value = (value * factor).astype(jnp.bfloat16)
        product[...] = value.reshape(product.shape)
        for k, out in enumerate(blocks):
            place = jnp.where(here + k < depth, here + k, here + k - depth)
            out[:, lanes] = product[place]
        return carry

    lax.fori_loop(0, grad_window.shape[1] // (2 * LANES), outer, 0)


def back_kernel(
    factor, places, plan, lengths, grad_window, slope, window, taps, *refs
):
    blocks, (grad_own, grad_other, kernel_grad, weights, conv_grad, inputs) = refs[:-6], refs[-6:]
    rows = blocks[0].shape[0]
    depth = weights.shape[0] // rows
    for block, (step, offset, count) in zip(blocks, places):
        place = lax.axis_index("z") + step
        place = jnp.where(place < depth, place, place - depth) * rows + offset
        weights[pl.ds(pl.multiple_of(place, ROWS), count), :] = block[0:count, :]
    side = lax.axis_index("x")
    frames = grad_own.shape[0]
    chunks = taps.shape[1] // LANES
    origin = lax.axis_index("z") * 2 * frames
    bwd_len = lengths[plan[0, 1]]

    def product(index, carry):
        lanes = pl.ds(pl.multiple_of(index * 2 * LANES, 2 * LANES), 2 * LANES)
        hidden_grad = lax.dot_general(
            grad_window[...],
            weights[lanes, :],
            (((1,), (1,)), ((), ())),
            preferred_element_type=jnp.float32,
        )
        value = (hidden_grad * slope[:, lanes].astype(jnp.float32)).astype(jnp.bfloat16).astype(jnp.float32)
        for part in range(2):
            chunk = 2 * index + part
            conv_grad[chunk, 0 : 2 * frames + 2 * HALO, :] = value[:, part * LANES : (part + 1) * LANES]
            conv_grad[chunk, 2 * frames + 2 * HALO :, :] = jnp.zeros((8, LANES), jnp.float32)
        return carry

    lax.fori_loop(0, chunks // 2, product, 0)

    def body(chunk, carry):
        lanes = pl.ds(pl.multiple_of(chunk * LANES, LANES), LANES)

        inputs[0, 0 : window.shape[0], :] = window[:, lanes].astype(jnp.float32)
        inputs[0, window.shape[0] :, :] = jnp.zeros((8, LANES), jnp.float32)

        def weight(offset):
            return taps[KW - offset : KW - offset + 1, lanes]

        for half in range(2):
            total = slide(conv_grad, chunk, half * frames, frames, weight)
            frame = origin + half * frames + lax.broadcasted_iota(jnp.int32, (frames, 1), 0)
            total = (total * (frame < bwd_len).astype(jnp.float32)).astype(jnp.bfloat16)

            @pl.when(side == half)
            def _():
                grad_own[:, lanes] = total

            @pl.when(side != half)
            def _():
                grad_other[:, lanes] = total

        for shift in range(8):
            sums = [jnp.zeros((8, LANES), jnp.float32) for _ in range(4)]
            for half in range(2):
                left = conv_grad[chunk, pl.ds(HALO + half * frames, frames), :]
                right = inputs[0, pl.ds(HALO + half * frames + shift, frames + 24), :]
                for step in range(4):
                    if 1 <= 8 * step + shift <= KW:
                        term = left * right[8 * step : 8 * step + frames]
                        sums[step] = sums[step] + jnp.sum(term.reshape(frames // 8, 8, LANES), axis=0)
            for step in range(4):
                tap = 8 * step + shift - 1
                if 0 <= tap < KW:
                    row = jnp.sum(sums[step], axis=0, keepdims=True) * factor
                    kernel_grad[tap : tap + 1, lanes] = row
        kernel_grad[KW : KW + 1, lanes] = jnp.zeros((1, LANES), jnp.float32)
        return carry

    lax.fori_loop(0, chunks, body, 0)


def leave_kernel(block, own, got, saved, grad, gain, out):
    first = lax.axis_index("x") == 0
    gain_row = gain[...]

    def body(i, carry):
        at = pl.ds(pl.multiple_of(i * ROWS, ROWS), ROWS)
        mine, theirs = own[at, :], got[at, :]
        even, odd = jnp.where(first, mine, theirs), jnp.where(first, theirs, mine)
        hat_grad = unite(even, odd, block).astype(jnp.float32) * gain_row
        hat, inverse = normalize(saved[at, :].astype(jnp.float32))
        back = grad[at, :].astype(jnp.float32) + inverse * (
            hat_grad
            - jnp.mean(hat_grad, axis=-1, keepdims=True)
            - hat * jnp.mean(hat_grad * hat, axis=-1, keepdims=True)
        )
        out[at, :] = back.astype(jnp.bfloat16)
        return carry

    lax.fori_loop(0, saved.shape[0] // ROWS, body, 0)


def totals_kernel(block, own, got, kernel, gain, kernel_out, gain_out):
    first = lax.axis_index("x") == 0
    mine, theirs = own[...], got[...]
    even, odd = jnp.where(first, mine, theirs), jnp.where(first, theirs, mine)
    total = unite(even.astype(jnp.float32), odd.astype(jnp.float32), block)[:KW]
    kernel_out[:, 0, :] = total
    gain_out[...] = jnp.sum(kernel[:, 0, :] * total, axis=0, keepdims=True) / gain[...]


def per_device(fwd_input, saved_input, grad_in, gain, kernel, w_out, lengths, plan):
    frames, width = fwd_input.shape[1:]
    depth = lax.axis_size("z")
    rows = w_out.shape[1]
    half = rows * depth
    pair = 2 * frames
    factor = float(pair * depth) ** (-0.5)
    fwd_rows = fwd_input[0]
    saved_rows = saved_input[0]
    upstream = grad_in[0]
    bf16, f32 = jnp.bfloat16, jnp.float32

    barrier = lax.optimization_barrier

    up = [(i, (i + 1) % depth) for i in range(depth)]
    down = [(j, i) for i, j in up]

    def ring(pair_of):
        return lax.ppermute(pair_of[0], "z", up), lax.ppermute(pair_of[1], "z", down)

    grad_got = partner(upstream)
    (edges,) = call(
        edge_kernel,
        [((4 * HALO, width), bf16)],
        [HBM] * 3,
        [pltpu.SemaphoreType.DMA((3,))],
        limit=None,
        size=16 * HALO * width,
    )(saved_rows, fwd_rows, upstream)
    count = 2 * depth
    tm = ("z", "x")
    hops = [(t, t + 1 if t % 2 else t - 1) for t in range(count)]
    near = lax.ppermute(edges, tm, [(a, b) for a, b in hops if 0 <= b < count])
    hops = [(t, t + 2 if t % 2 else t - 2) for t in range(count)]
    far = lax.ppermute(edges, tm, [(a, b) for a, b in hops if 0 <= b < count])

    block = w_out[0]
    round_1 = ring((block, block))
    tap_rows = jnp.transpose(kernel, (1, 0, 2))

    own, own_fwd, other, other_fwd, taps = call(
        functools.partial(enter_kernel, rows),
        [((frames, half), bf16)] * 4 + [((KW + 1, half), f32)],
        [HBM] * 6,
        [
            pltpu.SMEM(plan.shape, jnp.int32),
            pltpu.SMEM(lengths.shape, jnp.int32),
            pltpu.VMEM((frames, width), bf16),
            pltpu.VMEM((frames, width), bf16),
            pltpu.VMEM(gain.shape, f32),
            pltpu.VMEM(tap_rows.shape, f32),
            pltpu.SemaphoreType.DMA((6,)),
        ],
        limit=None,
        flops=12 * 2 * frames * width,
        size=10 * frames * width,
    )(plan, lengths, saved_rows, fwd_rows, gain, tap_rows)
    got = partner(other)
    got_fwd = partner(other_fwd)
    round_2 = ring(round_1)
    got, near, far, grad_got, round_2 = barrier((got, near, far, grad_got, round_2))
    round_3 = ring(round_2)
    *partial, slope, window, grad_window = call(
        functools.partial(conv_kernel, rows, factor),
        [
            *[((rows, width), bf16)] * depth,
            ((pair + 2 * HALO, half), bf16),
            ((pair + 4 * HALO, half), bf16),
            ((pair + 2 * HALO, width), bf16),
        ],
        [SMEM, SMEM] + [VMEM] * 3 + [HBM] + [VMEM] * 4,
        [
            pltpu.VMEM((pair, half), bf16),
            pltpu.VMEM((1, pair + 4 * HALO + 8, LANES), f32),
            pltpu.VMEM((4 * HALO, half), bf16),
            pltpu.VMEM((depth, rows, 2 * LANES), bf16),
            pltpu.SemaphoreType.DMA(()),
        ],
        limit=None,
        flops=2 * KW * 2 * pair * half,
        size=16 * pair * half,
    )(plan, lengths, own, got, taps, upstream, grad_got, near, far, gain)

    hidden_own, hidden_other = call(
        functools.partial(fwd_kernel, rows),
        [((frames, half), bf16)] * 2,
        [SMEM, SMEM] + [VMEM] * 6,
        [
            pltpu.VMEM((1, pair + 2 * HALO + 8, LANES), f32),
            pltpu.VMEM((2 * HALO, half), bf16),
        ],
        limit=None,
        flops=2 * KW * pair * half,
        size=8 * pair * half,
    )(plan, lengths, own_fwd, got_fwd, taps, near, far, gain)
    partial, round_3 = barrier((partial, round_3))

    def plus(arrived, own_part):
        return (arrived.astype(f32) + own_part.astype(f32)).astype(bf16)

    round_4 = lax.ppermute(round_3[0], "z", up)
    back_1 = lax.ppermute(partial[depth // 2], "z", down)
    blocks = [block]
    places = [(0, 0, rows)]
    for k, (behind, ahead) in enumerate((round_1, round_2, round_3), 1):
        blocks += [behind, ahead]
        places += [(depth - k, 0, rows), (k, 0, rows)]
    blocks += [round_4]
    places += [(depth // 2, 0, rows)]
    back_2 = ring((partial[depth // 2 - 1], plus(back_1, partial[depth // 2 + 1])))
    norm_own, norm_other, kernel_local, w_half = call(
        functools.partial(back_kernel, factor, tuple(places)),
        [
            ((frames, half), bf16),
            ((frames, half), bf16),
            ((KW + 1, half), f32),
            ((half, width), bf16),
        ],
        [SMEM, SMEM] + [VMEM] * (4 + len(blocks)),
        [
            pltpu.VMEM((half // LANES, pair + 2 * HALO + 8, LANES), f32),
            pltpu.VMEM((1, pair + 4 * HALO + 8, LANES), f32),
        ],
        flops=4 * KW * pair * half,
        size=12 * pair * half,
    )(plan, lengths, grad_window, slope, window, taps, *blocks)
    norm_got = partner(norm_other)
    total = kernel_local.astype(bf16)
    step = 1
    while step < depth:
        arrived = lax.ppermute(total, "z", [(i, i ^ step) for i in range(depth)])
        total = (total.astype(f32) + arrived.astype(f32)).astype(bf16)
        step *= 2
    total_got = partner(total)

    back_3 = ring((plus(back_2[0], partial[2]), plus(back_2[1], partial[-2])))
    back_4 = ring((plus(back_3[0], partial[1]), plus(back_3[1], partial[-1])))
    weight_grad = back_4[0].astype(f32) + back_4[1].astype(f32) + partial[0].astype(f32)

    product = jnp.dot(hidden_other, w_half, preferred_element_type=f32).astype(bf16)
    product_got = partner(product)
    output = (
        fwd_rows.astype(f32)
        + (jnp.dot(hidden_own, w_half, preferred_element_type=f32) + product_got.astype(f32))
    ).astype(bf16)
    passed_activation = from_behind(output[None], 1)

    (input_back,) = call(
        functools.partial(leave_kernel, rows),
        [((frames, width), bf16)],
        [VMEM] * 5,
        flops=20 * frames * width,
        size=8 * frames * width,
    )(norm_own, norm_got, saved_rows, upstream, gain)
    passed_gradient = from_behind(input_back[None], -1)
    kernel_grad, gain_grad = call(
        functools.partial(totals_kernel, rows),
        [((KW, 1, width), f32), ((1, width), f32)],
        [VMEM] * 4,
        flops=4 * KW * width,
        size=12 * KW * width,
    )(total, total_got, tap_rows, gain)
    return (
        passed_activation,
        passed_gradient,
        weight_grad[None],
        jnp.transpose(kernel_grad, (1, 0, 2)),
        gain_grad,
    )


def solution(mesh):
    sections, pieces = mesh.devices.shape
    folded = Mesh(mesh.devices.reshape(sections, pieces // 2, 2), ("section", "z", "x"))
    split = P("section", ("z", "x"), None)
    placed = (
        split,
        split,
        split,
        P("section", None),
        P("section", None, None),
        split,
        P(),
        P("section", None),
    )

    return jax.shard_map(
        per_device,
        mesh=folded,
        in_specs=placed,
        out_specs=(split, split, split, P("section", None, None), P("section", None)),
        check_vma=False,
    )
```

time: 110 us -> 117 us (1.064)
  waiting for transfers between devices: 19.6 us -> 30.1 us
  Pallas kernels: 19.8 us -> 29.5 us
  starting transfers between devices: 57.2 us -> 48.8 us
  local copies, waits for them, and re-layouts: 7.89 us -> 4.31 us
  matrix products: 2.66 us -> 0.97 us
    ppermute x1, waiting for transfers between devices: 11.1 us -> 0.01 us  [per_device(): far = lax.ppermute(edges, tm, [(a, b) for a, b in hops if 0 <= b < count])]
    pallas_call x4 -> x6, Pallas kernels: 18.4 us -> 28.7 us  [the longest x1 8.01 us: per_device(): call(functools.partial(conv_kernel, rows, factor), [*[((rows, width), bf1...]
    ppermute x5 -> x6, waiting for transfers between devices: 3.4 us -> 11.6 us  [partner(): return lax.ppermute(array, 'x', [(0, 1), (1, 0)])]
    ppermute x8 -> x6, starting transfers between devices: 21 us -> 12.9 us  [ring(): lax.ppermute(pair_of[1], 'z', down)]
    ppermute x8 -> x6, waiting for transfers between devices: 0.02 us -> 7.46 us  [ring(): lax.ppermute(pair_of[1], 'z', down)]
    ppermute x0 -> x2, waiting for transfers between devices: none -> 5.88 us  [the longest x1 5.87 us: per_device(): round_4 = lax.ppermute(round_3[0], 'z', up)]
    ppermute x3, waiting for transfers between devices: 0.01 us -> 5.1 us  [per_device(): arrived = lax.ppermute(total, 'z', [(i, i ^ step) for i in range(depth)])]
    ppermute x8 -> x6, waiting for transfers between devices: 5.04 us -> 0.02 us  [ring(): lax.ppermute(pair_of[0], 'z', up)]
  transfers between devices with their start and end apart: 28 -> 27, of which waited for: 5 -> 9; matrix products, arithmetic and copies ran while one was open for 3% -> 2% of each run, Pallas kernels for 14% -> 25%
where the time goes in v1:
time: 117 us
  starting transfers between devices  48.8 us (42%)
  waiting for transfers between devices  30.1 us (26%)
  Pallas kernels  29.5 us (25%)
  local copies, waits for them, and re-layouts  4.31 us (4%)
  other arithmetic  2.33 us (2%)
    ppermute x2, starting transfers between devices, from_behind(): return lax.ppermute(array, 'section', pairs)  15 us
    ppermute x6, starting transfers between devices, ring(): lax.ppermute(pair_of[1], 'z', down)  12.9 us
    ppermute x6, waiting for transfers between devices, partner(): return lax.ppermute(array, 'x', [(0, 1), (1, 0)])  11.6 us
    pallas_call x1, Pallas kernels, per_device(): call(functools.partial(conv_kernel, rows, factor), [*[((rows, width), bf1...  8.01 us
    ppermute x6, waiting for transfers between devices, ring(): lax.ppermute(pair_of[1], 'z', down)  7.46 us
    ppermute x6, starting transfers between devices, ring(): lax.ppermute(pair_of[0], 'z', up)  7.41 us
    pallas_call x1, Pallas kernels, per_device(): call(functools.partial(enter_kernel, rows), [((frames, half), bf16)] * 4...  6.58 us
    ppermute x1, waiting for transfers between devices, per_device(): round_4 = lax.ppermute(round_3[0], 'z', up)  5.87 us
  transfers between devices with their start and end apart: 27, of which 9 were waited for; matrix products, arithmetic and copies ran while one was open for 2% of the time, Pallas kernels for 25%

profile of v1, /device:TPU:1, one launch (start us, length us, event | category | flops | bytes accessed | tf_op | source)
XLA Modules:
  0.0 117.1 jit_solution(12208081229775128967)
XLA Ops:
  0.6 6.5 %collective-permute-start.7 = (bf16[96,1536]{1,0:T(8,128)(2,1)}, bf16[96,1536]{1,0:T(8,128)(2,1)S(1)}, u32[]{:S(2)}, u32[]{:S(2)}) collective-permute-start(bf16[96,1536]{1,0:T(8,128)(2,1)} %bitcast.26), channel_id=1, source_target_pairs={{2,0},{4,2},{6,4},{8,6},{10,8},{12,10},{14,12},{0,14},{3,1},{5,3},... | collective-permute-start | bytes 884744 | tf_op jit(solution)/shard_map/ppermute | solution.py:402
  7.1 1.6 %shard_map.120 = bf16[64,1536]{1,0:T(8,128)(2,1)} custom-call(bf16[128,1536]{1,0:T(8,128)(2,1)} %bitcast.16, bf16[128,1536]{1,0:T(8,128)(2,1)} %bitcast.29, bf16[128,1536]{1,0:T(8,128)(2,1)} %bitcast.19), custom_call_target="tpu_custom_call" | custom-call | bytes 393216 | tf_op jit(solution)/shard_map/pallas_call | solution.py:405
  11.5 1.6 %collective-permute-done.7.refs_2_ = bf16[96,1536]{1,0:T(8,128)(2,1)S(1)} collective-permute-done((bf16[96,1536]{1,0:T(8,128)(2,1)}, bf16[96,1536]{1,0:T(8,128)(2,1)S(1)}, u32[]{:S(2)}, u32[]{:S(2)}) %collective-permute-start.7) | collective-permute-done | bytes 294944 | tf_op jit(solution)/shard_map/ppermute | solution.py:402
  13.1 3.3 %collective-permute-start.8 = (bf16[96,1536]{1,0:T(8,128)(2,1)S(1)}, bf16[96,1536]{1,0:T(8,128)(2,1)S(1)}, u32[]{:S(2)}, u32[]{:S(2)}) collective-permute-start(bf16[96,1536]{1,0:T(8,128)(2,1)S(1)} %collective-permute-done.7.refs_2_), channel_id=1, source_target_pairs={{2,0},{4,2},{6,4},{8,6},{10,8},{12,10},{14,12},{0,14},{3,1},{5,3},... | collective-permute-start | bytes 884744 | tf_op jit(solution)/shard_map/ppermute | solution.py:402
  17.1 6.6 %shard_map.119 = (bf16[128,768]{1,0:T(8,128)(2,1)}, bf16[128,768]{1,0:T(8,128)(2,1)}, bf16[128,768]{1,0:T(8,128)(2,1)}, bf16[128,768]{1,0:T(8,128)(2,1)}, f32[32,768]{1,0:T(8,128)}) custom-call(s32[1,2]{1,0:T(1,128)} %plan.5, s32[32]{0:T(128)} %lengths.5, bf16[128,1536]{1,0:T(8,128)(2,1)} %bitcast.17, bf16[128,1536]{1,0:T(8,128)(2,1)} %bitcast.30, ...), custom_call_target="tpu_custom_call" | custom-call | flops 4718592 | bytes 1966080 | tf_op jit(solution)/shard_map/pallas_call | solution.py:424
  23.7 2.5 %collective-permute-start.1 = (bf16[128,768]{1,0:T(8,128)(2,1)}, bf16[128,768]{1,0:T(8,128)(2,1)S(1)}, u32[]{:S(2)}, u32[]{:S(2)}) collective-permute-start(bf16[128,768]{1,0:T(8,128)(2,1)} %get-tuple-element.48), channel_id=1, source_target_pairs={{0,1},{1,0},{2,3},{3,2},{4,5},{5,4},{6,7},{7,6},{8,9},{9,8},{10,11... | collective-permute-start | bytes 589832 | tf_op jit(solution)/shard_map/ppermute | solution.py:36
  26.3 3.7 %collective-permute-done.1.got = bf16[128,768]{1,0:T(8,128)(2,1)S(1)} collective-permute-done((bf16[128,768]{1,0:T(8,128)(2,1)}, bf16[128,768]{1,0:T(8,128)(2,1)S(1)}, u32[]{:S(2)}, u32[]{:S(2)}) %collective-permute-start.1) | collective-permute-done | bytes 196640 | tf_op jit(solution)/shard_map/ppermute | solution.py:36
  30.0 5.6 %collective-permute-start.9 = (bf16[96,1536]{1,0:T(8,128)(2,1)S(1)}, bf16[96,1536]{1,0:T(8,128)(2,1)S(1)}, u32[]{:S(2)}, u32[]{:S(2)}) collective-permute-start(bf16[96,1536]{1,0:T(8,128)(2,1)S(1)} %collective-permute-done.6.refs_3_), channel_id=1, source_target_pairs={{0,2},{2,4},{4,6},{6,8},{8,10},{10,12},{12,14},{14,0},{1,3},{3,5},... | collective-permute-start | bytes 884744 | tf_op jit(solution)/shard_map/ppermute | solution.py:402
  36.7 8.0 %shard_map.122 = (bf16[96,1536]{1,0:T(8,128)(2,1)}, bf16[96,1536]{1,0:T(8,128)(2,1)}, bf16[96,1536]{1,0:T(8,128)(2,1)}, bf16[96,1536]{1,0:T(8,128)(2,1)}, bf16[9...) custom-call(s32[1,2]{1,0:T(1,128)} %plan.5, ...), custom_call_target="tpu_custom_call" | custom-call | flops 24379392 | bytes 3145728 | tf_op jit(solution)/shard_map/pallas_call | solution.py:446
  45.1 4.7 %collective-permute-done.got = bf16[128,768]{1,0:T(8,128)(2,1)S(1)} collective-permute-done((bf16[128,768]{1,0:T(8,128)(2,1)}, bf16[128,768]{1,0:T(8,128)(2,1)S(1)}, u32[]{:S(2)}, u32[]{:S(2)}) %collective-permute-start) | collective-permute-done | bytes 196640 | tf_op jit(solution)/shard_map/ppermute | solution.py:36
  50.5 4.3 %shard_map.121 = (bf16[128,768]{1,0:T(8,128)(2,1)}, bf16[128,768]{1,0:T(8,128)(2,1)}) custom-call(s32[1,2]{1,0:T(1,128)} %plan.5, s32[32]{0:T(128)} %lengths.5, bf16[128,768]{1,0:T(8,128)(2,1)} %get-tuple-element.45.own, bf16[128,768]{1,0:T(8,128)(2,1)} %copy-done.22, f32[32,768]{1,0:T(8,128)} %get-tuple-element.47.taps, bf16[64,1536]{1,0:T(8,128)(2,1)} %copy-done.13, ...), custom_call_target="tpu_custom_call" | custom-call | flops 12189696 | bytes 1572864 | tf_op jit(solution)/shard_map/pallas_call | solution.py:467
  54.8 2.9 %collective-permute-start.19 = (bf16[96,1536]{1,0:T(8,128)(2,1)}, bf16[96,1536]{1,0:T(8,128)(2,1)S(1)}, u32[]{:S(2)}, u32[]{:S(2)}) collective-permute-start(bf16[96,1536]{1,0:T(8,128)(2,1)} %get-tuple-element.77), channel_id=1, source_target_pairs={{2,0},{4,2},{6,4},{8,6},{10,8},{12,10},{14,12},{0,14},{3,1},{5,3},... | collective-permute-start | bytes 884744 | tf_op jit(solution)/shard_map/ppermute | solution.py:485
  59.1 5.9 %collective-permute-done.11.refs_7_ = bf16[96,1536]{1,0:T(8,128)(2,1)S(1)} collective-permute-done((bf16[96,1536]{1,0:T(8,128)(2,1)S(1)}, bf16[96,1536]{1,0:T(8,128)(2,1)S(1)}, u32[]{:S(2)}, u32[]{:S(2)}) %collective-permute-start.11) | collective-permute-done | bytes 294944 | tf_op jit(solution)/shard_map/ppermute | solution.py:484
  67.1 5.9 %shard_map.123 = (bf16[128,768]{1,0:T(8,128)(2,1)S(1)}, bf16[128,768]{1,0:T(8,128)(2,1)S(1)}, f32[32,768]{1,0:T(8,128)S(1)}, bf16[768,1536]{1,0:T(8,128)(2,1)S(1)}) custom-call(s32[1,2]{1,0:T(1,128)S(1)} %copy-done.9, s32[32]{0:T(128)S(1)} %copy-done.10, bf16[288,1536]{1,0:T(8,128)(2,1)S(1)} %copy-done.2, bf16[288,768]{1,0:T(8,128)(2,1)S(1)} %copy-done.6, ...), custom_call_target="tpu_custom_call" | custom-call | flops 24379392 | bytes 2359296 | tf_op jit(solution)/shard_map/pallas_call | solution.py:494
  73.9 2.1 %collective-permute-done.23 = bf16[32,768]{1,0:T(8,128)(2,1)S(1)} collective-permute-done((bf16[32,768]{1,0:T(8,128)(2,1)S(1)}, bf16[32,768]{1,0:T(8,128)(2,1)S(1)}, u32[]{:S(2)}, u32[]{:S(2)}) %collective-permute-start.23) | collective-permute-done | bytes 49184 | tf_op jit(solution)/shard_map/ppermute | solution.py:514
  78.0 3.0 %collective-permute-done.24 = bf16[32,768]{1,0:T(8,128)(2,1)S(1)} collective-permute-done((bf16[32,768]{1,0:T(8,128)(2,1)S(1)}, bf16[32,768]{1,0:T(8,128)(2,1)S(1)}, u32[]{:S(2)}, u32[]{:S(2)}) %collective-permute-start.24) | collective-permute-done | bytes 49184 | tf_op jit(solution)/shard_map/ppermute | solution.py:514
  81.0 2.3 %collective-permute-start.25 = (bf16[32,768]{1,0:T(8,128)(2,1)S(1)}, bf16[32,768]{1,0:T(8,128)(2,1)S(1)}, u32[]{:S(2)}, u32[]{:S(2)}) collective-permute-start(bf16[32,768]{1,0:T(8,128)(2,1)S(1)} %add_convert_fusion.6), channel_id=1, source_target_pairs={{0,8},{2,10},{4,12},{6,14},{8,0},{10,2},{12,4},{14,6},{1,9},{3,11}... | collective-permute-start | bytes 147464 | tf_op jit(solution)/shard_map/ppermute | solution.py:514
  83.4 2.4 %shard_map.124 = bf16[128,1536]{1,0:T(8,128)(2,1)S(1)} custom-call(bf16[128,768]{1,0:T(8,128)(2,1)S(1)} %get-tuple-element.72.own, bf16[128,768]{1,0:T(8,128)(2,1)S(1)} %collective-permute-done.14.got, bf16[128,1536]{1,0:T(8,128)(2,1)S(1)} %bitcast.18, bf16[128,1536]{1,0:T(8,128)(2,1)S(1)} %bitcast.22, f32[1,1536]{1,0:T(1,128)S(1)} %copy-done.8), custom_call_target="tpu_custom_call" | custom-call | flops 3932160 | bytes 1572864 | tf_op jit(solution)/shard_map/pallas_call | solution.py:531
  85.8 11.3 %collective-permute-start.15 = (bf16[1,128,1536]{2,1,0:T(8,128)(2,1)S(1)}, bf16[1,128,1536]{2,1,0:T(8,128)(2,1)S(1)}, u32[]{:S(2)}, u32[]{:S(2)}) collective-permute-start(bf16[1,128,1536]{2,1,0:T(8,128)(2,1)S(1)} %bitcast.25), channel_id=1, source_target_pairs={{16,0},{32,16},{48,32},{64,48},{80,64},{96,80},{112,96},{128,112},... | collective-permute-start | bytes 1179656 | tf_op jit(solution)/shard_map/ppermute | solution.py:42
  99.4 3.7 %collective-permute-start.13 = (bf16[1,128,1536]{2,1,0:T(8,128)(2,1)S(1)}, bf16[1,128,1536]{2,1,0:T(8,128)(2,1)S(1)}, u32[]{:S(2)}, u32[]{:S(2)}) collective-permute-start(bf16[1,128,1536]{2,1,0:T(8,128)(2,1)S(1)} %fusion.2), channel_id=1, source_target_pairs={{0,16},{16,32},{32,48},{48,64},{64,80},{80,96},{96,112},{112,128},... | collective-permute-start | bytes 1179656 | tf_op jit(solution)/shard_map/ppermute | solution.py:42
  103.1 3.0 %collective-permute-done.21 = bf16[96,1536]{1,0:T(8,128)(2,1)S(1)} collective-permute-done((bf16[96,1536]{1,0:T(8,128)(2,1)S(1)}, bf16[96,1536]{1,0:T(8,128)(2,1)S(1)}, u32[]{:S(2)}, u32[]{:S(2)}) %collective-permute-start.21) | collective-permute-done | bytes 294944 | tf_op jit(solution)/shard_map/ppermute | solution.py:402
  106.2 1.4 %collective-permute-start.22 = (bf16[96,1536]{1,0:T(8,128)(2,1)S(1)}, bf16[96,1536]{1,0:T(8,128)(2,1)S(1)}, u32[]{:S(2)}, u32[]{:S(2)}) collective-permute-start(bf16[96,1536]{1,0:T(8,128)(2,1)S(1)} %add_convert_fusion), channel_id=1, source_target_pairs={{2,0},{4,2},{6,4},{8,6},{10,8},{12,10},{14,12},{0,14},{3,1},{5,3},... | collective-permute-start | bytes 884744 | tf_op jit(solution)/shard_map/ppermute | solution.py:402
  107.8 3.2 %collective-permute-done.26.got = bf16[32,768]{1,0:T(8,128)(2,1)S(1)} collective-permute-done((bf16[32,768]{1,0:T(8,128)(2,1)S(1)}, bf16[32,768]{1,0:T(8,128)(2,1)S(1)}, u32[]{:S(2)}, u32[]{:S(2)}) %collective-permute-start.26) | collective-permute-done | bytes 49184 | tf_op jit(solution)/shard_map/ppermute | solution.py:36
  111.9 2.8 %collective-permute-done.22 = bf16[96,1536]{1,0:T(8,128)(2,1)S(1)} collective-permute-done((bf16[96,1536]{1,0:T(8,128)(2,1)S(1)}, bf16[96,1536]{1,0:T(8,128)(2,1)S(1)}, u32[]{:S(2)}, u32[]{:S(2)}) %collective-permute-start.22) | collective-permute-done | bytes 294944 | tf_op jit(solution)/shard_map/ppermute | solution.py:402
  (99 shorter events, 17.7 us)
Async XLA Ops:
  0.6 12.5 %collective-permute-start.7 = (bf16[96,1536]{1,0:T(8,128)(2,1)}, bf16[96,1536]{1,0:T(8,128)(2,1)S(1)}, u32[]{:S(2)}, u32[]{:S(2)}) collective-permute-start(bf16[96,1536]{1,0:T(8,128)(2,1)} %bitcast.26), channel_id=1, source_target_pairs={{2,0},{4,2},{6,4},{8,6},{10,8},{12,10},{14,12},{0,14},{3,1},{5,3},... | collective-permute-start | bytes 884744 | tf_op jit(solution)/shard_map/ppermute | solution.py:402
  7.1 9.3 %collective-permute-start.5 = (bf16[96,1536]{1,0:T(8,128)(2,1)}, bf16[96,1536]{1,0:T(8,128)(2,1)S(1)}, u32[]{:S(2)}, u32[]{:S(2)}) collective-permute-start(bf16[96,1536]{1,0:T(8,128)(2,1)} %bitcast.27), channel_id=1, source_target_pairs={{0,2},{2,4},{4,6},{6,8},{8,10},{10,12},{12,14},{14,0},{1,3},{3,5},... | collective-permute-start | bytes 884744 | tf_op jit(solution)/shard_map/ppermute | solution.py:402
  8.7 14.9 %collective-permute-start.3 = (bf16[64,1536]{1,0:T(8,128)(2,1)}, bf16[64,1536]{1,0:T(8,128)(2,1)S(1)}, u32[]{:S(2)}, u32[]{:S(2)}) collective-permute-start(bf16[64,1536]{1,0:T(8,128)(2,1)} %shard_map.120), channel_id=1, source_target_pairs={{1,3},{2,0},{3,5},{4,2},{5,7},{6,4},{7,9},{8,6},{9,11},{10,8},{11,... | collective-permute-start | bytes 589832 | tf_op jit(solution)/shard_map/ppermute | solution.py:418
  10.2 19.8 %collective-permute-start.4 = (bf16[128,1536]{1,0:T(8,128)(2,1)}, bf16[128,1536]{1,0:T(8,128)(2,1)S(1)}, u32[]{:S(2)}, u32[]{:S(2)}) collective-permute-start(bf16[128,1536]{1,0:T(8,128)(2,1)} %bitcast.20), channel_id=1, source_target_pairs={{0,1},{1,0},{2,3},{3,2},{4,5},{5,4},{6,7},{7,6},{8,9},{9,8},{10,11... | collective-permute-start | bytes 1179656 | tf_op jit(solution)/shard_map/ppermute | solution.py:36
  13.1 16.8 %collective-permute-start.8 = (bf16[96,1536]{1,0:T(8,128)(2,1)S(1)}, bf16[96,1536]{1,0:T(8,128)(2,1)S(1)}, u32[]{:S(2)}, u32[]{:S(2)}) collective-permute-start(bf16[96,1536]{1,0:T(8,128)(2,1)S(1)} %collective-permute-done.7.refs_2_), channel_id=1, source_target_pairs={{2,0},{4,2},{6,4},{8,6},{10,8},{12,10},{14,12},{0,14},{3,1},{5,3},... | collective-permute-start | bytes 884744 | tf_op jit(solution)/shard_map/ppermute | solution.py:402
  16.4 13.5 %collective-permute-start.6 = (bf16[96,1536]{1,0:T(8,128)(2,1)S(1)}, bf16[96,1536]{1,0:T(8,128)(2,1)S(1)}, u32[]{:S(2)}, u32[]{:S(2)}) collective-permute-start(bf16[96,1536]{1,0:T(8,128)(2,1)S(1)} %collective-permute-done.5.refs_1_), channel_id=1, source_target_pairs={{0,2},{2,4},{4,6},{6,8},{8,10},{10,12},{12,14},{14,0},{1,3},{3,5},... | collective-permute-start | bytes 884744 | tf_op jit(solution)/shard_map/ppermute | solution.py:402
  16.4 9.8 %collective-permute-start.2 = (bf16[64,1536]{1,0:T(8,128)(2,1)}, bf16[64,1536]{1,0:T(8,128)(2,1)S(1)}, u32[]{:S(2)}, u32[]{:S(2)}) collective-permute-start(bf16[64,1536]{1,0:T(8,128)(2,1)} %shard_map.120), channel_id=1, source_target_pairs={{1,2},{2,1},{3,4},{4,3},{5,6},{6,5},{7,8},{8,7},{9,10},{10,9},{11,... | collective-permute-start | bytes 589832 | tf_op jit(solution)/shard_map/ppermute | solution.py:416
  23.7 6.2 %collective-permute-start.1 = (bf16[128,768]{1,0:T(8,128)(2,1)}, bf16[128,768]{1,0:T(8,128)(2,1)S(1)}, u32[]{:S(2)}, u32[]{:S(2)}) collective-permute-start(bf16[128,768]{1,0:T(8,128)(2,1)} %get-tuple-element.48), channel_id=1, source_target_pairs={{0,1},{1,0},{2,3},{3,2},{4,5},{5,4},{6,7},{7,6},{8,9},{9,8},{10,11... | collective-permute-start | bytes 589832 | tf_op jit(solution)/shard_map/ppermute | solution.py:36
  30.0 14.8 %collective-permute-start.9 = (bf16[96,1536]{1,0:T(8,128)(2,1)S(1)}, bf16[96,1536]{1,0:T(8,128)(2,1)S(1)}, u32[]{:S(2)}, u32[]{:S(2)}) collective-permute-start(bf16[96,1536]{1,0:T(8,128)(2,1)S(1)} %collective-permute-done.6.refs_3_), channel_id=1, source_target_pairs={{0,2},{2,4},{4,6},{6,8},{8,10},{10,12},{12,14},{14,0},{1,3},{3,5},... | collective-permute-start | bytes 884744 | tf_op jit(solution)/shard_map/ppermute | solution.py:402
  35.5 9.2 %collective-permute-start.10 = (bf16[96,1536]{1,0:T(8,128)(2,1)S(1)}, bf16[96,1536]{1,0:T(8,128)(2,1)S(1)}, u32[]{:S(2)}, u32[]{:S(2)}) collective-permute-start(bf16[96,1536]{1,0:T(8,128)(2,1)S(1)} %collective-permute-done.8.refs_4_), channel_id=1, source_target_pairs={{2,0},{4,2},{6,4},{8,6},{10,8},{12,10},{14,12},{0,14},{3,1},{5,3},... | collective-permute-start | bytes 884744 | tf_op jit(solution)/shard_map/ppermute | solution.py:402
  44.8 13.0 %collective-permute-start.16 = (bf16[96,1536]{1,0:T(8,128)(2,1)}, bf16[96,1536]{1,0:T(8,128)(2,1)S(1)}, u32[]{:S(2)}, u32[]{:S(2)}) collective-permute-start(bf16[96,1536]{1,0:T(8,128)(2,1)} %get-tuple-element.74), channel_id=1, source_target_pairs={{0,2},{2,4},{4,6},{6,8},{8,10},{10,12},{12,14},{14,0},{1,3},{3,5},... | collective-permute-start | bytes 884744 | tf_op jit(solution)/shard_map/ppermute | solution.py:402
  54.8 18.3 %collective-permute-start.19 = (bf16[96,1536]{1,0:T(8,128)(2,1)}, bf16[96,1536]{1,0:T(8,128)(2,1)S(1)}, u32[]{:S(2)}, u32[]{:S(2)}) collective-permute-start(bf16[96,1536]{1,0:T(8,128)(2,1)} %get-tuple-element.77), channel_id=1, source_target_pairs={{2,0},{4,2},{6,4},{8,6},{10,8},{12,10},{14,12},{0,14},{3,1},{5,3},... | collective-permute-start | bytes 884744 | tf_op jit(solution)/shard_map/ppermute | solution.py:485
  57.7 7.2 %collective-permute-start.11 = (bf16[96,1536]{1,0:T(8,128)(2,1)S(1)}, bf16[96,1536]{1,0:T(8,128)(2,1)S(1)}, u32[]{:S(2)}, u32[]{:S(2)}) collective-permute-start(bf16[96,1536]{1,0:T(8,128)(2,1)S(1)} %collective-permute-done.9.refs_5_), channel_id=1, source_target_pairs={{0,2},{2,4},{4,6},{6,8},{8,10},{10,12},{12,14},{14,0},{1,3},{3,5},... | collective-permute-start | bytes 884744 | tf_op jit(solution)/shard_map/ppermute | solution.py:484
  58.8 38.8 %collective-permute-start.17 = (bf16[96,1536]{1,0:T(8,128)(2,1)S(1)}, bf16[96,1536]{1,0:T(8,128)(2,1)S(1)}, u32[]{:S(2)}, u32[]{:S(2)}) collective-permute-start(bf16[96,1536]{1,0:T(8,128)(2,1)S(1)} %add_convert_fusion.4), channel_id=1, source_target_pairs={{0,2},{2,4},{4,6},{6,8},{8,10},{10,12},{12,14},{14,0},{1,3},{3,5},... | collective-permute-start | bytes 884744 | tf_op jit(solution)/shard_map/ppermute | solution.py:402
  73.2 23.9 %collective-permute-start.20 = (bf16[96,1536]{1,0:T(8,128)(2,1)S(1)}, bf16[96,1536]{1,0:T(8,128)(2,1)S(1)}, u32[]{:S(2)}, u32[]{:S(2)}) collective-permute-start(bf16[96,1536]{1,0:T(8,128)(2,1)S(1)} %add_convert_fusion.2), channel_id=1, source_target_pairs={{2,0},{4,2},{6,4},{8,6},{10,8},{12,10},{14,12},{0,14},{3,1},{5,3},... | collective-permute-start | bytes 884744 | tf_op jit(solution)/shard_map/ppermute | solution.py:402
  73.3 10.1 %collective-permute-start.14 = (bf16[128,768]{1,0:T(8,128)(2,1)S(1)}, bf16[128,768]{1,0:T(8,128)(2,1)S(1)}, u32[]{:S(2)}, u32[]{:S(2)}) collective-permute-start(bf16[128,768]{1,0:T(8,128)(2,1)S(1)} %get-tuple-element.73), channel_id=1, source_target_pairs={{0,1},{1,0},{2,3},{3,2},{4,5},{5,4},{6,7},{7,6},{8,9},{9,8},{10,11... | collective-permute-start | bytes 589832 | tf_op jit(solution)/shard_map/ppermute | solution.py:36
  76.0 5.0 %collective-permute-start.24 = (bf16[32,768]{1,0:T(8,128)(2,1)S(1)}, bf16[32,768]{1,0:T(8,128)(2,1)S(1)}, u32[]{:S(2)}, u32[]{:S(2)}) collective-permute-start(bf16[32,768]{1,0:T(8,128)(2,1)S(1)} %add_convert_fusion.7), channel_id=1, source_target_pairs={{0,4},{2,6},{4,0},{6,2},{8,12},{10,14},{12,8},{14,10},{1,5},{3,7},... | collective-permute-start | bytes 147464 | tf_op jit(solution)/shard_map/ppermute | solution.py:514
  77.0 21.9 %collective-permute-start.12 = (bf16[128,1536]{1,0:T(8,128)(2,1)S(1)}, bf16[128,1536]{1,0:T(8,128)(2,1)S(1)}, u32[]{:S(2)}, u32[]{:S(2)}) collective-permute-start(bf16[128,1536]{1,0:T(8,128)(2,1)S(1)} %convolution_convert_fusion), channel_id=1, source_target_pairs={{0,1},{1,0},{2,3},{3,2},{4,5},{5,4},{6,7},{7,6},{8,9},{9,8},{10,11... | collective-permute-start | bytes 1179656 | tf_op jit(solution)/shard_map/ppermute | solution.py:36
  81.0 26.6 %collective-permute-start.25 = (bf16[32,768]{1,0:T(8,128)(2,1)S(1)}, bf16[32,768]{1,0:T(8,128)(2,1)S(1)}, u32[]{:S(2)}, u32[]{:S(2)}) collective-permute-start(bf16[32,768]{1,0:T(8,128)(2,1)S(1)} %add_convert_fusion.6), channel_id=1, source_target_pairs={{0,8},{2,10},{4,12},{6,14},{8,0},{10,2},{12,4},{14,6},{1,9},{3,11}... | collective-permute-start | bytes 147464 | tf_op jit(solution)/shard_map/ppermute | solution.py:514
  85.8 26.1 %collective-permute-start.15 = (bf16[1,128,1536]{2,1,0:T(8,128)(2,1)S(1)}, bf16[1,128,1536]{2,1,0:T(8,128)(2,1)S(1)}, u32[]{:S(2)}, u32[]{:S(2)}) collective-permute-start(bf16[1,128,1536]{2,1,0:T(8,128)(2,1)S(1)} %bitcast.25), channel_id=1, source_target_pairs={{16,0},{32,16},{48,32},{64,48},{80,64},{96,80},{112,96},{128,112},... | collective-permute-start | bytes 1179656 | tf_op jit(solution)/shard_map/ppermute | solution.py:42
  97.2 8.9 %collective-permute-start.21 = (bf16[96,1536]{1,0:T(8,128)(2,1)S(1)}, bf16[96,1536]{1,0:T(8,128)(2,1)S(1)}, u32[]{:S(2)}, u32[]{:S(2)}) collective-permute-start(bf16[96,1536]{1,0:T(8,128)(2,1)S(1)} %add_convert_fusion.1), channel_id=1, source_target_pairs={{2,0},{4,2},{6,4},{8,6},{10,8},{12,10},{14,12},{0,14},{3,1},{5,3},... | collective-permute-start | bytes 884744 | tf_op jit(solution)/shard_map/ppermute | solution.py:402
  97.7 14.2 %collective-permute-start.18 = (bf16[96,1536]{1,0:T(8,128)(2,1)S(1)}, bf16[96,1536]{1,0:T(8,128)(2,1)S(1)}, u32[]{:S(2)}, u32[]{:S(2)}) collective-permute-start(bf16[96,1536]{1,0:T(8,128)(2,1)S(1)} %add_convert_fusion.3), channel_id=1, source_target_pairs={{0,2},{2,4},{4,6},{6,8},{8,10},{10,12},{12,14},{14,0},{1,3},{3,5},... | collective-permute-start | bytes 884744 | tf_op jit(solution)/shard_map/ppermute | solution.py:402
  99.4 12.4 %collective-permute-start.13 = (bf16[1,128,1536]{2,1,0:T(8,128)(2,1)S(1)}, bf16[1,128,1536]{2,1,0:T(8,128)(2,1)S(1)}, u32[]{:S(2)}, u32[]{:S(2)}) collective-permute-start(bf16[1,128,1536]{2,1,0:T(8,128)(2,1)S(1)} %fusion.2), channel_id=1, source_target_pairs={{0,16},{16,32},{32,48},{48,64},{64,80},{80,96},{96,112},{112,128},... | collective-permute-start | bytes 1179656 | tf_op jit(solution)/shard_map/ppermute | solution.py:42
  106.2 8.4 %collective-permute-start.22 = (bf16[96,1536]{1,0:T(8,128)(2,1)S(1)}, bf16[96,1536]{1,0:T(8,128)(2,1)S(1)}, u32[]{:S(2)}, u32[]{:S(2)}) collective-permute-start(bf16[96,1536]{1,0:T(8,128)(2,1)S(1)} %add_convert_fusion), channel_id=1, source_target_pairs={{2,0},{4,2},{6,4},{8,6},{10,8},{12,10},{14,12},{0,14},{3,1},{5,3},... | collective-permute-start | bytes 884744 | tf_op jit(solution)/shard_map/ppermute | solution.py:402
  (27 other events, 460.0 us)

commit v2 on v1

--- a/solution.py
+++ b/solution.py
@@ -128,7 +128,7 @@
             theirs_out[pl.ds(at, ROWS), :] = theirs
             return carry
 
-        lax.fori_loop(0, frames // ROWS, body, 0)
+        lax.fori_loop(0, frames // ROWS, body, 0, unroll=4)
 
     copies[0].wait()
     pass_over(saved, own, other, bwd_len)
@@ -204,8 +204,8 @@
     block, factor, plan, lengths, own, got, taps, grad_hbm, grad_got, near, far, gain,
     *refs,
 ):
-    blocks = refs[:-8]
-    slope, keep_window, grad_window, hidden_saved, window, halo, product, sem = refs[-8:]
+    blocks = refs[:-7]
+    keep, grad_window, hidden_saved, window, halo, product, sem = refs[-7:]
     side = lax.axis_index("x")
     frames = grad_got.shape[0]
     mine = side * frames
@@ -241,16 +241,16 @@
         def weight(offset):
             return taps[offset - 1 : offset, lanes]
 
-        keep_window[:, lanes] = window[0, 0 : keep_window.shape[0], :].astype(jnp.bfloat16)
+        keep[2 * frames + 2 * HALO :, lanes] = window[0, 0 : 2 * frames + 4 * HALO, :].astype(jnp.bfloat16)
         span = frames + HALO
         for half in range(2):
             mixed = slide(window, 0, half * span, span, weight)
             gate = jax.nn.sigmoid(mixed)
             hidden = mixed * gate
             value = gate + hidden * (1.0 - gate)
-            slope[pl.ds(half * span, span), lanes] = value.astype(jnp.bfloat16)
-            keep = hidden[HALO:] if half == 0 else hidden[:frames]
-            hidden_saved[pl.ds(half * frames, frames), lanes] = keep.astype(jnp.bfloat16)
+            keep[pl.ds(half * span, span), lanes] = value.astype(jnp.bfloat16)
+            inner = hidden[HALO:] if half == 0 else hidden[:frames]
+            hidden_saved[pl.ds(half * frames, frames), lanes] = inner.astype(jnp.bfloat16)
         return carry
 
     lax.fori_loop(0, chunks, body, 0)
@@ -277,7 +277,7 @@
 
 
 def back_kernel(
-    factor, places, plan, lengths, grad_window, slope, window, taps, *refs
+    factor, places, plan, lengths, grad_window, kept, taps, *refs
 ):
     blocks, (grad_own, grad_other, kernel_grad, weights, conv_grad, inputs) = refs[:-6], refs[-6:]
     rows = blocks[0].shape[0]
@@ -300,7 +300,7 @@
             (((1,), (1,)), ((), ())),
             preferred_element_type=jnp.float32,
         )
-        value = (hidden_grad * slope[:, lanes].astype(jnp.float32)).astype(jnp.bfloat16).astype(jnp.float32)
+        value = (hidden_grad * kept[0 : 2 * frames + 2 * HALO, lanes].astype(jnp.float32)).astype(jnp.bfloat16).astype(jnp.float32)
         for part in range(2):
             chunk = 2 * index + part
             conv_grad[chunk, 0 : 2 * frames + 2 * HALO, :] = value[:, part * LANES : (part + 1) * LANES]
@@ -312,8 +312,9 @@
     def body(chunk, carry):
         lanes = pl.ds(pl.multiple_of(chunk * LANES, LANES), LANES)
 
-        inputs[0, 0 : window.shape[0], :] = window[:, lanes].astype(jnp.float32)
-        inputs[0, window.shape[0] :, :] = jnp.zeros((8, LANES), jnp.float32)
+        size = 2 * frames + 4 * HALO
+        inputs[0, 0:size, :] = kept[2 * frames + 2 * HALO :, lanes].astype(jnp.float32)
+        inputs[0, size:, :] = jnp.zeros((8, LANES), jnp.float32)
 
         def weight(offset):
             return taps[KW - offset : KW - offset + 1, lanes]
@@ -369,7 +370,7 @@
         out[at, :] = back.astype(jnp.bfloat16)
         return carry
 
-    lax.fori_loop(0, saved.shape[0] // ROWS, body, 0)
+    lax.fori_loop(0, saved.shape[0] // ROWS, body, 0, unroll=4)
 
 
 def totals_kernel(block, own, got, kernel, gain, kernel_out, gain_out):
@@ -441,14 +442,12 @@
     got = partner(other)
     got_fwd = partner(other_fwd)
     round_2 = ring(round_1)
-    got, near, far, grad_got, round_2 = barrier((got, near, far, grad_got, round_2))
     round_3 = ring(round_2)
-    *partial, slope, window, grad_window = call(
+    *partial, kept, grad_window = call(
         functools.partial(conv_kernel, rows, factor),
         [
             *[((rows, width), bf16)] * depth,
-            ((pair + 2 * HALO, half), bf16),
-            ((pair + 4 * HALO, half), bf16),
+            ((2 * pair + 6 * HALO, half), bf16),
             ((pair + 2 * HALO, width), bf16),
         ],
         [SMEM, SMEM] + [VMEM] * 3 + [HBM] + [VMEM] * 4,
@@ -499,14 +498,15 @@
             ((KW + 1, half), f32),
             ((half, width), bf16),
         ],
-        [SMEM, SMEM] + [VMEM] * (4 + len(blocks)),
+        [SMEM, SMEM] + [VMEM] * (3 + len(blocks)),
         [
             pltpu.VMEM((half // LANES, pair + 2 * HALO + 8, LANES), f32),
             pltpu.VMEM((1, pair + 4 * HALO + 8, LANES), f32),
         ],
         flops=4 * KW * pair * half,
         size=12 * pair * half,
-    )(plan, lengths, grad_window, slope, window, taps, *blocks)
+        limit=40<<20,
+    )(plan, lengths, grad_window, kept, taps, *blocks)
     norm_got = partner(norm_other)
     total = kernel_local.astype(bf16)
     step = 1
@@ -540,6 +540,7 @@
         functools.partial(totals_kernel, rows),
         [((KW, 1, width), f32), ((1, width), f32)],
         [VMEM] * 4,
+        limit=40<<20,
         flops=4 * KW * width,
         size=12 * KW * width,
     )(total, total_got, tap_rows, gain)

time: 117 us -> 120 us (1.026)
  Pallas kernels: 29.5 us -> 24.9 us
  starting transfers between devices: 48.8 us -> 52.7 us
  waiting for transfers between devices: 30.1 us -> 33.8 us
    ppermute x6, waiting for transfers between devices: 7.46 us -> 13 us  [ring(): lax.ppermute(pair_of[1], 'z', down)]
    ppermute x3, starting transfers between devices: 2.88 us -> 6.78 us  [per_device(): arrived = lax.ppermute(total, 'z', [(i, i ^ step) for i in range(depth)])]
    ppermute x6, starting transfers between devices: 12.9 us -> 16.6 us  [ring(): lax.ppermute(pair_of[1], 'z', down)]
    ppermute x6, waiting for transfers between devices: 11.6 us -> 15.1 us  [partner(): return lax.ppermute(array, 'x', [(0, 1), (1, 0)])]
    ppermute x3, waiting for transfers between devices: 5.1 us -> 1.69 us  [per_device(): arrived = lax.ppermute(total, 'z', [(i, i ^ step) for i in range(depth)])]
    pallas_call x1, Pallas kernels: 6.58 us -> 3.46 us  [per_device(): call(functools.partial(enter_kernel, rows), [((frames, half), bf16)] * 4...]
    ppermute x1, starting transfers between devices: 2.94 us -> 0.01 us  [per_device(): back_1 = lax.ppermute(partial[depth // 2], 'z', down)]
    ppermute x6, starting transfers between devices: 7.41 us -> 5.41 us  [ring(): lax.ppermute(pair_of[0], 'z', up)]
  transfers between devices with their start and end apart: 27 -> 27, of which waited for: 9 -> 9; matrix products, arithmetic and copies ran while one was open for 2% -> 2% of each run, Pallas kernels for 25% -> 21%
where the time goes in v2:
time: 120 us; the launch traced here: 119 us
  starting transfers between devices  52.7 us (44%)
  waiting for transfers between devices  33.8 us (28%)
  Pallas kernels  24.9 us (21%)
  local copies, waits for them, and re-layouts  3.54 us (3%)
  other arithmetic  2.33 us (2%)
    ppermute x6, starting transfers between devices, ring(): lax.ppermute(pair_of[1], 'z', down)  16.6 us
    ppermute x6, waiting for transfers between devices, partner(): return lax.ppermute(array, 'x', [(0, 1), (1, 0)])  15.1 us
    ppermute x2, starting transfers between devices, from_behind(): return lax.ppermute(array, 'section', pairs)  15.1 us
    ppermute x6, waiting for transfers between devices, ring(): lax.ppermute(pair_of[1], 'z', down)  13 us
    pallas_call x1, Pallas kernels, per_device(): call(functools.partial(conv_kernel, rows, factor), [*[((rows, width), bf1...  7.95 us
    ppermute x3, starting transfers between devices, per_device(): arrived = lax.ppermute(total, 'z', [(i, i ^ step) for i in range(depth)])  6.78 us
    pallas_call x1, Pallas kernels, per_device(): call(functools.partial(back_kernel, factor, tuple(places)), [((frames, ha...  5.85 us
    ppermute x6, starting transfers between devices, ring(): lax.ppermute(pair_of[0], 'z', up)  5.41 us
  transfers between devices with their start and end apart: 27, of which 9 were waited for; matrix products, arithmetic and copies ran while one was open for 2% of the time, Pallas kernels for 21%

profile of v2, /device:TPU:1, one launch (start us, length us, event | category | flops | bytes accessed | tf_op | source)
XLA Modules:
  0.0 119.3 jit_solution(13752092291297723560)
XLA Ops:
  0.6 6.5 %collective-permute-start.6 = (bf16[96,1536]{1,0:T(8,128)(2,1)}, bf16[96,1536]{1,0:T(8,128)(2,1)S(1)}, u32[]{:S(2)}, u32[]{:S(2)}) collective-permute-start(bf16[96,1536]{1,0:T(8,128)(2,1)} %bitcast.26), channel_id=1, source_target_pairs={{2,0},{4,2},{6,4},{8,6},{10,8},{12,10},{14,12},{0,14},{3,1},{5,3},... | collective-permute-start | bytes 884744 | tf_op jit(solution)/shard_map/ppermute | solution.py:403
  7.1 6.0 %collective-permute-done.6.refs_2_ = bf16[96,1536]{1,0:T(8,128)(2,1)S(1)} collective-permute-done((bf16[96,1536]{1,0:T(8,128)(2,1)}, bf16[96,1536]{1,0:T(8,128)(2,1)S(1)}, u32[]{:S(2)}, u32[]{:S(2)}) %collective-permute-start.6) | collective-permute-done | bytes 294944 | tf_op jit(solution)/shard_map/ppermute | solution.py:403
  13.1 3.3 %collective-permute-start.8 = (bf16[96,1536]{1,0:T(8,128)(2,1)S(1)}, bf16[96,1536]{1,0:T(8,128)(2,1)S(1)}, u32[]{:S(2)}, u32[]{:S(2)}) collective-permute-start(bf16[96,1536]{1,0:T(8,128)(2,1)S(1)} %collective-permute-done.6.refs_2_), channel_id=1, source_target_pairs={{2,0},{4,2},{6,4},{8,6},{10,8},{12,10},{14,12},{0,14},{3,1},{5,3},... | collective-permute-start | bytes 884744 | tf_op jit(solution)/shard_map/ppermute | solution.py:403
  16.4 1.6 %shard_map.120 = bf16[64,1536]{1,0:T(8,128)(2,1)} custom-call(bf16[128,1536]{1,0:T(8,128)(2,1)} %bitcast.16, bf16[128,1536]{1,0:T(8,128)(2,1)} %bitcast.29, bf16[128,1536]{1,0:T(8,128)(2,1)} %bitcast.19), custom_call_target="tpu_custom_call" | custom-call | bytes 393216 | tf_op jit(solution)/shard_map/pallas_call | solution.py:406
  21.3 3.4 %collective-permute-start.10 = (bf16[96,1536]{1,0:T(8,128)(2,1)S(1)}, bf16[96,1536]{1,0:T(8,128)(2,1)S(1)}, u32[]{:S(2)}, u32[]{:S(2)}) collective-permute-start(bf16[96,1536]{1,0:T(8,128)(2,1)S(1)} %collective-permute-done.8.refs_4_), channel_id=1, source_target_pairs={{2,0},{4,2},{6,4},{8,6},{10,8},{12,10},{14,12},{0,14},{3,1},{5,3},... | collective-permute-start | bytes 884744 | tf_op jit(solution)/shard_map/ppermute | solution.py:403
  25.3 3.5 %shard_map.119 = (bf16[128,768]{1,0:T(8,128)(2,1)}, bf16[128,768]{1,0:T(8,128)(2,1)}, bf16[128,768]{1,0:T(8,128)(2,1)}, bf16[128,768]{1,0:T(8,128)(2,1)}, f32[32,768]{1,0:T(8,128)}) custom-call(s32[1,2]{1,0:T(1,128)} %plan.5, s32[32]{0:T(128)} %lengths.5, bf16[128,1536]{1,0:T(8,128)(2,1)} %bitcast.17, bf16[128,1536]{1,0:T(8,128)(2,1)} %bitcast.30, ...), custom_call_target="tpu_custom_call" | custom-call | flops 4718592 | bytes 1966080 | tf_op jit(solution)/shard_map/pallas_call | solution.py:425
  28.8 2.5 %collective-permute-start.3 = (bf16[128,768]{1,0:T(8,128)(2,1)}, bf16[128,768]{1,0:T(8,128)(2,1)S(1)}, u32[]{:S(2)}, u32[]{:S(2)}) collective-permute-start(bf16[128,768]{1,0:T(8,128)(2,1)} %get-tuple-element.43), channel_id=1, source_target_pairs={{0,1},{1,0},{2,3},{3,2},{4,5},{5,4},{6,7},{7,6},{8,9},{9,8},{10,11... | collective-permute-start | bytes 589832 | tf_op jit(solution)/shard_map/ppermute | solution.py:36
  31.4 6.9 %collective-permute-done.3.got = bf16[128,768]{1,0:T(8,128)(2,1)S(1)} collective-permute-done((bf16[128,768]{1,0:T(8,128)(2,1)}, bf16[128,768]{1,0:T(8,128)(2,1)S(1)}, u32[]{:S(2)}, u32[]{:S(2)}) %collective-permute-start.3) | collective-permute-done | bytes 196640 | tf_op jit(solution)/shard_map/ppermute | solution.py:36
  39.1 7.9 %shard_map.122 = (bf16[96,1536]{1,0:T(8,128)(2,1)}, bf16[96,1536]{1,0:T(8,128)(2,1)}, bf16[96,1536]{1,0:T(8,128)(2,1)}, bf16[96,1536]{1,0:T(8,128)(2,1)}, bf16[9...) custom-call(s32[1,2]{1,0:T(1,128)} %plan.5, ...), custom_call_target="tpu_custom_call" | custom-call | flops 24379392 | bytes 3145728 | tf_op jit(solution)/shard_map/pallas_call | solution.py:446
  47.1 3.6 %collective-permute-start.16 = (bf16[96,1536]{1,0:T(8,128)(2,1)}, bf16[96,1536]{1,0:T(8,128)(2,1)S(1)}, u32[]{:S(2)}, u32[]{:S(2)}) collective-permute-start(bf16[96,1536]{1,0:T(8,128)(2,1)} %get-tuple-element.60), channel_id=1, source_target_pairs={{0,2},{2,4},{4,6},{6,8},{8,10},{10,12},{12,14},{14,0},{1,3},{3,5},... | collective-permute-start | bytes 884744 | tf_op jit(solution)/shard_map/ppermute | solution.py:403
  50.7 5.0 %collective-permute-done.got = bf16[128,768]{1,0:T(8,128)(2,1)} collective-permute-done((bf16[128,768]{1,0:T(8,128)(2,1)}, bf16[128,768]{1,0:T(8,128)(2,1)}, u32[]{:S(2)}, u32[]{:S(2)}) %collective-permute-start) | collective-permute-done | bytes 196640 | tf_op jit(solution)/shard_map/ppermute | solution.py:36
  55.7 4.2 %shard_map.121 = (bf16[128,768]{1,0:T(8,128)(2,1)}, bf16[128,768]{1,0:T(8,128)(2,1)}) custom-call(s32[1,2]{1,0:T(1,128)} %plan.5, s32[32]{0:T(128)} %lengths.5, bf16[128,768]{1,0:T(8,128)(2,1)} %get-tuple-element.38.own, bf16[128,768]{1,0:T(8,128)(2,1)} %collective-permute-done.got, f32[32,768]{1,0:T(8,128)} %get-tuple-element.40.taps, ...), custom_call_target="tpu_custom_call" | custom-call | flops 12189696 | bytes 1572864 | tf_op jit(solution)/shard_map/pallas_call | solution.py:466
  60.0 1.5 %collective-permute-start.11 = (bf16[96,1536]{1,0:T(8,128)(2,1)S(1)}, bf16[96,1536]{1,0:T(8,128)(2,1)S(1)}, u32[]{:S(2)}, u32[]{:S(2)}) collective-permute-start(bf16[96,1536]{1,0:T(8,128)(2,1)S(1)} %collective-permute-done.9.refs_5_), channel_id=1, source_target_pairs={{0,2},{2,4},{4,6},{6,8},{8,10},{10,12},{12,14},{14,0},{1,3},{3,5},... | collective-permute-start | bytes 884744 | tf_op jit(solution)/shard_map/ppermute | solution.py:483
  62.8 4.0 %collective-permute-done.11.refs_7_ = bf16[96,1536]{1,0:T(8,128)(2,1)S(1)} collective-permute-done((bf16[96,1536]{1,0:T(8,128)(2,1)S(1)}, bf16[96,1536]{1,0:T(8,128)(2,1)S(1)}, u32[]{:S(2)}, u32[]{:S(2)}) %collective-permute-start.11) | collective-permute-done | bytes 294944 | tf_op jit(solution)/shard_map/ppermute | solution.py:483
  68.0 5.8 %shard_map.123 = (bf16[128,768]{1,0:T(8,128)(2,1)S(1)}, bf16[128,768]{1,0:T(8,128)(2,1)S(1)}, f32[32,768]{1,0:T(8,128)S(1)}, bf16[768,1536]{1,0:T(8,128)(2,1)S(1)}) custom-call(s32[1,2]{1,0:T(1,128)S(1)} %copy-done.8, s32[32]{0:T(128)S(1)} %copy-done.9, bf16[288,1536]{1,0:T(8,128)(2,1)S(1)} %copy-done.3, bf16[608,768]{1,0:T(8,128)(2,1)S(1)} %copy-done.2, ...), custom_call_target="tpu_custom_call" | custom-call | flops 24379392 | bytes 2359296 | tf_op jit(solution)/shard_map/pallas_call | solution.py:493
  74.6 2.6 %collective-permute-start.20 = (bf16[96,1536]{1,0:T(8,128)(2,1)S(1)}, bf16[96,1536]{1,0:T(8,128)(2,1)S(1)}, u32[]{:S(2)}, u32[]{:S(2)}) collective-permute-start(bf16[96,1536]{1,0:T(8,128)(2,1)S(1)} %add_convert_fusion.2), channel_id=1, source_target_pairs={{2,0},{4,2},{6,4},{8,6},{10,8},{12,10},{14,12},{0,14},{3,1},{5,3},... | collective-permute-start | bytes 884744 | tf_op jit(solution)/shard_map/ppermute | solution.py:403
  79.7 1.7 %collective-permute-done.24 = bf16[32,768]{1,0:T(8,128)(2,1)S(1)} collective-permute-done((bf16[32,768]{1,0:T(8,128)(2,1)S(1)}, bf16[32,768]{1,0:T(8,128)(2,1)S(1)}, u32[]{:S(2)}, u32[]{:S(2)}) %collective-permute-start.24) | collective-permute-done | bytes 49184 | tf_op jit(solution)/shard_map/ppermute | solution.py:514
  81.4 5.5 %collective-permute-start.25 = (bf16[32,768]{1,0:T(8,128)(2,1)S(1)}, bf16[32,768]{1,0:T(8,128)(2,1)S(1)}, u32[]{:S(2)}, u32[]{:S(2)}) collective-permute-start(bf16[32,768]{1,0:T(8,128)(2,1)S(1)} %add_convert_fusion.6), channel_id=1, source_target_pairs={{0,8},{2,10},{4,12},{6,14},{8,0},{10,2},{12,4},{14,6},{1,9},{3,11}... | collective-permute-start | bytes 147464 | tf_op jit(solution)/shard_map/ppermute | solution.py:514
  87.9 11.4 %collective-permute-start.15 = (bf16[1,128,1536]{2,1,0:T(8,128)(2,1)S(1)}, bf16[1,128,1536]{2,1,0:T(8,128)(2,1)S(1)}, u32[]{:S(2)}, u32[]{:S(2)}) collective-permute-start(bf16[1,128,1536]{2,1,0:T(8,128)(2,1)S(1)} %bitcast.25), channel_id=1, source_target_pairs={{16,0},{32,16},{48,32},{64,48},{80,64},{96,80},{112,96},{128,112},... | collective-permute-start | bytes 1179656 | tf_op jit(solution)/shard_map/ppermute | solution.py:42
  99.6 1.5 %collective-permute-start.18 = (bf16[96,1536]{1,0:T(8,128)(2,1)S(1)}, bf16[96,1536]{1,0:T(8,128)(2,1)S(1)}, u32[]{:S(2)}, u32[]{:S(2)}) collective-permute-start(bf16[96,1536]{1,0:T(8,128)(2,1)S(1)} %add_convert_fusion.3), channel_id=1, source_target_pairs={{0,2},{2,4},{4,6},{6,8},{8,10},{10,12},{12,14},{14,0},{1,3},{3,5},... | collective-permute-start | bytes 884744 | tf_op jit(solution)/shard_map/ppermute | solution.py:403
  101.7 3.6 %collective-permute-start.13 = (bf16[1,128,1536]{2,1,0:T(8,128)(2,1)S(1)}, bf16[1,128,1536]{2,1,0:T(8,128)(2,1)S(1)}, u32[]{:S(2)}, u32[]{:S(2)}) collective-permute-start(bf16[1,128,1536]{2,1,0:T(8,128)(2,1)S(1)} %fusion.2), channel_id=1, source_target_pairs={{0,16},{16,32},{32,48},{48,64},{64,80},{80,96},{96,112},{112,128},... | collective-permute-start | bytes 1179656 | tf_op jit(solution)/shard_map/ppermute | solution.py:42
  105.3 3.1 %collective-permute-done.21 = bf16[96,1536]{1,0:T(8,128)(2,1)S(1)} collective-permute-done((bf16[96,1536]{1,0:T(8,128)(2,1)S(1)}, bf16[96,1536]{1,0:T(8,128)(2,1)S(1)}, u32[]{:S(2)}, u32[]{:S(2)}) %collective-permute-start.21) | collective-permute-done | bytes 294944 | tf_op jit(solution)/shard_map/ppermute | solution.py:403
  109.3 3.2 %collective-permute-done.26.got = bf16[32,768]{1,0:T(8,128)(2,1)S(1)} collective-permute-done((bf16[32,768]{1,0:T(8,128)(2,1)S(1)}, bf16[32,768]{1,0:T(8,128)(2,1)S(1)}, u32[]{:S(2)}, u32[]{:S(2)}) %collective-permute-start.26) | collective-permute-done | bytes 49184 | tf_op jit(solution)/shard_map/ppermute | solution.py:36
  113.4 3.5 %collective-permute-done.22 = bf16[96,1536]{1,0:T(8,128)(2,1)S(1)} collective-permute-done((bf16[96,1536]{1,0:T(8,128)(2,1)S(1)}, bf16[96,1536]{1,0:T(8,128)(2,1)S(1)}, u32[]{:S(2)}, u32[]{:S(2)}) %collective-permute-start.22) | collective-permute-done | bytes 294944 | tf_op jit(solution)/shard_map/ppermute | solution.py:403
  (95 shorter events, 16.3 us)
Async XLA Ops:
  0.6 12.5 %collective-permute-start.6 = (bf16[96,1536]{1,0:T(8,128)(2,1)}, bf16[96,1536]{1,0:T(8,128)(2,1)S(1)}, u32[]{:S(2)}, u32[]{:S(2)}) collective-permute-start(bf16[96,1536]{1,0:T(8,128)(2,1)} %bitcast.26), channel_id=1, source_target_pairs={{2,0},{4,2},{6,4},{8,6},{10,8},{12,10},{14,12},{0,14},{3,1},{5,3},... | collective-permute-start | bytes 884744 | tf_op jit(solution)/shard_map/ppermute | solution.py:403
  7.1 9.3 %collective-permute-start.5 = (bf16[96,1536]{1,0:T(8,128)(2,1)}, bf16[96,1536]{1,0:T(8,128)(2,1)S(1)}, u32[]{:S(2)}, u32[]{:S(2)}) collective-permute-start(bf16[96,1536]{1,0:T(8,128)(2,1)} %bitcast.27), channel_id=1, source_target_pairs={{0,2},{2,4},{4,6},{6,8},{8,10},{10,12},{12,14},{14,0},{1,3},{3,5},... | collective-permute-start | bytes 884744 | tf_op jit(solution)/shard_map/ppermute | solution.py:403
  13.1 8.1 %collective-permute-start.8 = (bf16[96,1536]{1,0:T(8,128)(2,1)S(1)}, bf16[96,1536]{1,0:T(8,128)(2,1)S(1)}, u32[]{:S(2)}, u32[]{:S(2)}) collective-permute-start(bf16[96,1536]{1,0:T(8,128)(2,1)S(1)} %collective-permute-done.6.refs_2_), channel_id=1, source_target_pairs={{2,0},{4,2},{6,4},{8,6},{10,8},{12,10},{14,12},{0,14},{3,1},{5,3},... | collective-permute-start | bytes 884744 | tf_op jit(solution)/shard_map/ppermute | solution.py:403
  16.4 8.2 %collective-permute-start.7 = (bf16[96,1536]{1,0:T(8,128)(2,1)S(1)}, bf16[96,1536]{1,0:T(8,128)(2,1)S(1)}, u32[]{:S(2)}, u32[]{:S(2)}) collective-permute-start(bf16[96,1536]{1,0:T(8,128)(2,1)S(1)} %collective-permute-done.5.refs_1_), channel_id=1, source_target_pairs={{0,2},{2,4},{4,6},{6,8},{8,10},{10,12},{12,14},{14,0},{1,3},{3,5},... | collective-permute-start | bytes 884744 | tf_op jit(solution)/shard_map/ppermute | solution.py:403
  18.1 10.8 %collective-permute-start.2 = (bf16[64,1536]{1,0:T(8,128)(2,1)}, bf16[64,1536]{1,0:T(8,128)(2,1)S(1)}, u32[]{:S(2)}, u32[]{:S(2)}) collective-permute-start(bf16[64,1536]{1,0:T(8,128)(2,1)} %shard_map.120), channel_id=1, source_target_pairs={{1,3},{2,0},{3,5},{4,2},{5,7},{6,4},{7,9},{8,6},{9,11},{10,8},{11,... | collective-permute-start | bytes 589832 | tf_op jit(solution)/shard_map/ppermute | solution.py:419
  19.5 18.8 %collective-permute-start.4 = (bf16[128,1536]{1,0:T(8,128)(2,1)}, bf16[128,1536]{1,0:T(8,128)(2,1)S(1)}, u32[]{:S(2)}, u32[]{:S(2)}) collective-permute-start(bf16[128,1536]{1,0:T(8,128)(2,1)} %bitcast.20), channel_id=1, source_target_pairs={{0,1},{1,0},{2,3},{3,2},{4,5},{5,4},{6,7},{7,6},{8,9},{9,8},{10,11... | collective-permute-start | bytes 1179656 | tf_op jit(solution)/shard_map/ppermute | solution.py:36
  21.3 25.8 %collective-permute-start.10 = (bf16[96,1536]{1,0:T(8,128)(2,1)S(1)}, bf16[96,1536]{1,0:T(8,128)(2,1)S(1)}, u32[]{:S(2)}, u32[]{:S(2)}) collective-permute-start(bf16[96,1536]{1,0:T(8,128)(2,1)S(1)} %collective-permute-done.8.refs_4_), channel_id=1, source_target_pairs={{2,0},{4,2},{6,4},{8,6},{10,8},{12,10},{14,12},{0,14},{3,1},{5,3},... | collective-permute-start | bytes 884744 | tf_op jit(solution)/shard_map/ppermute | solution.py:403
  24.7 22.4 %collective-permute-start.9 = (bf16[96,1536]{1,0:T(8,128)(2,1)S(1)}, bf16[96,1536]{1,0:T(8,128)(2,1)S(1)}, u32[]{:S(2)}, u32[]{:S(2)}) collective-permute-start(bf16[96,1536]{1,0:T(8,128)(2,1)S(1)} %collective-permute-done.7.refs_3_), channel_id=1, source_target_pairs={{0,2},{2,4},{4,6},{6,8},{8,10},{10,12},{12,14},{14,0},{1,3},{3,5},... | collective-permute-start | bytes 884744 | tf_op jit(solution)/shard_map/ppermute | solution.py:403
  24.7 6.7 %collective-permute-start.1 = (bf16[64,1536]{1,0:T(8,128)(2,1)}, bf16[64,1536]{1,0:T(8,128)(2,1)S(1)}, u32[]{:S(2)}, u32[]{:S(2)}) collective-permute-start(bf16[64,1536]{1,0:T(8,128)(2,1)} %shard_map.120), channel_id=1, source_target_pairs={{1,2},{2,1},{3,4},{4,3},{5,6},{6,5},{7,8},{8,7},{9,10},{10,9},{11,... | collective-permute-start | bytes 589832 | tf_op jit(solution)/shard_map/ppermute | solution.py:417
  28.8 9.4 %collective-permute-start.3 = (bf16[128,768]{1,0:T(8,128)(2,1)}, bf16[128,768]{1,0:T(8,128)(2,1)S(1)}, u32[]{:S(2)}, u32[]{:S(2)}) collective-permute-start(bf16[128,768]{1,0:T(8,128)(2,1)} %get-tuple-element.43), channel_id=1, source_target_pairs={{0,1},{1,0},{2,3},{3,2},{4,5},{5,4},{6,7},{7,6},{8,9},{9,8},{10,11... | collective-permute-start | bytes 589832 | tf_op jit(solution)/shard_map/ppermute | solution.py:36
  47.1 14.4 %collective-permute-start.16 = (bf16[96,1536]{1,0:T(8,128)(2,1)}, bf16[96,1536]{1,0:T(8,128)(2,1)S(1)}, u32[]{:S(2)}, u32[]{:S(2)}) collective-permute-start(bf16[96,1536]{1,0:T(8,128)(2,1)} %get-tuple-element.60), channel_id=1, source_target_pairs={{0,2},{2,4},{4,6},{6,8},{8,10},{10,12},{12,14},{14,0},{1,3},{3,5},... | collective-permute-start | bytes 884744 | tf_op jit(solution)/shard_map/ppermute | solution.py:403
  50.7 5.0 %collective-permute-start = (bf16[128,768]{1,0:T(8,128)(2,1)}, bf16[128,768]{1,0:T(8,128)(2,1)}, u32[]{:S(2)}, u32[]{:S(2)}) collective-permute-start(bf16[128,768]{1,0:T(8,128)(2,1)} %get-tuple-element.39), channel_id=1, source_target_pairs={{0,1},{1,0},{2,3},{3,2},{4,5},{5,4},{6,7},{7,6},{8,9},{9,8},{10,11... | collective-permute-start | bytes 589832 | tf_op jit(solution)/shard_map/ppermute | solution.py:36
  60.0 14.5 %collective-permute-start.19 = (bf16[96,1536]{1,0:T(8,128)(2,1)}, bf16[96,1536]{1,0:T(8,128)(2,1)S(1)}, u32[]{:S(2)}, u32[]{:S(2)}) collective-permute-start(bf16[96,1536]{1,0:T(8,128)(2,1)} %get-tuple-element.63), channel_id=1, source_target_pairs={{2,0},{4,2},{6,4},{8,6},{10,8},{12,10},{14,12},{0,14},{3,1},{5,3},... | collective-permute-start | bytes 884744 | tf_op jit(solution)/shard_map/ppermute | solution.py:484
  60.0 6.8 %collective-permute-start.11 = (bf16[96,1536]{1,0:T(8,128)(2,1)S(1)}, bf16[96,1536]{1,0:T(8,128)(2,1)S(1)}, u32[]{:S(2)}, u32[]{:S(2)}) collective-permute-start(bf16[96,1536]{1,0:T(8,128)(2,1)S(1)} %collective-permute-done.9.refs_5_), channel_id=1, source_target_pairs={{0,2},{2,4},{4,6},{6,8},{8,10},{10,12},{12,14},{14,0},{1,3},{3,5},... | collective-permute-start | bytes 884744 | tf_op jit(solution)/shard_map/ppermute | solution.py:483
  62.5 37.0 %collective-permute-start.17 = (bf16[96,1536]{1,0:T(8,128)(2,1)S(1)}, bf16[96,1536]{1,0:T(8,128)(2,1)S(1)}, u32[]{:S(2)}, u32[]{:S(2)}) collective-permute-start(bf16[96,1536]{1,0:T(8,128)(2,1)S(1)} %add_convert_fusion.4), channel_id=1, source_target_pairs={{0,2},{2,4},{4,6},{6,8},{8,10},{10,12},{12,14},{14,0},{1,3},{3,5},... | collective-permute-start | bytes 884744 | tf_op jit(solution)/shard_map/ppermute | solution.py:403
  74.6 24.8 %collective-permute-start.20 = (bf16[96,1536]{1,0:T(8,128)(2,1)S(1)}, bf16[96,1536]{1,0:T(8,128)(2,1)S(1)}, u32[]{:S(2)}, u32[]{:S(2)}) collective-permute-start(bf16[96,1536]{1,0:T(8,128)(2,1)S(1)} %add_convert_fusion.2), channel_id=1, source_target_pairs={{2,0},{4,2},{6,4},{8,6},{10,8},{12,10},{14,12},{0,14},{3,1},{5,3},... | collective-permute-start | bytes 884744 | tf_op jit(solution)/shard_map/ppermute | solution.py:403
  77.2 9.7 %collective-permute-start.14 = (bf16[128,768]{1,0:T(8,128)(2,1)S(1)}, bf16[128,768]{1,0:T(8,128)(2,1)S(1)}, u32[]{:S(2)}, u32[]{:S(2)}) collective-permute-start(bf16[128,768]{1,0:T(8,128)(2,1)S(1)} %get-tuple-element.59), channel_id=1, source_target_pairs={{0,1},{1,0},{2,3},{3,2},{4,5},{5,4},{6,7},{7,6},{8,9},{9,8},{10,11... | collective-permute-start | bytes 589832 | tf_op jit(solution)/shard_map/ppermute | solution.py:36
  78.6 22.5 %collective-permute-start.12 = (bf16[128,1536]{1,0:T(8,128)(2,1)S(1)}, bf16[128,1536]{1,0:T(8,128)(2,1)S(1)}, u32[]{:S(2)}, u32[]{:S(2)}) collective-permute-start(bf16[128,1536]{1,0:T(8,128)(2,1)S(1)} %convolution_convert_fusion), channel_id=1, source_target_pairs={{0,1},{1,0},{2,3},{3,2},{4,5},{5,4},{6,7},{7,6},{8,9},{9,8},{10,11... | collective-permute-start | bytes 1179656 | tf_op jit(solution)/shard_map/ppermute | solution.py:36
  81.4 27.7 %collective-permute-start.25 = (bf16[32,768]{1,0:T(8,128)(2,1)S(1)}, bf16[32,768]{1,0:T(8,128)(2,1)S(1)}, u32[]{:S(2)}, u32[]{:S(2)}) collective-permute-start(bf16[32,768]{1,0:T(8,128)(2,1)S(1)} %add_convert_fusion.6), channel_id=1, source_target_pairs={{0,8},{2,10},{4,12},{6,14},{8,0},{10,2},{12,4},{14,6},{1,9},{3,11}... | collective-permute-start | bytes 147464 | tf_op jit(solution)/shard_map/ppermute | solution.py:514
  87.9 25.5 %collective-permute-start.15 = (bf16[1,128,1536]{2,1,0:T(8,128)(2,1)S(1)}, bf16[1,128,1536]{2,1,0:T(8,128)(2,1)S(1)}, u32[]{:S(2)}, u32[]{:S(2)}) collective-permute-start(bf16[1,128,1536]{2,1,0:T(8,128)(2,1)S(1)} %bitcast.25), channel_id=1, source_target_pairs={{16,0},{32,16},{48,32},{64,48},{80,64},{96,80},{112,96},{128,112},... | collective-permute-start | bytes 1179656 | tf_op jit(solution)/shard_map/ppermute | solution.py:42
  99.4 8.9 %collective-permute-start.21 = (bf16[96,1536]{1,0:T(8,128)(2,1)S(1)}, bf16[96,1536]{1,0:T(8,128)(2,1)S(1)}, u32[]{:S(2)}, u32[]{:S(2)}) collective-permute-start(bf16[96,1536]{1,0:T(8,128)(2,1)S(1)} %add_convert_fusion.1), channel_id=1, source_target_pairs={{2,0},{4,2},{6,4},{8,6},{10,8},{12,10},{14,12},{0,14},{3,1},{5,3},... | collective-permute-start | bytes 884744 | tf_op jit(solution)/shard_map/ppermute | solution.py:403
  99.6 13.7 %collective-permute-start.18 = (bf16[96,1536]{1,0:T(8,128)(2,1)S(1)}, bf16[96,1536]{1,0:T(8,128)(2,1)S(1)}, u32[]{:S(2)}, u32[]{:S(2)}) collective-permute-start(bf16[96,1536]{1,0:T(8,128)(2,1)S(1)} %add_convert_fusion.3), channel_id=1, source_target_pairs={{0,2},{2,4},{4,6},{6,8},{8,10},{10,12},{12,14},{14,0},{1,3},{3,5},... | collective-permute-start | bytes 884744 | tf_op jit(solution)/shard_map/ppermute | solution.py:403
  101.7 11.7 %collective-permute-start.13 = (bf16[1,128,1536]{2,1,0:T(8,128)(2,1)S(1)}, bf16[1,128,1536]{2,1,0:T(8,128)(2,1)S(1)}, u32[]{:S(2)}, u32[]{:S(2)}) collective-permute-start(bf16[1,128,1536]{2,1,0:T(8,128)(2,1)S(1)} %fusion.2), channel_id=1, source_target_pairs={{0,16},{16,32},{32,48},{48,64},{64,80},{80,96},{96,112},{112,128},... | collective-permute-start | bytes 1179656 | tf_op jit(solution)/shard_map/ppermute | solution.py:42
  108.4 8.4 %collective-permute-start.22 = (bf16[96,1536]{1,0:T(8,128)(2,1)S(1)}, bf16[96,1536]{1,0:T(8,128)(2,1)S(1)}, u32[]{:S(2)}, u32[]{:S(2)}) collective-permute-start(bf16[96,1536]{1,0:T(8,128)(2,1)S(1)} %add_convert_fusion), channel_id=1, source_target_pairs={{2,0},{4,2},{6,4},{8,6},{10,8},{12,10},{14,12},{0,14},{3,1},{5,3},... | collective-permute-start | bytes 884744 | tf_op jit(solution)/shard_map/ppermute | solution.py:403
  (25 other events, 420.7 us)

commit v3 on v2

--- a/solution.py
+++ b/solution.py
@@ -75,20 +75,42 @@
     return jnp.where(first, even, odd), jnp.where(first, odd, even)
 
 
-def edge_kernel(saved, fwd, grad, edges, sems):
-    frames = saved.shape[0]
+def edge_kernel(
+    block, plan_hbm, lengths_hbm, saved_hbm, fwd_hbm, grad_hbm, gain_hbm,
+    to_near, to_far, plan, lengths, gain, rows, sems,
+):
+    frames = saved_hbm.shape[0]
+    half = to_near.shape[1]
     side = lax.axis_index("x")
-    wide = pl.ds(pl.multiple_of(side * (frames - 2 * HALO), HALO), 2 * HALO)
-    thin = pl.ds(pl.multiple_of(side * (frames - HALO), HALO), HALO)
-    copies = [
-        pltpu.make_async_copy(saved.at[wide, :], edges.at[0 : 2 * HALO, :], sems.at[0]),
-        pltpu.make_async_copy(fwd.at[thin, :], edges.at[2 * HALO : 3 * HALO, :], sems.at[1]),
-        pltpu.make_async_copy(grad.at[thin, :], edges.at[3 * HALO : 4 * HALO, :], sems.at[2]),
-    ]
+    wide = pl.multiple_of(side * (frames - 2 * HALO), HALO)
+    thin = pl.multiple_of(side * (frames - HALO), HALO)
+    pairs = (
+        (plan_hbm, plan),
+        (lengths_hbm, lengths),
+        (gain_hbm, gain),
+        (saved_hbm.at[pl.ds(wide, 2 * HALO), :], rows.at[0 : 2 * HALO, :]),
+        (fwd_hbm.at[pl.ds(thin, HALO), :], rows.at[2 * HALO : 3 * HALO, :]),
+        (grad_hbm.at[pl.ds(thin, HALO), :], rows.at[3 * HALO : 4 * HALO, :]),
+    )
+    copies = [pltpu.make_async_copy(a, b, sems.at[i]) for i, (a, b) in enumerate(pairs)]
     for copy in copies:
         copy.start()
     for copy in copies:
         copy.wait()
+    origin = lax.axis_index("z") * 2 * frames + side * frames
+    fwd_len = lengths[plan[0, 0]]
+    bwd_len = lengths[plan[0, 1]]
+    gain_row = gain[...]
+    for at, start, length in ((0, wide, bwd_len), (HALO, wide + HALO, bwd_len), (2 * HALO, thin, fwd_len)):
+        value = conv_input(rows[at : at + HALO, :], gain_row, origin + start, length)
+        mine, theirs = both(value, block, side == 0)
+        to_far[at : at + HALO, :] = mine
+        to_near[at : at + HALO, :] = theirs
+    for part in range(2):
+        at = (3 + part) * HALO
+        value = rows[3 * HALO : 4 * HALO, part * half : (part + 1) * half]
+        to_far[at : at + HALO, :] = value
+        to_near[at : at + HALO, :] = value
 
 
 def enter_kernel(
@@ -147,13 +169,9 @@
     return total
 
 
-def fill_halo(block, halo, near, far, gain, spots, origin, length):
+def outside(near, far, rows, lanes, ahead):
     first = lax.axis_index("x") == 0
-    gain_row = gain[...]
-    for row, out_row, start, ahead in spots:
-        rows = jnp.where(first == ahead, near[row : row + ROWS, :], far[row : row + ROWS, :])
-        value = conv_input(rows, gain_row, origin + start, length)
-        halo[out_row : out_row + ROWS, :] = both(value, block, first)[0]
+    return jnp.where(first == ahead, near[rows, lanes], far[rows, lanes])
 
 
 def store_rows(buffer, chunk, row, values):
@@ -162,22 +180,20 @@
     buffer[chunk, pl.ds(row, values.shape[0]), :] = values.astype(jnp.float32)
 
 
-def fwd_kernel(block, plan, lengths, own, got, taps, near, far, gain, hidden_own, hidden_other, window, halo):
+def fwd_kernel(own, got, taps, near, far, hidden_own, hidden_other, window):
     side = lax.axis_index("x")
     frames = own.shape[0]
     mine = side * frames
     theirs = frames - mine
-    spots = ((2 * HALO, 0, -HALO, True), (2 * HALO, HALO, 2 * frames, False))
-    origin = lax.axis_index("z") * 2 * frames
-    fill_halo(block, halo, near, far, gain, spots, origin, lengths[plan[0, 0]])
+    edge = slice(2 * HALO, 3 * HALO)
 
     def body(chunk, carry):
         lanes = pl.ds(pl.multiple_of(chunk * LANES, LANES), LANES)
         put = functools.partial(store_rows, window, 0)
-        put(0, halo[0:HALO, lanes])
+        put(0, outside(near, far, edge, lanes, True))
         put(HALO + mine, own[:, lanes])
         put(HALO + theirs, got[:, lanes])
-        put(HALO + 2 * frames, halo[HALO:, lanes])
+        put(HALO + 2 * frames, outside(near, far, edge, lanes, False))
         put(2 * HALO + 2 * frames, jnp.zeros((8, LANES), jnp.float32))
 
         def weight(offset):
@@ -201,11 +217,11 @@
 
 
 def conv_kernel(
-    block, factor, plan, lengths, own, got, taps, grad_hbm, grad_got, near, far, gain,
+    factor, own, got, taps, grad_hbm, grad_got, near, far,
     *refs,
 ):
-    blocks = refs[:-7]
-    keep, grad_window, hidden_saved, window, halo, product, sem = refs[-7:]
+    blocks = refs[:-6]
+    keep, grad_window, hidden_saved, window, product, sem = refs[-6:]
     side = lax.axis_index("x")
     frames = grad_got.shape[0]
     mine = side * frames
@@ -214,28 +230,23 @@
     copy.start()
     theirs = frames - mine
     chunks = own.shape[1] // LANES
-    first = side == 0
-    origin = lax.axis_index("z") * 2 * frames
-    spots = (
-        (0, 0, -2 * HALO, True),
-        (HALO, HALO, -HALO, True),
-        (0, 2 * HALO, 2 * frames, False),
-        (HALO, 3 * HALO, 2 * frames + HALO, False),
-    )
-    fill_halo(block, halo, near, far, gain, spots, origin, lengths[plan[0, 1]])
-
+    half = own.shape[1]
+    for part in range(2):
+        rows = slice((3 + part) * HALO, (4 + part) * HALO)
+        lanes = slice(part * half, (part + 1) * half)
+        grad_window[0:HALO, lanes] = outside(near, far, rows, slice(None), True)
+        grad_window[HALO + 2 * frames :, lanes] = outside(near, far, rows, slice(None), False)
     grad_window[pl.ds(pl.multiple_of(HALO + theirs, HALO), frames), :] = grad_got[...]
-    grad_window[0:HALO, :] = jnp.where(first, near[3 * HALO :, :], far[3 * HALO :, :])
-    grad_window[HALO + 2 * frames :, :] = jnp.where(first, far[3 * HALO :, :], near[3 * HALO :, :])
+    edge = slice(0, 2 * HALO)
 
     def body(chunk, carry):
         lanes = pl.ds(pl.multiple_of(chunk * LANES, LANES), LANES)
 
         put = functools.partial(store_rows, window, 0)
-        put(0, halo[0 : 2 * HALO, lanes])
+        put(0, outside(near, far, edge, lanes, True))
         put(2 * HALO + mine, own[:, lanes])
         put(2 * HALO + theirs, got[:, lanes])
-        put(2 * HALO + 2 * frames, halo[2 * HALO :, lanes])
+        put(2 * HALO + 2 * frames, outside(near, far, edge, lanes, False))
         put(4 * HALO + 2 * frames, jnp.zeros((8, LANES), jnp.float32))
 
         def weight(offset):
@@ -382,6 +393,14 @@
     gain_out[...] = jnp.sum(kernel[:, 0, :] * total, axis=0, keepdims=True) / gain[...]
 
 
+def relay_kernel(source, out):
+    out[...] = source[...]
+
+
+def finish_kernel(first, second, third, out):
+    out[...] = first[...].astype(jnp.float32) + second[...].astype(jnp.float32) + third[...].astype(jnp.float32)
+
+
 def per_device(fwd_input, saved_input, grad_in, gain, kernel, w_out, lengths, plan):
     frames, width = fwd_input.shape[1:]
     depth = lax.axis_size("z")
@@ -403,20 +422,26 @@
         return lax.ppermute(pair_of[0], "z", up), lax.ppermute(pair_of[1], "z", down)
 
     grad_got = partner(upstream)
-    (edges,) = call(
-        edge_kernel,
-        [((4 * HALO, width), bf16)],
-        [HBM] * 3,
-        [pltpu.SemaphoreType.DMA((3,))],
+    to_near, to_far = call(
+        functools.partial(edge_kernel, rows),
+        [((5 * HALO, half), bf16)] * 2,
+        [HBM] * 6,
+        [
+            pltpu.SMEM(plan.shape, jnp.int32),
+            pltpu.SMEM(lengths.shape, jnp.int32),
+            pltpu.VMEM(gain.shape, f32),
+            pltpu.VMEM((4 * HALO, width), bf16),
+            pltpu.SemaphoreType.DMA((6,)),
+        ],
         limit=None,
         size=16 * HALO * width,
-    )(saved_rows, fwd_rows, upstream)
+    )(plan, lengths, saved_rows, fwd_rows, upstream, gain)
     count = 2 * depth
     tm = ("z", "x")
     hops = [(t, t + 1 if t % 2 else t - 1) for t in range(count)]
-    near = lax.ppermute(edges, tm, [(a, b) for a, b in hops if 0 <= b < count])
+    near = lax.ppermute(to_near, tm, [(a, b) for a, b in hops if 0 <= b < count])
     hops = [(t, t + 2 if t % 2 else t - 2) for t in range(count)]
-    far = lax.ppermute(edges, tm, [(a, b) for a, b in hops if 0 <= b < count])
+    far = lax.ppermute(to_far, tm, [(a, b) for a, b in hops if 0 <= b < count])
 
     block = w_out[0]
     round_1 = ring((block, block))
@@ -444,37 +469,33 @@
     round_2 = ring(round_1)
     round_3 = ring(round_2)
     *partial, kept, grad_window = call(
-        functools.partial(conv_kernel, rows, factor),
+        functools.partial(conv_kernel, factor),
         [
             *[((rows, width), bf16)] * depth,
             ((2 * pair + 6 * HALO, half), bf16),
             ((pair + 2 * HALO, width), bf16),
         ],
-        [SMEM, SMEM] + [VMEM] * 3 + [HBM] + [VMEM] * 4,
+        [VMEM] * 3 + [HBM] + [VMEM] * 3,
         [
             pltpu.VMEM((pair, half), bf16),
             pltpu.VMEM((1, pair + 4 * HALO + 8, LANES), f32),
-            pltpu.VMEM((4 * HALO, half), bf16),
             pltpu.VMEM((depth, rows, 2 * LANES), bf16),
             pltpu.SemaphoreType.DMA(()),
         ],
         limit=None,
         flops=2 * KW * 2 * pair * half,
         size=16 * pair * half,
-    )(plan, lengths, own, got, taps, upstream, grad_got, near, far, gain)
+    )(own, got, taps, upstream, grad_got, near, far)
 
     hidden_own, hidden_other = call(
-        functools.partial(fwd_kernel, rows),
+        fwd_kernel,
         [((frames, half), bf16)] * 2,
-        [SMEM, SMEM] + [VMEM] * 6,
-        [
-            pltpu.VMEM((1, pair + 2 * HALO + 8, LANES), f32),
-            pltpu.VMEM((2 * HALO, half), bf16),
-        ],
+        [VMEM] * 5,
+        [pltpu.VMEM((1, pair + 2 * HALO + 8, LANES), f32)],
         limit=None,
         flops=2 * KW * pair * half,
         size=8 * pair * half,
-    )(plan, lengths, own_fwd, got_fwd, taps, near, far, gain)
+    )(own_fwd, got_fwd, taps, near, far)
     partial, round_3 = barrier((partial, round_3))
 
     def plus(arrived, own_part):
@@ -518,7 +539,9 @@
 
     back_3 = ring((plus(back_2[0], partial[2]), plus(back_2[1], partial[-2])))
     back_4 = ring((plus(back_3[0], partial[1]), plus(back_3[1], partial[-1])))
-    weight_grad = back_4[0].astype(f32) + back_4[1].astype(f32) + partial[0].astype(f32)
+    (weight_grad,) = call(
+        finish_kernel, [((rows, width), f32)], [VMEM] * 3, size=10 * rows * width
+    )(back_4[0], back_4[1], partial[0])
 
     product = jnp.dot(hidden_other, w_half, preferred_element_type=f32).astype(bf16)
     product_got = partner(product)
@@ -544,6 +567,9 @@
         flops=4 * KW * width,
         size=12 * KW * width,
     )(total, total_got, tap_rows, gain)
+    (passed_gradient,) = call(
+        relay_kernel, [(passed_gradient.shape, bf16)], [VMEM], size=4 * frames * width
+    )(passed_gradient)
     return (
         passed_activation,
         passed_gradient,

time: 120 us -> 121 us (level)
  the two profiles are of different devices: /device:TPU:1 before, /device:TPU:2 now
where the time goes in v3:
time: 121 us; the launch traced here: 120 us
  starting transfers between devices  44.8 us (37%)
  waiting for transfers between devices  41 us (34%)
  Pallas kernels  26.2 us (22%)
  local copies, waits for them, and re-layouts  4.68 us (4%)
  other arithmetic  1.42 us (1%)
    ppermute x6, waiting for transfers between devices, ring(): lax.ppermute(pair_of[1], 'z', down)  18.4 us
    ppermute x6, starting transfers between devices, ring(): lax.ppermute(pair_of[1], 'z', down)  16.4 us
    ppermute x6, waiting for transfers between devices, partner(): return lax.ppermute(array, 'x', [(0, 1), (1, 0)])  9.93 us
    ppermute x3, starting transfers between devices, per_device(): arrived = lax.ppermute(total, 'z', [(i, i ^ step) for i in range(depth)])  8.56 us
    pallas_call x1, Pallas kernels, per_device(): call(functools.partial(conv_kernel, factor), [*[((rows, width), bf16)] *...  7.56 us
    ppermute x6, starting transfers between devices, ring(): lax.ppermute(pair_of[0], 'z', up)  6.44 us
    pallas_call x1, Pallas kernels, per_device(): call(functools.partial(back_kernel, factor, tuple(places)), [((frames, ha...  5.85 us
    unnamed x47, local copies, waits for them, and re-layouts  4.68 us
  transfers between devices with their start and end apart: 27, of which 11 were waited for; matrix products, arithmetic and copies ran while one was open for 2% of the time, Pallas kernels for 21%

profile of v3, /device:TPU:2, one launch (start us, length us, event | category | flops | bytes accessed | tf_op | source)
XLA Modules:
  0.0 120.1 jit_solution(17899503292986379793)
XLA Ops:
  0.6 5.9 %collective-permute-start.6 = (bf16[96,1536]{1,0:T(8,128)(2,1)}, bf16[96,1536]{1,0:T(8,128)(2,1)S(1)}, u32[]{:S(2)}, u32[]{:S(2)}) collective-permute-start(bf16[96,1536]{1,0:T(8,128)(2,1)} %bitcast.25), channel_id=1, source_target_pairs={{2,0},{4,2},{6,4},{8,6},{10,8},{12,10},{14,12},{0,14},{3,1},{5,3},... | collective-permute-start | bytes 884744 | tf_op jit(solution)/shard_map/ppermute | solution.py:422
  6.6 6.6 %collective-permute-done.6.refs_2_ = bf16[96,1536]{1,0:T(8,128)(2,1)S(1)} collective-permute-done((bf16[96,1536]{1,0:T(8,128)(2,1)}, bf16[96,1536]{1,0:T(8,128)(2,1)S(1)}, u32[]{:S(2)}, u32[]{:S(2)}) %collective-permute-start.6) | collective-permute-done | bytes 294944 | tf_op jit(solution)/shard_map/ppermute | solution.py:422
  13.1 3.6 %collective-permute-start.8 = (bf16[96,1536]{1,0:T(8,128)(2,1)S(1)}, bf16[96,1536]{1,0:T(8,128)(2,1)S(1)}, u32[]{:S(2)}, u32[]{:S(2)}) collective-permute-start(bf16[96,1536]{1,0:T(8,128)(2,1)S(1)} %collective-permute-done.6.refs_2_), channel_id=1, source_target_pairs={{2,0},{4,2},{6,4},{8,6},{10,8},{12,10},{14,12},{0,14},{3,1},{5,3},... | collective-permute-start | bytes 884744 | tf_op jit(solution)/shard_map/ppermute | solution.py:422
  17.3 4.9 %collective-permute-done.8.refs_4_ = bf16[96,1536]{1,0:T(8,128)(2,1)S(1)} collective-permute-done((bf16[96,1536]{1,0:T(8,128)(2,1)S(1)}, bf16[96,1536]{1,0:T(8,128)(2,1)S(1)}, u32[]{:S(2)}, u32[]{:S(2)}) %collective-permute-start.8) | collective-permute-done | bytes 294944 | tf_op jit(solution)/shard_map/ppermute | solution.py:422
  22.1 3.7 %collective-permute-start.10 = (bf16[96,1536]{1,0:T(8,128)(2,1)S(1)}, bf16[96,1536]{1,0:T(8,128)(2,1)S(1)}, u32[]{:S(2)}, u32[]{:S(2)}) collective-permute-start(bf16[96,1536]{1,0:T(8,128)(2,1)S(1)} %collective-permute-done.8.refs_4_), channel_id=1, source_target_pairs={{2,0},{4,2},{6,4},{8,6},{10,8},{12,10},{14,12},{0,14},{3,1},{5,3},... | collective-permute-start | bytes 884744 | tf_op jit(solution)/shard_map/ppermute | solution.py:422
  27.9 2.1 %collective-permute-start.1 = (bf16[80,768]{1,0:T(8,128)(2,1)}, bf16[80,768]{1,0:T(8,128)(2,1)S(1)}, u32[]{:S(2)}, u32[]{:S(2)}) collective-permute-start(bf16[80,768]{1,0:T(8,128)(2,1)} %get-tuple-element.43), channel_id=1, source_target_pairs={{1,2},{2,1},{3,4},{4,3},{5,6},{6,5},{7,8},{8,7},{9,10},{10,9},{11,... | collective-permute-start | bytes 368648 | tf_op jit(solution)/shard_map/ppermute | solution.py:442
  29.9 3.5 %shard_map.119 = (bf16[128,768]{1,0:T(8,128)(2,1)}, bf16[128,768]{1,0:T(8,128)(2,1)}, bf16[128,768]{1,0:T(8,128)(2,1)}, bf16[128,768]{1,0:T(8,128)(2,1)}, f32[32,768]{1,0:T(8,128)}) custom-call(s32[1,2]{1,0:T(1,128)} %plan.1, s32[32]{0:T(128)} %lengths.1, bf16[128,1536]{1,0:T(8,128)(2,1)} %bitcast.16, bf16[128,1536]{1,0:T(8,128)(2,1)} %bitcast.29, ...), custom_call_target="tpu_custom_call" | custom-call | flops 4718592 | bytes 1966080 | tf_op jit(solution)/shard_map/pallas_call | solution.py:450
  33.5 2.5 %collective-permute-done.1.near = bf16[80,768]{1,0:T(8,128)(2,1)S(1)} collective-permute-done((bf16[80,768]{1,0:T(8,128)(2,1)}, bf16[80,768]{1,0:T(8,128)(2,1)S(1)}, u32[]{:S(2)}, u32[]{:S(2)}) %collective-permute-start.1) | collective-permute-done | bytes 122912 | tf_op jit(solution)/shard_map/ppermute | solution.py:442
  36.0 2.9 %collective-permute-start.2 = (bf16[80,768]{1,0:T(8,128)(2,1)}, bf16[80,768]{1,0:T(8,128)(2,1)S(1)}, u32[]{:S(2)}, u32[]{:S(2)}) collective-permute-start(bf16[80,768]{1,0:T(8,128)(2,1)} %get-tuple-element.44), channel_id=1, source_target_pairs={{1,3},{2,0},{3,5},{4,2},{5,7},{6,4},{7,9},{8,6},{9,11},{10,8},{11,... | collective-permute-start | bytes 368648 | tf_op jit(solution)/shard_map/ppermute | solution.py:444
  38.9 2.7 %collective-permute-done.2.far = bf16[80,768]{1,0:T(8,128)(2,1)S(1)} collective-permute-done((bf16[80,768]{1,0:T(8,128)(2,1)}, bf16[80,768]{1,0:T(8,128)(2,1)S(1)}, u32[]{:S(2)}, u32[]{:S(2)}) %collective-permute-start.2) | collective-permute-done | bytes 122912 | tf_op jit(solution)/shard_map/ppermute | solution.py:444
  42.5 7.6 %shard_map.122 = (bf16[96,1536]{1,0:T(8,128)(2,1)}, bf16[96,1536]{1,0:T(8,128)(2,1)}, bf16[96,1536]{1,0:T(8,128)(2,1)}, bf16[96,1536]{1,0:T(8,128)(2,1)}, bf16[9...) custom-call(bf16[128,768]{1,0:T(8,128)(2,1)} %get-tuple-element.46.o, ...), custom_call_target="tpu_custom_call" | custom-call | flops 24379392 | bytes 3145728 | tf_op jit(solution)/shard_map/pallas_call | solution.py:471
  50.1 2.4 %collective-permute-start.16 = (bf16[96,1536]{1,0:T(8,128)(2,1)}, bf16[96,1536]{1,0:T(8,128)(2,1)S(1)}, u32[]{:S(2)}, u32[]{:S(2)}) collective-permute-start(bf16[96,1536]{1,0:T(8,128)(2,1)} %get-tuple-element.64), channel_id=1, source_target_pairs={{0,2},{2,4},{4,6},{6,8},{8,10},{10,12},{12,14},{14,0},{1,3},{3,5},... | collective-permute-start | bytes 884744 | tf_op jit(solution)/shard_map/ppermute | solution.py:422
  52.5 5.8 %collective-permute-done.got = bf16[128,768]{1,0:T(8,128)(2,1)S(1)} collective-permute-done((bf16[128,768]{1,0:T(8,128)(2,1)}, bf16[128,768]{1,0:T(8,128)(2,1)S(1)}, u32[]{:S(2)}, u32[]{:S(2)}) %collective-permute-start) | collective-permute-done | bytes 196640 | tf_op jit(solution)/shard_map/ppermute | solution.py:36
  59.0 3.9 %shard_map.121 = (bf16[128,768]{1,0:T(8,128)(2,1)}, bf16[128,768]{1,0:T(8,128)(2,1)}) custom-call(bf16[128,768]{1,0:T(8,128)(2,1)} %get-tuple-element.40.own, bf16[128,768]{1,0:T(8,128)(2,1)} %copy-done.22, f32[32,768]{1,0:T(8,128)} %get-tuple-element.42.taps, bf16[80,768]{1,0:T(8,128)(2,1)} %copy-done.12, bf16[80,768]{1,0:T(8,128)(2,1)} %copy-done.13), custom_call_target="tpu_custom_call" | custom-call | flops 12189696 | bytes 1572864 | tf_op jit(solution)/shard_map/pallas_call | solution.py:490
  68.0 3.8 %collective-permute-done.11.refs_7_ = bf16[96,1536]{1,0:T(8,128)(2,1)S(1)} collective-permute-done((bf16[96,1536]{1,0:T(8,128)(2,1)S(1)}, bf16[96,1536]{1,0:T(8,128)(2,1)S(1)}, u32[]{:S(2)}, u32[]{:S(2)}) %collective-permute-start.11) | collective-permute-done | bytes 294944 | tf_op jit(solution)/shard_map/ppermute | solution.py:504
  74.2 5.8 %shard_map.123 = (bf16[128,768]{1,0:T(8,128)(2,1)S(1)}, bf16[128,768]{1,0:T(8,128)(2,1)S(1)}, f32[32,768]{1,0:T(8,128)S(1)}, bf16[768,1536]{1,0:T(8,128)(2,1)S(1)}) custom-call(s32[1,2]{1,0:T(1,128)S(1)} %copy-done.9, s32[32]{0:T(128)S(1)} %copy-done.10, bf16[288,1536]{1,0:T(8,128)(2,1)S(1)} %copy-done.3, bf16[608,768]{1,0:T(8,128)(2,1)S(1)} %copy-done.2, ...), custom_call_target="tpu_custom_call" | custom-call | flops 24379392 | bytes 2359296 | tf_op jit(solution)/shard_map/pallas_call | solution.py:514
  80.3 2.1 %collective-permute-start.20 = (bf16[96,1536]{1,0:T(8,128)(2,1)S(1)}, bf16[96,1536]{1,0:T(8,128)(2,1)S(1)}, u32[]{:S(2)}, u32[]{:S(2)}) collective-permute-start(bf16[96,1536]{1,0:T(8,128)(2,1)S(1)} %add_convert_fusion.2), channel_id=1, source_target_pairs={{2,0},{4,2},{6,4},{8,6},{10,8},{12,10},{14,12},{0,14},{3,1},{5,3},... | collective-permute-start | bytes 884744 | tf_op jit(solution)/shard_map/ppermute | solution.py:422
  87.2 3.3 %collective-permute-done.24 = bf16[32,768]{1,0:T(8,128)(2,1)S(1)} collective-permute-done((bf16[32,768]{1,0:T(8,128)(2,1)S(1)}, bf16[32,768]{1,0:T(8,128)(2,1)S(1)}, u32[]{:S(2)}, u32[]{:S(2)}) %collective-permute-start.24) | collective-permute-done | bytes 49184 | tf_op jit(solution)/shard_map/ppermute | solution.py:535
  90.5 6.4 %collective-permute-start.25 = (bf16[32,768]{1,0:T(8,128)(2,1)S(1)}, bf16[32,768]{1,0:T(8,128)(2,1)S(1)}, u32[]{:S(2)}, u32[]{:S(2)}) collective-permute-start(bf16[32,768]{1,0:T(8,128)(2,1)S(1)} %add_convert_fusion.6), channel_id=1, source_target_pairs={{0,8},{2,10},{4,12},{6,14},{8,0},{10,2},{12,4},{14,6},{1,9},{3,11}... | collective-permute-start | bytes 147464 | tf_op jit(solution)/shard_map/ppermute | solution.py:535
  99.5 2.1 %collective-permute-start.18 = (bf16[96,1536]{1,0:T(8,128)(2,1)S(1)}, bf16[96,1536]{1,0:T(8,128)(2,1)S(1)}, u32[]{:S(2)}, u32[]{:S(2)}) collective-permute-start(bf16[96,1536]{1,0:T(8,128)(2,1)S(1)} %add_convert_fusion.3), channel_id=1, source_target_pairs={{0,2},{2,4},{4,6},{6,8},{8,10},{10,12},{12,14},{14,0},{1,3},{3,5},... | collective-permute-start | bytes 884744 | tf_op jit(solution)/shard_map/ppermute | solution.py:422
  102.1 2.5 %collective-permute-start.13 = (bf16[1,128,1536]{2,1,0:T(8,128)(2,1)S(1)}, bf16[1,128,1536]{2,1,0:T(8,128)(2,1)S(1)}, u32[]{:S(2)}, u32[]{:S(2)}) collective-permute-start(bf16[1,128,1536]{2,1,0:T(8,128)(2,1)S(1)} %fusion.2), channel_id=1, source_target_pairs={{0,16},{16,32},{32,48},{48,64},{64,80},{80,96},{96,112},{112,128},... | collective-permute-start | bytes 1179656 | tf_op jit(solution)/shard_map/ppermute | solution.py:42
  104.6 4.5 %collective-permute-done.21 = bf16[96,1536]{1,0:T(8,128)(2,1)S(1)} collective-permute-done((bf16[96,1536]{1,0:T(8,128)(2,1)S(1)}, bf16[96,1536]{1,0:T(8,128)(2,1)S(1)}, u32[]{:S(2)}, u32[]{:S(2)}) %collective-permute-start.21) | collective-permute-done | bytes 294944 | tf_op jit(solution)/shard_map/ppermute | solution.py:422
  110.4 4.1 %collective-permute-done.26.got = bf16[32,768]{1,0:T(8,128)(2,1)S(1)} collective-permute-done((bf16[32,768]{1,0:T(8,128)(2,1)S(1)}, bf16[32,768]{1,0:T(8,128)(2,1)S(1)}, u32[]{:S(2)}, u32[]{:S(2)}) %collective-permute-start.26) | collective-permute-done | bytes 49184 | tf_op jit(solution)/shard_map/ppermute | solution.py:36
  116.1 2.4 %collective-permute-done.22.second = bf16[96,1536]{1,0:T(8,128)(2,1)S(1)} collective-permute-done((bf16[96,1536]{1,0:T(8,128)(2,1)S(1)}, bf16[96,1536]{1,0:T(8,128)(2,1)S(1)}, u32[]{:S(2)}, u32[]{:S(2)}) %collective-permute-start.22) | collective-permute-done | bytes 294944 | tf_op jit(solution)/shard_map/ppermute | solution.py:422
  (97 shorter events, 24.1 us)
Async XLA Ops:
  0.6 12.5 %collective-permute-start.6 = (bf16[96,1536]{1,0:T(8,128)(2,1)}, bf16[96,1536]{1,0:T(8,128)(2,1)S(1)}, u32[]{:S(2)}, u32[]{:S(2)}) collective-permute-start(bf16[96,1536]{1,0:T(8,128)(2,1)} %bitcast.25), channel_id=1, source_target_pairs={{2,0},{4,2},{6,4},{8,6},{10,8},{12,10},{14,12},{0,14},{3,1},{5,3},... | collective-permute-start | bytes 884744 | tf_op jit(solution)/shard_map/ppermute | solution.py:422
  6.6 10.2 %collective-permute-start.5 = (bf16[96,1536]{1,0:T(8,128)(2,1)}, bf16[96,1536]{1,0:T(8,128)(2,1)S(1)}, u32[]{:S(2)}, u32[]{:S(2)}) collective-permute-start(bf16[96,1536]{1,0:T(8,128)(2,1)} %bitcast.26), channel_id=1, source_target_pairs={{0,2},{2,4},{4,6},{6,8},{8,10},{10,12},{12,14},{14,0},{1,3},{3,5},... | collective-permute-start | bytes 884744 | tf_op jit(solution)/shard_map/ppermute | solution.py:422
  13.1 9.0 %collective-permute-start.8 = (bf16[96,1536]{1,0:T(8,128)(2,1)S(1)}, bf16[96,1536]{1,0:T(8,128)(2,1)S(1)}, u32[]{:S(2)}, u32[]{:S(2)}) collective-permute-start(bf16[96,1536]{1,0:T(8,128)(2,1)S(1)} %collective-permute-done.6.refs_2_), channel_id=1, source_target_pairs={{2,0},{4,2},{6,4},{8,6},{10,8},{12,10},{14,12},{0,14},{3,1},{5,3},... | collective-permute-start | bytes 884744 | tf_op jit(solution)/shard_map/ppermute | solution.py:422
  16.7 9.1 %collective-permute-start.7 = (bf16[96,1536]{1,0:T(8,128)(2,1)S(1)}, bf16[96,1536]{1,0:T(8,128)(2,1)S(1)}, u32[]{:S(2)}, u32[]{:S(2)}) collective-permute-start(bf16[96,1536]{1,0:T(8,128)(2,1)S(1)} %collective-permute-done.5.refs_1_), channel_id=1, source_target_pairs={{0,2},{2,4},{4,6},{6,8},{8,10},{10,12},{12,14},{14,0},{1,3},{3,5},... | collective-permute-start | bytes 884744 | tf_op jit(solution)/shard_map/ppermute | solution.py:422
  16.7 24.9 %collective-permute-start.4 = (bf16[128,1536]{1,0:T(8,128)(2,1)}, bf16[128,1536]{1,0:T(8,128)(2,1)S(1)}, u32[]{:S(2)}, u32[]{:S(2)}) collective-permute-start(bf16[128,1536]{1,0:T(8,128)(2,1)} %bitcast.18), channel_id=1, source_target_pairs={{0,1},{1,0},{2,3},{3,2},{4,5},{5,4},{6,7},{7,6},{8,9},{9,8},{10,11... | collective-permute-start | bytes 1179656 | tf_op jit(solution)/shard_map/ppermute | solution.py:36
  22.1 27.9 %collective-permute-start.10 = (bf16[96,1536]{1,0:T(8,128)(2,1)S(1)}, bf16[96,1536]{1,0:T(8,128)(2,1)S(1)}, u32[]{:S(2)}, u32[]{:S(2)}) collective-permute-start(bf16[96,1536]{1,0:T(8,128)(2,1)S(1)} %collective-permute-done.8.refs_4_), channel_id=1, source_target_pairs={{2,0},{4,2},{6,4},{8,6},{10,8},{12,10},{14,12},{0,14},{3,1},{5,3},... | collective-permute-start | bytes 884744 | tf_op jit(solution)/shard_map/ppermute | solution.py:422
  25.8 24.2 %collective-permute-start.9 = (bf16[96,1536]{1,0:T(8,128)(2,1)S(1)}, bf16[96,1536]{1,0:T(8,128)(2,1)S(1)}, u32[]{:S(2)}, u32[]{:S(2)}) collective-permute-start(bf16[96,1536]{1,0:T(8,128)(2,1)S(1)} %collective-permute-done.7.refs_3_), channel_id=1, source_target_pairs={{0,2},{2,4},{4,6},{6,8},{8,10},{10,12},{12,14},{14,0},{1,3},{3,5},... | collective-permute-start | bytes 884744 | tf_op jit(solution)/shard_map/ppermute | solution.py:422
  27.9 8.1 %collective-permute-start.1 = (bf16[80,768]{1,0:T(8,128)(2,1)}, bf16[80,768]{1,0:T(8,128)(2,1)S(1)}, u32[]{:S(2)}, u32[]{:S(2)}) collective-permute-start(bf16[80,768]{1,0:T(8,128)(2,1)} %get-tuple-element.43), channel_id=1, source_target_pairs={{1,2},{2,1},{3,4},{4,3},{5,6},{6,5},{7,8},{8,7},{9,10},{10,9},{11,... | collective-permute-start | bytes 368648 | tf_op jit(solution)/shard_map/ppermute | solution.py:442
  33.4 8.2 %collective-permute-start.3 = (bf16[128,768]{1,0:T(8,128)(2,1)}, bf16[128,768]{1,0:T(8,128)(2,1)S(1)}, u32[]{:S(2)}, u32[]{:S(2)}) collective-permute-start(bf16[128,768]{1,0:T(8,128)(2,1)} %get-tuple-element.47), channel_id=1, source_target_pairs={{0,1},{1,0},{2,3},{3,2},{4,5},{5,4},{6,7},{7,6},{8,9},{9,8},{10,11... | collective-permute-start | bytes 589832 | tf_op jit(solution)/shard_map/ppermute | solution.py:36
  50.1 14.9 %collective-permute-start.16 = (bf16[96,1536]{1,0:T(8,128)(2,1)}, bf16[96,1536]{1,0:T(8,128)(2,1)S(1)}, u32[]{:S(2)}, u32[]{:S(2)}) collective-permute-start(bf16[96,1536]{1,0:T(8,128)(2,1)} %get-tuple-element.64), channel_id=1, source_target_pairs={{0,2},{2,4},{4,6},{6,8},{8,10},{10,12},{12,14},{14,0},{1,3},{3,5},... | collective-permute-start | bytes 884744 | tf_op jit(solution)/shard_map/ppermute | solution.py:422
  52.5 5.9 %collective-permute-start = (bf16[128,768]{1,0:T(8,128)(2,1)}, bf16[128,768]{1,0:T(8,128)(2,1)S(1)}, u32[]{:S(2)}, u32[]{:S(2)}) collective-permute-start(bf16[128,768]{1,0:T(8,128)(2,1)} %get-tuple-element.41), channel_id=1, source_target_pairs={{0,1},{1,0},{2,3},{3,2},{4,5},{5,4},{6,7},{7,6},{8,9},{9,8},{10,11... | collective-permute-start | bytes 589832 | tf_op jit(solution)/shard_map/ppermute | solution.py:36
  62.9 17.3 %collective-permute-start.19 = (bf16[96,1536]{1,0:T(8,128)(2,1)}, bf16[96,1536]{1,0:T(8,128)(2,1)S(1)}, u32[]{:S(2)}, u32[]{:S(2)}) collective-permute-start(bf16[96,1536]{1,0:T(8,128)(2,1)} %get-tuple-element.67), channel_id=1, source_target_pairs={{2,0},{4,2},{6,4},{8,6},{10,8},{12,10},{14,12},{0,14},{3,1},{5,3},... | collective-permute-start | bytes 884744 | tf_op jit(solution)/shard_map/ppermute | solution.py:505
  63.8 8.0 %collective-permute-start.11 = (bf16[96,1536]{1,0:T(8,128)(2,1)S(1)}, bf16[96,1536]{1,0:T(8,128)(2,1)S(1)}, u32[]{:S(2)}, u32[]{:S(2)}) collective-permute-start(bf16[96,1536]{1,0:T(8,128)(2,1)S(1)} %collective-permute-done.9.refs_5_), channel_id=1, source_target_pairs={{0,2},{2,4},{4,6},{6,8},{8,10},{10,12},{12,14},{14,0},{1,3},{3,5},... | collective-permute-start | bytes 884744 | tf_op jit(solution)/shard_map/ppermute | solution.py:504
  66.0 33.4 %collective-permute-start.17 = (bf16[96,1536]{1,0:T(8,128)(2,1)S(1)}, bf16[96,1536]{1,0:T(8,128)(2,1)S(1)}, u32[]{:S(2)}, u32[]{:S(2)}) collective-permute-start(bf16[96,1536]{1,0:T(8,128)(2,1)S(1)} %add_convert_fusion.4), channel_id=1, source_target_pairs={{0,2},{2,4},{4,6},{6,8},{8,10},{10,12},{12,14},{14,0},{1,3},{3,5},... | collective-permute-start | bytes 884744 | tf_op jit(solution)/shard_map/ppermute | solution.py:422
  80.3 18.9 %collective-permute-start.20 = (bf16[96,1536]{1,0:T(8,128)(2,1)S(1)}, bf16[96,1536]{1,0:T(8,128)(2,1)S(1)}, u32[]{:S(2)}, u32[]{:S(2)}) collective-permute-start(bf16[96,1536]{1,0:T(8,128)(2,1)S(1)} %add_convert_fusion.2), channel_id=1, source_target_pairs={{2,0},{4,2},{6,4},{8,6},{10,8},{12,10},{14,12},{0,14},{3,1},{5,3},... | collective-permute-start | bytes 884744 | tf_op jit(solution)/shard_map/ppermute | solution.py:422
  82.4 14.6 %collective-permute-start.14 = (bf16[128,768]{1,0:T(8,128)(2,1)S(1)}, bf16[128,768]{1,0:T(8,128)(2,1)S(1)}, u32[]{:S(2)}, u32[]{:S(2)}) collective-permute-start(bf16[128,768]{1,0:T(8,128)(2,1)S(1)} %get-tuple-element.63), channel_id=1, source_target_pairs={{0,1},{1,0},{2,3},{3,2},{4,5},{5,4},{6,7},{7,6},{8,9},{9,8},{10,11... | collective-permute-start | bytes 589832 | tf_op jit(solution)/shard_map/ppermute | solution.py:36
  84.3 6.2 %collective-permute-start.24 = (bf16[32,768]{1,0:T(8,128)(2,1)S(1)}, bf16[32,768]{1,0:T(8,128)(2,1)S(1)}, u32[]{:S(2)}, u32[]{:S(2)}) collective-permute-start(bf16[32,768]{1,0:T(8,128)(2,1)S(1)} %add_convert_fusion.7), channel_id=1, source_target_pairs={{0,4},{2,6},{4,0},{6,2},{8,12},{10,14},{12,8},{14,10},{1,5},{3,7},... | collective-permute-start | bytes 147464 | tf_op jit(solution)/shard_map/ppermute | solution.py:535
  86.9 14.7 %collective-permute-start.12 = (bf16[128,1536]{1,0:T(8,128)(2,1)S(1)}, bf16[128,1536]{1,0:T(8,128)(2,1)S(1)}, u32[]{:S(2)}, u32[]{:S(2)}) collective-permute-start(bf16[128,1536]{1,0:T(8,128)(2,1)S(1)} %convolution_convert_fusion), channel_id=1, source_target_pairs={{0,1},{1,0},{2,3},{3,2},{4,5},{5,4},{6,7},{7,6},{8,9},{9,8},{10,11... | collective-permute-start | bytes 1179656 | tf_op jit(solution)/shard_map/ppermute | solution.py:36
  90.5 19.7 %collective-permute-start.25 = (bf16[32,768]{1,0:T(8,128)(2,1)S(1)}, bf16[32,768]{1,0:T(8,128)(2,1)S(1)}, u32[]{:S(2)}, u32[]{:S(2)}) collective-permute-start(bf16[32,768]{1,0:T(8,128)(2,1)S(1)} %add_convert_fusion.6), channel_id=1, source_target_pairs={{0,8},{2,10},{4,12},{6,14},{8,0},{10,2},{12,4},{14,6},{1,9},{3,11}... | collective-permute-start | bytes 147464 | tf_op jit(solution)/shard_map/ppermute | solution.py:535
  97.9 17.3 %collective-permute-start.15 = (bf16[1,128,1536]{2,1,0:T(8,128)(2,1)S(1)}, bf16[1,128,1536]{2,1,0:T(8,128)(2,1)S(1)}, u32[]{:S(2)}, u32[]{:S(2)}) collective-permute-start(bf16[1,128,1536]{2,1,0:T(8,128)(2,1)S(1)} %bitcast.24), channel_id=1, source_target_pairs={{16,0},{32,16},{48,32},{64,48},{80,64},{96,80},{112,96},{128,112},... | collective-permute-start | bytes 1179656 | tf_op jit(solution)/shard_map/ppermute | solution.py:42
  99.3 9.8 %collective-permute-start.21 = (bf16[96,1536]{1,0:T(8,128)(2,1)S(1)}, bf16[96,1536]{1,0:T(8,128)(2,1)S(1)}, u32[]{:S(2)}, u32[]{:S(2)}) collective-permute-start(bf16[96,1536]{1,0:T(8,128)(2,1)S(1)} %add_convert_fusion.1), channel_id=1, source_target_pairs={{2,0},{4,2},{6,4},{8,6},{10,8},{12,10},{14,12},{0,14},{3,1},{5,3},... | collective-permute-start | bytes 884744 | tf_op jit(solution)/shard_map/ppermute | solution.py:422
  99.5 16.5 %collective-permute-start.18 = (bf16[96,1536]{1,0:T(8,128)(2,1)S(1)}, bf16[96,1536]{1,0:T(8,128)(2,1)S(1)}, u32[]{:S(2)}, u32[]{:S(2)}) collective-permute-start(bf16[96,1536]{1,0:T(8,128)(2,1)S(1)} %add_convert_fusion.3), channel_id=1, source_target_pairs={{0,2},{2,4},{4,6},{6,8},{8,10},{10,12},{12,14},{14,0},{1,3},{3,5},... | collective-permute-start | bytes 884744 | tf_op jit(solution)/shard_map/ppermute | solution.py:422
  102.1 13.9 %collective-permute-start.13 = (bf16[1,128,1536]{2,1,0:T(8,128)(2,1)S(1)}, bf16[1,128,1536]{2,1,0:T(8,128)(2,1)S(1)}, u32[]{:S(2)}, u32[]{:S(2)}) collective-permute-start(bf16[1,128,1536]{2,1,0:T(8,128)(2,1)S(1)} %fusion.2), channel_id=1, source_target_pairs={{0,16},{16,32},{32,48},{48,64},{64,80},{80,96},{96,112},{112,128},... | collective-permute-start | bytes 1179656 | tf_op jit(solution)/shard_map/ppermute | solution.py:42
  109.2 9.3 %collective-permute-start.22 = (bf16[96,1536]{1,0:T(8,128)(2,1)S(1)}, bf16[96,1536]{1,0:T(8,128)(2,1)S(1)}, u32[]{:S(2)}, u32[]{:S(2)}) collective-permute-start(bf16[96,1536]{1,0:T(8,128)(2,1)S(1)} %add_convert_fusion), channel_id=1, source_target_pairs={{2,0},{4,2},{6,4},{8,6},{10,8},{12,10},{14,12},{0,14},{3,1},{5,3},... | collective-permute-start | bytes 884744 | tf_op jit(solution)/shard_map/ppermute | solution.py:422
  (26 other events, 370.4 us)

commit v4 on v3

--- a/solution.py
+++ b/solution.py
@@ -213,7 +213,7 @@
 
         return carry
 
-    lax.fori_loop(0, own.shape[1] // LANES, body, 0)
+    lax.fori_loop(0, own.shape[1] // LANES, body, 0, unroll=2)
 
 
 def conv_kernel(
@@ -264,13 +264,13 @@
             hidden_saved[pl.ds(half * frames, frames), lanes] = inner.astype(jnp.bfloat16)
         return carry
 
-    lax.fori_loop(0, chunks, body, 0)
+    lax.fori_loop(0, chunks, body, 0, unroll=2)
     copy.wait()
     depth = len(blocks)
     here = lax.axis_index("z")
 
     def outer(index, carry):
-        lanes = pl.ds(pl.multiple_of(index * 2 * LANES, 2 * LANES), 2 * LANES)
+        lanes = pl.ds(pl.multiple_of(index * 6 * LANES, 6 * LANES), 6 * LANES)
         value = lax.dot_general(
             hidden_saved[...],
             grad_window[HALO : HALO + 2 * frames, lanes],
@@ -284,7 +284,7 @@
             out[:, lanes] = product[place]
         return carry
 
-    lax.fori_loop(0, grad_window.shape[1] // (2 * LANES), outer, 0)
+    lax.fori_loop(0, grad_window.shape[1] // (6 * LANES), outer, 0)
 
 
 def back_kernel(
@@ -360,7 +360,7 @@
         kernel_grad[KW : KW + 1, lanes] = jnp.zeros((1, LANES), jnp.float32)
         return carry
 
-    lax.fori_loop(0, chunks, body, 0)
+    lax.fori_loop(0, chunks, body, 0, unroll=2)
 
 
 def leave_kernel(block, own, got, saved, grad, gain, out):
@@ -479,7 +479,7 @@
         [
             pltpu.VMEM((pair, half), bf16),
             pltpu.VMEM((1, pair + 4 * HALO + 8, LANES), f32),
-            pltpu.VMEM((depth, rows, 2 * LANES), bf16),
+            pltpu.VMEM((depth, rows, 6 * LANES), bf16),
             pltpu.SemaphoreType.DMA(()),
         ],
         limit=None,

time: 121 us -> 120 us (level)
  no operation moved by 1% of the time
where the time goes in v4:
time: 120 us; the launch traced here: 119 us
  starting transfers between devices  44.8 us (37%)
  waiting for transfers between devices  41 us (34%)
  Pallas kernels  25.4 us (21%)
  local copies, waits for them, and re-layouts  4.68 us (4%)
  other arithmetic  1.42 us (1%)
    ppermute x6, waiting for transfers between devices, ring(): lax.ppermute(pair_of[1], 'z', down)  18.4 us
    ppermute x6, starting transfers between devices, ring(): lax.ppermute(pair_of[1], 'z', down)  16.4 us
    ppermute x6, waiting for transfers between devices, partner(): return lax.ppermute(array, 'x', [(0, 1), (1, 0)])  9.93 us
    ppermute x3, starting transfers between devices, per_device(): arrived = lax.ppermute(total, 'z', [(i, i ^ step) for i in range(depth)])  8.56 us
    pallas_call x1, Pallas kernels, per_device(): call(functools.partial(conv_kernel, factor), [*[((rows, width), bf16)] *...  6.71 us
    ppermute x6, starting transfers between devices, ring(): lax.ppermute(pair_of[0], 'z', up)  6.42 us
    pallas_call x1, Pallas kernels, per_device(): call(functools.partial(back_kernel, factor, tuple(places)), [((frames, ha...  5.87 us
    unnamed x47, local copies, waits for them, and re-layouts  4.68 us
  transfers between devices with their start and end apart: 27, of which 11 were waited for; matrix products, arithmetic and copies ran while one was open for 2% of the time, Pallas kernels for 21%

profile of v4, /device:TPU:2, one launch (start us, length us, event | category | flops | bytes accessed | tf_op | source)
XLA Modules:
  0.0 119.3 jit_solution(11345669398102976340)
XLA Ops:
  0.6 5.9 %collective-permute-start.6 = (bf16[96,1536]{1,0:T(8,128)(2,1)}, bf16[96,1536]{1,0:T(8,128)(2,1)S(1)}, u32[]{:S(2)}, u32[]{:S(2)}) collective-permute-start(bf16[96,1536]{1,0:T(8,128)(2,1)} %bitcast.25), channel_id=1, source_target_pairs={{2,0},{4,2},{6,4},{8,6},{10,8},{12,10},{14,12},{0,14},{3,1},{5,3},... | collective-permute-start | bytes 884744 | tf_op jit(solution)/shard_map/ppermute | solution.py:422
  6.6 6.6 %collective-permute-done.6.refs_2_ = bf16[96,1536]{1,0:T(8,128)(2,1)S(1)} collective-permute-done((bf16[96,1536]{1,0:T(8,128)(2,1)}, bf16[96,1536]{1,0:T(8,128)(2,1)S(1)}, u32[]{:S(2)}, u32[]{:S(2)}) %collective-permute-start.6) | collective-permute-done | bytes 294944 | tf_op jit(solution)/shard_map/ppermute | solution.py:422
  13.1 3.6 %collective-permute-start.8 = (bf16[96,1536]{1,0:T(8,128)(2,1)S(1)}, bf16[96,1536]{1,0:T(8,128)(2,1)S(1)}, u32[]{:S(2)}, u32[]{:S(2)}) collective-permute-start(bf16[96,1536]{1,0:T(8,128)(2,1)S(1)} %collective-permute-done.6.refs_2_), channel_id=1, source_target_pairs={{2,0},{4,2},{6,4},{8,6},{10,8},{12,10},{14,12},{0,14},{3,1},{5,3},... | collective-permute-start | bytes 884744 | tf_op jit(solution)/shard_map/ppermute | solution.py:422
  17.3 4.9 %collective-permute-done.8.refs_4_ = bf16[96,1536]{1,0:T(8,128)(2,1)S(1)} collective-permute-done((bf16[96,1536]{1,0:T(8,128)(2,1)S(1)}, bf16[96,1536]{1,0:T(8,128)(2,1)S(1)}, u32[]{:S(2)}, u32[]{:S(2)}) %collective-permute-start.8) | collective-permute-done | bytes 294944 | tf_op jit(solution)/shard_map/ppermute | solution.py:422
  22.1 3.7 %collective-permute-start.10 = (bf16[96,1536]{1,0:T(8,128)(2,1)S(1)}, bf16[96,1536]{1,0:T(8,128)(2,1)S(1)}, u32[]{:S(2)}, u32[]{:S(2)}) collective-permute-start(bf16[96,1536]{1,0:T(8,128)(2,1)S(1)} %collective-permute-done.8.refs_4_), channel_id=1, source_target_pairs={{2,0},{4,2},{6,4},{8,6},{10,8},{12,10},{14,12},{0,14},{3,1},{5,3},... | collective-permute-start | bytes 884744 | tf_op jit(solution)/shard_map/ppermute | solution.py:422
  27.9 2.1 %collective-permute-start.1 = (bf16[80,768]{1,0:T(8,128)(2,1)}, bf16[80,768]{1,0:T(8,128)(2,1)S(1)}, u32[]{:S(2)}, u32[]{:S(2)}) collective-permute-start(bf16[80,768]{1,0:T(8,128)(2,1)} %get-tuple-element.43), channel_id=1, source_target_pairs={{1,2},{2,1},{3,4},{4,3},{5,6},{6,5},{7,8},{8,7},{9,10},{10,9},{11,... | collective-permute-start | bytes 368648 | tf_op jit(solution)/shard_map/ppermute | solution.py:442
  29.9 3.5 %shard_map.119 = (bf16[128,768]{1,0:T(8,128)(2,1)}, bf16[128,768]{1,0:T(8,128)(2,1)}, bf16[128,768]{1,0:T(8,128)(2,1)}, bf16[128,768]{1,0:T(8,128)(2,1)}, f32[32,768]{1,0:T(8,128)}) custom-call(s32[1,2]{1,0:T(1,128)} %plan.1, s32[32]{0:T(128)} %lengths.1, bf16[128,1536]{1,0:T(8,128)(2,1)} %bitcast.16, bf16[128,1536]{1,0:T(8,128)(2,1)} %bitcast.29, ...), custom_call_target="tpu_custom_call" | custom-call | flops 4718592 | bytes 1966080 | tf_op jit(solution)/shard_map/pallas_call | solution.py:450
  33.5 2.5 %collective-permute-done.1.near = bf16[80,768]{1,0:T(8,128)(2,1)S(1)} collective-permute-done((bf16[80,768]{1,0:T(8,128)(2,1)}, bf16[80,768]{1,0:T(8,128)(2,1)S(1)}, u32[]{:S(2)}, u32[]{:S(2)}) %collective-permute-start.1) | collective-permute-done | bytes 122912 | tf_op jit(solution)/shard_map/ppermute | solution.py:442
  36.0 2.9 %collective-permute-start.2 = (bf16[80,768]{1,0:T(8,128)(2,1)}, bf16[80,768]{1,0:T(8,128)(2,1)S(1)}, u32[]{:S(2)}, u32[]{:S(2)}) collective-permute-start(bf16[80,768]{1,0:T(8,128)(2,1)} %get-tuple-element.44), channel_id=1, source_target_pairs={{1,3},{2,0},{3,5},{4,2},{5,7},{6,4},{7,9},{8,6},{9,11},{10,8},{11,... | collective-permute-start | bytes 368648 | tf_op jit(solution)/shard_map/ppermute | solution.py:444
  38.9 2.7 %collective-permute-done.2.far = bf16[80,768]{1,0:T(8,128)(2,1)S(1)} collective-permute-done((bf16[80,768]{1,0:T(8,128)(2,1)}, bf16[80,768]{1,0:T(8,128)(2,1)S(1)}, u32[]{:S(2)}, u32[]{:S(2)}) %collective-permute-start.2) | collective-permute-done | bytes 122912 | tf_op jit(solution)/shard_map/ppermute | solution.py:444
  42.5 6.7 %shard_map.122 = (bf16[96,1536]{1,0:T(8,128)(2,1)}, bf16[96,1536]{1,0:T(8,128)(2,1)}, bf16[96,1536]{1,0:T(8,128)(2,1)}, bf16[96,1536]{1,0:T(8,128)(2,1)}, bf16[9...) custom-call(bf16[128,768]{1,0:T(8,128)(2,1)} %get-tuple-element.46.o, ...), custom_call_target="tpu_custom_call" | custom-call | flops 24379392 | bytes 3145728 | tf_op jit(solution)/shard_map/pallas_call | solution.py:471
  49.2 2.4 %collective-permute-start.16 = (bf16[96,1536]{1,0:T(8,128)(2,1)}, bf16[96,1536]{1,0:T(8,128)(2,1)S(1)}, u32[]{:S(2)}, u32[]{:S(2)}) collective-permute-start(bf16[96,1536]{1,0:T(8,128)(2,1)} %get-tuple-element.64), channel_id=1, source_target_pairs={{0,2},{2,4},{4,6},{6,8},{8,10},{10,12},{12,14},{14,0},{1,3},{3,5},... | collective-permute-start | bytes 884744 | tf_op jit(solution)/shard_map/ppermute | solution.py:422
  51.7 5.8 %collective-permute-done.got = bf16[128,768]{1,0:T(8,128)(2,1)S(1)} collective-permute-done((bf16[128,768]{1,0:T(8,128)(2,1)}, bf16[128,768]{1,0:T(8,128)(2,1)S(1)}, u32[]{:S(2)}, u32[]{:S(2)}) %collective-permute-start) | collective-permute-done | bytes 196640 | tf_op jit(solution)/shard_map/ppermute | solution.py:36
  58.2 3.9 %shard_map.121 = (bf16[128,768]{1,0:T(8,128)(2,1)}, bf16[128,768]{1,0:T(8,128)(2,1)}) custom-call(bf16[128,768]{1,0:T(8,128)(2,1)} %get-tuple-element.40.own, bf16[128,768]{1,0:T(8,128)(2,1)} %copy-done.22, f32[32,768]{1,0:T(8,128)} %get-tuple-element.42.taps, bf16[80,768]{1,0:T(8,128)(2,1)} %copy-done.12, bf16[80,768]{1,0:T(8,128)(2,1)} %copy-done.13), custom_call_target="tpu_custom_call" | custom-call | flops 12189696 | bytes 1572864 | tf_op jit(solution)/shard_map/pallas_call | solution.py:490
  67.1 3.9 %collective-permute-done.11.refs_7_ = bf16[96,1536]{1,0:T(8,128)(2,1)S(1)} collective-permute-done((bf16[96,1536]{1,0:T(8,128)(2,1)S(1)}, bf16[96,1536]{1,0:T(8,128)(2,1)S(1)}, u32[]{:S(2)}, u32[]{:S(2)}) %collective-permute-start.11) | collective-permute-done | bytes 294944 | tf_op jit(solution)/shard_map/ppermute | solution.py:504
  73.4 5.9 %shard_map.123 = (bf16[128,768]{1,0:T(8,128)(2,1)S(1)}, bf16[128,768]{1,0:T(8,128)(2,1)S(1)}, f32[32,768]{1,0:T(8,128)S(1)}, bf16[768,1536]{1,0:T(8,128)(2,1)S(1)}) custom-call(s32[1,2]{1,0:T(1,128)S(1)} %copy-done.9, s32[32]{0:T(128)S(1)} %copy-done.10, bf16[288,1536]{1,0:T(8,128)(2,1)S(1)} %copy-done.3, bf16[608,768]{1,0:T(8,128)(2,1)S(1)} %copy-done.2, ...), custom_call_target="tpu_custom_call" | custom-call | flops 24379392 | bytes 2359296 | tf_op jit(solution)/shard_map/pallas_call | solution.py:514
  79.5 2.1 %collective-permute-start.20 = (bf16[96,1536]{1,0:T(8,128)(2,1)S(1)}, bf16[96,1536]{1,0:T(8,128)(2,1)S(1)}, u32[]{:S(2)}, u32[]{:S(2)}) collective-permute-start(bf16[96,1536]{1,0:T(8,128)(2,1)S(1)} %add_convert_fusion.2), channel_id=1, source_target_pairs={{2,0},{4,2},{6,4},{8,6},{10,8},{12,10},{14,12},{0,14},{3,1},{5,3},... | collective-permute-start | bytes 884744 | tf_op jit(solution)/shard_map/ppermute | solution.py:422
  86.4 3.3 %collective-permute-done.24 = bf16[32,768]{1,0:T(8,128)(2,1)S(1)} collective-permute-done((bf16[32,768]{1,0:T(8,128)(2,1)S(1)}, bf16[32,768]{1,0:T(8,128)(2,1)S(1)}, u32[]{:S(2)}, u32[]{:S(2)}) %collective-permute-start.24) | collective-permute-done | bytes 49184 | tf_op jit(solution)/shard_map/ppermute | solution.py:535
  89.7 6.4 %collective-permute-start.25 = (bf16[32,768]{1,0:T(8,128)(2,1)S(1)}, bf16[32,768]{1,0:T(8,128)(2,1)S(1)}, u32[]{:S(2)}, u32[]{:S(2)}) collective-permute-start(bf16[32,768]{1,0:T(8,128)(2,1)S(1)} %add_convert_fusion.6), channel_id=1, source_target_pairs={{0,8},{2,10},{4,12},{6,14},{8,0},{10,2},{12,4},{14,6},{1,9},{3,11}... | collective-permute-start | bytes 147464 | tf_op jit(solution)/shard_map/ppermute | solution.py:535
  98.7 2.1 %collective-permute-start.18 = (bf16[96,1536]{1,0:T(8,128)(2,1)S(1)}, bf16[96,1536]{1,0:T(8,128)(2,1)S(1)}, u32[]{:S(2)}, u32[]{:S(2)}) collective-permute-start(bf16[96,1536]{1,0:T(8,128)(2,1)S(1)} %add_convert_fusion.3), channel_id=1, source_target_pairs={{0,2},{2,4},{4,6},{6,8},{8,10},{10,12},{12,14},{14,0},{1,3},{3,5},... | collective-permute-start | bytes 884744 | tf_op jit(solution)/shard_map/ppermute | solution.py:422
  101.3 2.5 %collective-permute-start.13 = (bf16[1,128,1536]{2,1,0:T(8,128)(2,1)S(1)}, bf16[1,128,1536]{2,1,0:T(8,128)(2,1)S(1)}, u32[]{:S(2)}, u32[]{:S(2)}) collective-permute-start(bf16[1,128,1536]{2,1,0:T(8,128)(2,1)S(1)} %fusion.2), channel_id=1, source_target_pairs={{0,16},{16,32},{32,48},{48,64},{64,80},{80,96},{96,112},{112,128},... | collective-permute-start | bytes 1179656 | tf_op jit(solution)/shard_map/ppermute | solution.py:42
  103.8 4.5 %collective-permute-done.21 = bf16[96,1536]{1,0:T(8,128)(2,1)S(1)} collective-permute-done((bf16[96,1536]{1,0:T(8,128)(2,1)S(1)}, bf16[96,1536]{1,0:T(8,128)(2,1)S(1)}, u32[]{:S(2)}, u32[]{:S(2)}) %collective-permute-start.21) | collective-permute-done | bytes 294944 | tf_op jit(solution)/shard_map/ppermute | solution.py:422
  109.5 4.1 %collective-permute-done.26.got = bf16[32,768]{1,0:T(8,128)(2,1)S(1)} collective-permute-done((bf16[32,768]{1,0:T(8,128)(2,1)S(1)}, bf16[32,768]{1,0:T(8,128)(2,1)S(1)}, u32[]{:S(2)}, u32[]{:S(2)}) %collective-permute-start.26) | collective-permute-done | bytes 49184 | tf_op jit(solution)/shard_map/ppermute | solution.py:36
  115.2 2.4 %collective-permute-done.22.second = bf16[96,1536]{1,0:T(8,128)(2,1)S(1)} collective-permute-done((bf16[96,1536]{1,0:T(8,128)(2,1)S(1)}, bf16[96,1536]{1,0:T(8,128)(2,1)S(1)}, u32[]{:S(2)}, u32[]{:S(2)}) %collective-permute-start.22) | collective-permute-done | bytes 294944 | tf_op jit(solution)/shard_map/ppermute | solution.py:422
  (97 shorter events, 24.1 us)
Async XLA Ops:
  0.6 12.5 %collective-permute-start.6 = (bf16[96,1536]{1,0:T(8,128)(2,1)}, bf16[96,1536]{1,0:T(8,128)(2,1)S(1)}, u32[]{:S(2)}, u32[]{:S(2)}) collective-permute-start(bf16[96,1536]{1,0:T(8,128)(2,1)} %bitcast.25), channel_id=1, source_target_pairs={{2,0},{4,2},{6,4},{8,6},{10,8},{12,10},{14,12},{0,14},{3,1},{5,3},... | collective-permute-start | bytes 884744 | tf_op jit(solution)/shard_map/ppermute | solution.py:422
  6.6 10.2 %collective-permute-start.5 = (bf16[96,1536]{1,0:T(8,128)(2,1)}, bf16[96,1536]{1,0:T(8,128)(2,1)S(1)}, u32[]{:S(2)}, u32[]{:S(2)}) collective-permute-start(bf16[96,1536]{1,0:T(8,128)(2,1)} %bitcast.26), channel_id=1, source_target_pairs={{0,2},{2,4},{4,6},{6,8},{8,10},{10,12},{12,14},{14,0},{1,3},{3,5},... | collective-permute-start | bytes 884744 | tf_op jit(solution)/shard_map/ppermute | solution.py:422
  13.1 9.0 %collective-permute-start.8 = (bf16[96,1536]{1,0:T(8,128)(2,1)S(1)}, bf16[96,1536]{1,0:T(8,128)(2,1)S(1)}, u32[]{:S(2)}, u32[]{:S(2)}) collective-permute-start(bf16[96,1536]{1,0:T(8,128)(2,1)S(1)} %collective-permute-done.6.refs_2_), channel_id=1, source_target_pairs={{2,0},{4,2},{6,4},{8,6},{10,8},{12,10},{14,12},{0,14},{3,1},{5,3},... | collective-permute-start | bytes 884744 | tf_op jit(solution)/shard_map/ppermute | solution.py:422
  16.7 9.1 %collective-permute-start.7 = (bf16[96,1536]{1,0:T(8,128)(2,1)S(1)}, bf16[96,1536]{1,0:T(8,128)(2,1)S(1)}, u32[]{:S(2)}, u32[]{:S(2)}) collective-permute-start(bf16[96,1536]{1,0:T(8,128)(2,1)S(1)} %collective-permute-done.5.refs_1_), channel_id=1, source_target_pairs={{0,2},{2,4},{4,6},{6,8},{8,10},{10,12},{12,14},{14,0},{1,3},{3,5},... | collective-permute-start | bytes 884744 | tf_op jit(solution)/shard_map/ppermute | solution.py:422
  16.7 24.9 %collective-permute-start.4 = (bf16[128,1536]{1,0:T(8,128)(2,1)}, bf16[128,1536]{1,0:T(8,128)(2,1)S(1)}, u32[]{:S(2)}, u32[]{:S(2)}) collective-permute-start(bf16[128,1536]{1,0:T(8,128)(2,1)} %bitcast.18), channel_id=1, source_target_pairs={{0,1},{1,0},{2,3},{3,2},{4,5},{5,4},{6,7},{7,6},{8,9},{9,8},{10,11... | collective-permute-start | bytes 1179656 | tf_op jit(solution)/shard_map/ppermute | solution.py:36
  22.1 27.0 %collective-permute-start.10 = (bf16[96,1536]{1,0:T(8,128)(2,1)S(1)}, bf16[96,1536]{1,0:T(8,128)(2,1)S(1)}, u32[]{:S(2)}, u32[]{:S(2)}) collective-permute-start(bf16[96,1536]{1,0:T(8,128)(2,1)S(1)} %collective-permute-done.8.refs_4_), channel_id=1, source_target_pairs={{2,0},{4,2},{6,4},{8,6},{10,8},{12,10},{14,12},{0,14},{3,1},{5,3},... | collective-permute-start | bytes 884744 | tf_op jit(solution)/shard_map/ppermute | solution.py:422
  25.8 23.4 %collective-permute-start.9 = (bf16[96,1536]{1,0:T(8,128)(2,1)S(1)}, bf16[96,1536]{1,0:T(8,128)(2,1)S(1)}, u32[]{:S(2)}, u32[]{:S(2)}) collective-permute-start(bf16[96,1536]{1,0:T(8,128)(2,1)S(1)} %collective-permute-done.7.refs_3_), channel_id=1, source_target_pairs={{0,2},{2,4},{4,6},{6,8},{8,10},{10,12},{12,14},{14,0},{1,3},{3,5},... | collective-permute-start | bytes 884744 | tf_op jit(solution)/shard_map/ppermute | solution.py:422
  27.9 8.1 %collective-permute-start.1 = (bf16[80,768]{1,0:T(8,128)(2,1)}, bf16[80,768]{1,0:T(8,128)(2,1)S(1)}, u32[]{:S(2)}, u32[]{:S(2)}) collective-permute-start(bf16[80,768]{1,0:T(8,128)(2,1)} %get-tuple-element.43), channel_id=1, source_target_pairs={{1,2},{2,1},{3,4},{4,3},{5,6},{6,5},{7,8},{8,7},{9,10},{10,9},{11,... | collective-permute-start | bytes 368648 | tf_op jit(solution)/shard_map/ppermute | solution.py:442
  33.4 8.2 %collective-permute-start.3 = (bf16[128,768]{1,0:T(8,128)(2,1)}, bf16[128,768]{1,0:T(8,128)(2,1)S(1)}, u32[]{:S(2)}, u32[]{:S(2)}) collective-permute-start(bf16[128,768]{1,0:T(8,128)(2,1)} %get-tuple-element.47), channel_id=1, source_target_pairs={{0,1},{1,0},{2,3},{3,2},{4,5},{5,4},{6,7},{7,6},{8,9},{9,8},{10,11... | collective-permute-start | bytes 589832 | tf_op jit(solution)/shard_map/ppermute | solution.py:36
  49.2 14.9 %collective-permute-start.16 = (bf16[96,1536]{1,0:T(8,128)(2,1)}, bf16[96,1536]{1,0:T(8,128)(2,1)S(1)}, u32[]{:S(2)}, u32[]{:S(2)}) collective-permute-start(bf16[96,1536]{1,0:T(8,128)(2,1)} %get-tuple-element.64), channel_id=1, source_target_pairs={{0,2},{2,4},{4,6},{6,8},{8,10},{10,12},{12,14},{14,0},{1,3},{3,5},... | collective-permute-start | bytes 884744 | tf_op jit(solution)/shard_map/ppermute | solution.py:422
  51.6 5.9 %collective-permute-start = (bf16[128,768]{1,0:T(8,128)(2,1)}, bf16[128,768]{1,0:T(8,128)(2,1)S(1)}, u32[]{:S(2)}, u32[]{:S(2)}) collective-permute-start(bf16[128,768]{1,0:T(8,128)(2,1)} %get-tuple-element.41), channel_id=1, source_target_pairs={{0,1},{1,0},{2,3},{3,2},{4,5},{5,4},{6,7},{7,6},{8,9},{9,8},{10,11... | collective-permute-start | bytes 589832 | tf_op jit(solution)/shard_map/ppermute | solution.py:36
  62.1 17.3 %collective-permute-start.19 = (bf16[96,1536]{1,0:T(8,128)(2,1)}, bf16[96,1536]{1,0:T(8,128)(2,1)S(1)}, u32[]{:S(2)}, u32[]{:S(2)}) collective-permute-start(bf16[96,1536]{1,0:T(8,128)(2,1)} %get-tuple-element.67), channel_id=1, source_target_pairs={{2,0},{4,2},{6,4},{8,6},{10,8},{12,10},{14,12},{0,14},{3,1},{5,3},... | collective-permute-start | bytes 884744 | tf_op jit(solution)/shard_map/ppermute | solution.py:505
  63.0 8.0 %collective-permute-start.11 = (bf16[96,1536]{1,0:T(8,128)(2,1)S(1)}, bf16[96,1536]{1,0:T(8,128)(2,1)S(1)}, u32[]{:S(2)}, u32[]{:S(2)}) collective-permute-start(bf16[96,1536]{1,0:T(8,128)(2,1)S(1)} %collective-permute-done.9.refs_5_), channel_id=1, source_target_pairs={{0,2},{2,4},{4,6},{6,8},{8,10},{10,12},{12,14},{14,0},{1,3},{3,5},... | collective-permute-start | bytes 884744 | tf_op jit(solution)/shard_map/ppermute | solution.py:504
  65.2 33.4 %collective-permute-start.17 = (bf16[96,1536]{1,0:T(8,128)(2,1)S(1)}, bf16[96,1536]{1,0:T(8,128)(2,1)S(1)}, u32[]{:S(2)}, u32[]{:S(2)}) collective-permute-start(bf16[96,1536]{1,0:T(8,128)(2,1)S(1)} %add_convert_fusion.4), channel_id=1, source_target_pairs={{0,2},{2,4},{4,6},{6,8},{8,10},{10,12},{12,14},{14,0},{1,3},{3,5},... | collective-permute-start | bytes 884744 | tf_op jit(solution)/shard_map/ppermute | solution.py:422
  79.5 18.9 %collective-permute-start.20 = (bf16[96,1536]{1,0:T(8,128)(2,1)S(1)}, bf16[96,1536]{1,0:T(8,128)(2,1)S(1)}, u32[]{:S(2)}, u32[]{:S(2)}) collective-permute-start(bf16[96,1536]{1,0:T(8,128)(2,1)S(1)} %add_convert_fusion.2), channel_id=1, source_target_pairs={{2,0},{4,2},{6,4},{8,6},{10,8},{12,10},{14,12},{0,14},{3,1},{5,3},... | collective-permute-start | bytes 884744 | tf_op jit(solution)/shard_map/ppermute | solution.py:422
  81.6 14.6 %collective-permute-start.14 = (bf16[128,768]{1,0:T(8,128)(2,1)S(1)}, bf16[128,768]{1,0:T(8,128)(2,1)S(1)}, u32[]{:S(2)}, u32[]{:S(2)}) collective-permute-start(bf16[128,768]{1,0:T(8,128)(2,1)S(1)} %get-tuple-element.63), channel_id=1, source_target_pairs={{0,1},{1,0},{2,3},{3,2},{4,5},{5,4},{6,7},{7,6},{8,9},{9,8},{10,11... | collective-permute-start | bytes 589832 | tf_op jit(solution)/shard_map/ppermute | solution.py:36
  83.5 6.2 %collective-permute-start.24 = (bf16[32,768]{1,0:T(8,128)(2,1)S(1)}, bf16[32,768]{1,0:T(8,128)(2,1)S(1)}, u32[]{:S(2)}, u32[]{:S(2)}) collective-permute-start(bf16[32,768]{1,0:T(8,128)(2,1)S(1)} %add_convert_fusion.7), channel_id=1, source_target_pairs={{0,4},{2,6},{4,0},{6,2},{8,12},{10,14},{12,8},{14,10},{1,5},{3,7},... | collective-permute-start | bytes 147464 | tf_op jit(solution)/shard_map/ppermute | solution.py:535
  86.0 14.7 %collective-permute-start.12 = (bf16[128,1536]{1,0:T(8,128)(2,1)S(1)}, bf16[128,1536]{1,0:T(8,128)(2,1)S(1)}, u32[]{:S(2)}, u32[]{:S(2)}) collective-permute-start(bf16[128,1536]{1,0:T(8,128)(2,1)S(1)} %convolution_convert_fusion), channel_id=1, source_target_pairs={{0,1},{1,0},{2,3},{3,2},{4,5},{5,4},{6,7},{7,6},{8,9},{9,8},{10,11... | collective-permute-start | bytes 1179656 | tf_op jit(solution)/shard_map/ppermute | solution.py:36
  89.7 19.7 %collective-permute-start.25 = (bf16[32,768]{1,0:T(8,128)(2,1)S(1)}, bf16[32,768]{1,0:T(8,128)(2,1)S(1)}, u32[]{:S(2)}, u32[]{:S(2)}) collective-permute-start(bf16[32,768]{1,0:T(8,128)(2,1)S(1)} %add_convert_fusion.6), channel_id=1, source_target_pairs={{0,8},{2,10},{4,12},{6,14},{8,0},{10,2},{12,4},{14,6},{1,9},{3,11}... | collective-permute-start | bytes 147464 | tf_op jit(solution)/shard_map/ppermute | solution.py:535
  97.1 17.3 %collective-permute-start.15 = (bf16[1,128,1536]{2,1,0:T(8,128)(2,1)S(1)}, bf16[1,128,1536]{2,1,0:T(8,128)(2,1)S(1)}, u32[]{:S(2)}, u32[]{:S(2)}) collective-permute-start(bf16[1,128,1536]{2,1,0:T(8,128)(2,1)S(1)} %bitcast.24), channel_id=1, source_target_pairs={{16,0},{32,16},{48,32},{64,48},{80,64},{96,80},{112,96},{128,112},... | collective-permute-start | bytes 1179656 | tf_op jit(solution)/shard_map/ppermute | solution.py:42
  98.5 9.8 %collective-permute-start.21 = (bf16[96,1536]{1,0:T(8,128)(2,1)S(1)}, bf16[96,1536]{1,0:T(8,128)(2,1)S(1)}, u32[]{:S(2)}, u32[]{:S(2)}) collective-permute-start(bf16[96,1536]{1,0:T(8,128)(2,1)S(1)} %add_convert_fusion.1), channel_id=1, source_target_pairs={{2,0},{4,2},{6,4},{8,6},{10,8},{12,10},{14,12},{0,14},{3,1},{5,3},... | collective-permute-start | bytes 884744 | tf_op jit(solution)/shard_map/ppermute | solution.py:422
  98.7 16.5 %collective-permute-start.18 = (bf16[96,1536]{1,0:T(8,128)(2,1)S(1)}, bf16[96,1536]{1,0:T(8,128)(2,1)S(1)}, u32[]{:S(2)}, u32[]{:S(2)}) collective-permute-start(bf16[96,1536]{1,0:T(8,128)(2,1)S(1)} %add_convert_fusion.3), channel_id=1, source_target_pairs={{0,2},{2,4},{4,6},{6,8},{8,10},{10,12},{12,14},{14,0},{1,3},{3,5},... | collective-permute-start | bytes 884744 | tf_op jit(solution)/shard_map/ppermute | solution.py:422
  101.3 13.9 %collective-permute-start.13 = (bf16[1,128,1536]{2,1,0:T(8,128)(2,1)S(1)}, bf16[1,128,1536]{2,1,0:T(8,128)(2,1)S(1)}, u32[]{:S(2)}, u32[]{:S(2)}) collective-permute-start(bf16[1,128,1536]{2,1,0:T(8,128)(2,1)S(1)} %fusion.2), channel_id=1, source_target_pairs={{0,16},{16,32},{32,48},{48,64},{64,80},{80,96},{96,112},{112,128},... | collective-permute-start | bytes 1179656 | tf_op jit(solution)/shard_map/ppermute | solution.py:42
  108.4 9.3 %collective-permute-start.22 = (bf16[96,1536]{1,0:T(8,128)(2,1)S(1)}, bf16[96,1536]{1,0:T(8,128)(2,1)S(1)}, u32[]{:S(2)}, u32[]{:S(2)}) collective-permute-start(bf16[96,1536]{1,0:T(8,128)(2,1)S(1)} %add_convert_fusion), channel_id=1, source_target_pairs={{2,0},{4,2},{6,4},{8,6},{10,8},{12,10},{14,12},{0,14},{3,1},{5,3},... | collective-permute-start | bytes 884744 | tf_op jit(solution)/shard_map/ppermute | solution.py:422
  (26 other events, 367.0 us)

commit v5 on v4

--- a/solution.py
+++ b/solution.py
@@ -150,7 +150,7 @@
             theirs_out[pl.ds(at, ROWS), :] = theirs
             return carry
 
-        lax.fori_loop(0, frames // ROWS, body, 0, unroll=4)
+        lax.fori_loop(0, frames // ROWS, body, 0, unroll=8)
 
     copies[0].wait()
     pass_over(saved, own, other, bwd_len)
@@ -213,7 +213,7 @@
 
         return carry
 
-    lax.fori_loop(0, own.shape[1] // LANES, body, 0, unroll=2)
+    lax.fori_loop(0, own.shape[1] // LANES, body, 0, unroll=3)
 
 
 def conv_kernel(
@@ -264,7 +264,7 @@
             hidden_saved[pl.ds(half * frames, frames), lanes] = inner.astype(jnp.bfloat16)
         return carry
 
-    lax.fori_loop(0, chunks, body, 0, unroll=2)
+    lax.fori_loop(0, chunks, body, 0, unroll=3)
     copy.wait()
     depth = len(blocks)
     here = lax.axis_index("z")
@@ -360,7 +360,7 @@
         kernel_grad[KW : KW + 1, lanes] = jnp.zeros((1, LANES), jnp.float32)
         return carry
 
-    lax.fori_loop(0, chunks, body, 0, unroll=2)
+    lax.fori_loop(0, chunks, body, 0, unroll=3)
 
 
 def leave_kernel(block, own, got, saved, grad, gain, out):
@@ -381,7 +381,7 @@
         out[at, :] = back.astype(jnp.bfloat16)
         return carry
 
-    lax.fori_loop(0, saved.shape[0] // ROWS, body, 0, unroll=4)
+    lax.fori_loop(0, saved.shape[0] // ROWS, body, 0, unroll=8)
 
 
 def totals_kernel(block, own, got, kernel, gain, kernel_out, gain_out):

time: 120 us -> 120 us (level)
  no operation moved by 1% of the time
where the time goes in v5:
time: 120 us; the launch traced here: 119 us
  starting transfers between devices  44.7 us (37%)
  waiting for transfers between devices  41.1 us (34%)
  Pallas kernels  25.5 us (21%)
  local copies, waits for them, and re-layouts  4.68 us (4%)
  other arithmetic  1.42 us (1%)
    ppermute x6, waiting for transfers between devices, ring(): lax.ppermute(pair_of[1], 'z', down)  18.4 us
    ppermute x6, starting transfers between devices, ring(): lax.ppermute(pair_of[1], 'z', down)  16.4 us
    ppermute x6, waiting for transfers between devices, partner(): return lax.ppermute(array, 'x', [(0, 1), (1, 0)])  9.83 us
    ppermute x3, starting transfers between devices, per_device(): arrived = lax.ppermute(total, 'z', [(i, i ^ step) for i in range(depth)])  8.58 us
    pallas_call x1, Pallas kernels, per_device(): call(functools.partial(conv_kernel, factor), [*[((rows, width), bf16)] *...  6.71 us
    ppermute x6, starting transfers between devices, ring(): lax.ppermute(pair_of[0], 'z', up)  6.37 us
    pallas_call x1, Pallas kernels, per_device(): call(functools.partial(back_kernel, factor, tuple(places)), [((frames, ha...  5.91 us
    unnamed x47, local copies, waits for them, and re-layouts  4.68 us
  transfers between devices with their start and end apart: 27, of which 11 were waited for; matrix products, arithmetic and copies ran while one was open for 2% of the time, Pallas kernels for 21%

profile of v5, /device:TPU:2, one launch (start us, length us, event | category | flops | bytes accessed | tf_op | source)
XLA Modules:
  0.0 119.4 jit_solution(10087199706497197171)
XLA Ops:
  0.6 5.9 %collective-permute-start.6 = (bf16[96,1536]{1,0:T(8,128)(2,1)}, bf16[96,1536]{1,0:T(8,128)(2,1)S(1)}, u32[]{:S(2)}, u32[]{:S(2)}) collective-permute-start(bf16[96,1536]{1,0:T(8,128)(2,1)} %bitcast.25), channel_id=1, source_target_pairs={{2,0},{4,2},{6,4},{8,6},{10,8},{12,10},{14,12},{0,14},{3,1},{5,3},... | collective-permute-start | bytes 884744 | tf_op jit(solution)/shard_map/ppermute | solution.py:422
  6.6 6.6 %collective-permute-done.6.refs_2_ = bf16[96,1536]{1,0:T(8,128)(2,1)S(1)} collective-permute-done((bf16[96,1536]{1,0:T(8,128)(2,1)}, bf16[96,1536]{1,0:T(8,128)(2,1)S(1)}, u32[]{:S(2)}, u32[]{:S(2)}) %collective-permute-start.6) | collective-permute-done | bytes 294944 | tf_op jit(solution)/shard_map/ppermute | solution.py:422
  13.1 3.6 %collective-permute-start.8 = (bf16[96,1536]{1,0:T(8,128)(2,1)S(1)}, bf16[96,1536]{1,0:T(8,128)(2,1)S(1)}, u32[]{:S(2)}, u32[]{:S(2)}) collective-permute-start(bf16[96,1536]{1,0:T(8,128)(2,1)S(1)} %collective-permute-done.6.refs_2_), channel_id=1, source_target_pairs={{2,0},{4,2},{6,4},{8,6},{10,8},{12,10},{14,12},{0,14},{3,1},{5,3},... | collective-permute-start | bytes 884744 | tf_op jit(solution)/shard_map/ppermute | solution.py:422
  17.3 4.9 %collective-permute-done.8.refs_4_ = bf16[96,1536]{1,0:T(8,128)(2,1)S(1)} collective-permute-done((bf16[96,1536]{1,0:T(8,128)(2,1)S(1)}, bf16[96,1536]{1,0:T(8,128)(2,1)S(1)}, u32[]{:S(2)}, u32[]{:S(2)}) %collective-permute-start.8) | collective-permute-done | bytes 294944 | tf_op jit(solution)/shard_map/ppermute | solution.py:422
  22.1 3.7 %collective-permute-start.10 = (bf16[96,1536]{1,0:T(8,128)(2,1)S(1)}, bf16[96,1536]{1,0:T(8,128)(2,1)S(1)}, u32[]{:S(2)}, u32[]{:S(2)}) collective-permute-start(bf16[96,1536]{1,0:T(8,128)(2,1)S(1)} %collective-permute-done.8.refs_4_), channel_id=1, source_target_pairs={{2,0},{4,2},{6,4},{8,6},{10,8},{12,10},{14,12},{0,14},{3,1},{5,3},... | collective-permute-start | bytes 884744 | tf_op jit(solution)/shard_map/ppermute | solution.py:422
  27.9 2.1 %collective-permute-start.1 = (bf16[80,768]{1,0:T(8,128)(2,1)}, bf16[80,768]{1,0:T(8,128)(2,1)S(1)}, u32[]{:S(2)}, u32[]{:S(2)}) collective-permute-start(bf16[80,768]{1,0:T(8,128)(2,1)} %get-tuple-element.43), channel_id=1, source_target_pairs={{1,2},{2,1},{3,4},{4,3},{5,6},{6,5},{7,8},{8,7},{9,10},{10,9},{11,... | collective-permute-start | bytes 368648 | tf_op jit(solution)/shard_map/ppermute | solution.py:442
  29.9 3.3 %shard_map.119 = (bf16[128,768]{1,0:T(8,128)(2,1)}, bf16[128,768]{1,0:T(8,128)(2,1)}, bf16[128,768]{1,0:T(8,128)(2,1)}, bf16[128,768]{1,0:T(8,128)(2,1)}, f32[32,768]{1,0:T(8,128)}) custom-call(s32[1,2]{1,0:T(1,128)} %plan.1, s32[32]{0:T(128)} %lengths.1, bf16[128,1536]{1,0:T(8,128)(2,1)} %bitcast.16, bf16[128,1536]{1,0:T(8,128)(2,1)} %bitcast.29, ...), custom_call_target="tpu_custom_call" | custom-call | flops 4718592 | bytes 1966080 | tf_op jit(solution)/shard_map/pallas_call | solution.py:450
  33.4 2.6 %collective-permute-done.1.near = bf16[80,768]{1,0:T(8,128)(2,1)S(1)} collective-permute-done((bf16[80,768]{1,0:T(8,128)(2,1)}, bf16[80,768]{1,0:T(8,128)(2,1)S(1)}, u32[]{:S(2)}, u32[]{:S(2)}) %collective-permute-start.1) | collective-permute-done | bytes 122912 | tf_op jit(solution)/shard_map/ppermute | solution.py:442
  36.0 2.8 %collective-permute-start.2 = (bf16[80,768]{1,0:T(8,128)(2,1)}, bf16[80,768]{1,0:T(8,128)(2,1)S(1)}, u32[]{:S(2)}, u32[]{:S(2)}) collective-permute-start(bf16[80,768]{1,0:T(8,128)(2,1)} %get-tuple-element.44), channel_id=1, source_target_pairs={{1,3},{2,0},{3,5},{4,2},{5,7},{6,4},{7,9},{8,6},{9,11},{10,8},{11,... | collective-permute-start | bytes 368648 | tf_op jit(solution)/shard_map/ppermute | solution.py:444
  38.8 2.7 %collective-permute-done.2.far = bf16[80,768]{1,0:T(8,128)(2,1)S(1)} collective-permute-done((bf16[80,768]{1,0:T(8,128)(2,1)}, bf16[80,768]{1,0:T(8,128)(2,1)S(1)}, u32[]{:S(2)}, u32[]{:S(2)}) %collective-permute-start.2) | collective-permute-done | bytes 122912 | tf_op jit(solution)/shard_map/ppermute | solution.py:444
  42.3 6.7 %shard_map.122 = (bf16[96,1536]{1,0:T(8,128)(2,1)}, bf16[96,1536]{1,0:T(8,128)(2,1)}, bf16[96,1536]{1,0:T(8,128)(2,1)}, bf16[96,1536]{1,0:T(8,128)(2,1)}, bf16[9...) custom-call(bf16[128,768]{1,0:T(8,128)(2,1)} %get-tuple-element.46.o, ...), custom_call_target="tpu_custom_call" | custom-call | flops 24379392 | bytes 3145728 | tf_op jit(solution)/shard_map/pallas_call | solution.py:471
  49.1 2.4 %collective-permute-start.16 = (bf16[96,1536]{1,0:T(8,128)(2,1)}, bf16[96,1536]{1,0:T(8,128)(2,1)S(1)}, u32[]{:S(2)}, u32[]{:S(2)}) collective-permute-start(bf16[96,1536]{1,0:T(8,128)(2,1)} %get-tuple-element.64), channel_id=1, source_target_pairs={{0,2},{2,4},{4,6},{6,8},{8,10},{10,12},{12,14},{14,0},{1,3},{3,5},... | collective-permute-start | bytes 884744 | tf_op jit(solution)/shard_map/ppermute | solution.py:422
  51.6 5.7 %collective-permute-done.got = bf16[128,768]{1,0:T(8,128)(2,1)S(1)} collective-permute-done((bf16[128,768]{1,0:T(8,128)(2,1)}, bf16[128,768]{1,0:T(8,128)(2,1)S(1)}, u32[]{:S(2)}, u32[]{:S(2)}) %collective-permute-start) | collective-permute-done | bytes 196640 | tf_op jit(solution)/shard_map/ppermute | solution.py:36
  58.0 3.9 %shard_map.121 = (bf16[128,768]{1,0:T(8,128)(2,1)}, bf16[128,768]{1,0:T(8,128)(2,1)}) custom-call(bf16[128,768]{1,0:T(8,128)(2,1)} %get-tuple-element.40.own, bf16[128,768]{1,0:T(8,128)(2,1)} %copy-done.22, f32[32,768]{1,0:T(8,128)} %get-tuple-element.42.taps, bf16[80,768]{1,0:T(8,128)(2,1)} %copy-done.12, bf16[80,768]{1,0:T(8,128)(2,1)} %copy-done.13), custom_call_target="tpu_custom_call" | custom-call | flops 12189696 | bytes 1572864 | tf_op jit(solution)/shard_map/pallas_call | solution.py:490
  67.0 3.9 %collective-permute-done.11.refs_7_ = bf16[96,1536]{1,0:T(8,128)(2,1)S(1)} collective-permute-done((bf16[96,1536]{1,0:T(8,128)(2,1)S(1)}, bf16[96,1536]{1,0:T(8,128)(2,1)S(1)}, u32[]{:S(2)}, u32[]{:S(2)}) %collective-permute-start.11) | collective-permute-done | bytes 294944 | tf_op jit(solution)/shard_map/ppermute | solution.py:504
  73.2 5.9 %shard_map.123 = (bf16[128,768]{1,0:T(8,128)(2,1)S(1)}, bf16[128,768]{1,0:T(8,128)(2,1)S(1)}, f32[32,768]{1,0:T(8,128)S(1)}, bf16[768,1536]{1,0:T(8,128)(2,1)S(1)}) custom-call(s32[1,2]{1,0:T(1,128)S(1)} %copy-done.9, s32[32]{0:T(128)S(1)} %copy-done.10, bf16[288,1536]{1,0:T(8,128)(2,1)S(1)} %copy-done.3, bf16[608,768]{1,0:T(8,128)(2,1)S(1)} %copy-done.2, ...), custom_call_target="tpu_custom_call" | custom-call | flops 24379392 | bytes 2359296 | tf_op jit(solution)/shard_map/pallas_call | solution.py:514
  79.4 2.1 %collective-permute-start.20 = (bf16[96,1536]{1,0:T(8,128)(2,1)S(1)}, bf16[96,1536]{1,0:T(8,128)(2,1)S(1)}, u32[]{:S(2)}, u32[]{:S(2)}) collective-permute-start(bf16[96,1536]{1,0:T(8,128)(2,1)S(1)} %add_convert_fusion.2), channel_id=1, source_target_pairs={{2,0},{4,2},{6,4},{8,6},{10,8},{12,10},{14,12},{0,14},{3,1},{5,3},... | collective-permute-start | bytes 884744 | tf_op jit(solution)/shard_map/ppermute | solution.py:422
  86.2 3.3 %collective-permute-done.24 = bf16[32,768]{1,0:T(8,128)(2,1)S(1)} collective-permute-done((bf16[32,768]{1,0:T(8,128)(2,1)S(1)}, bf16[32,768]{1,0:T(8,128)(2,1)S(1)}, u32[]{:S(2)}, u32[]{:S(2)}) %collective-permute-start.24) | collective-permute-done | bytes 49184 | tf_op jit(solution)/shard_map/ppermute | solution.py:535
  89.5 6.5 %collective-permute-start.25 = (bf16[32,768]{1,0:T(8,128)(2,1)S(1)}, bf16[32,768]{1,0:T(8,128)(2,1)S(1)}, u32[]{:S(2)}, u32[]{:S(2)}) collective-permute-start(bf16[32,768]{1,0:T(8,128)(2,1)S(1)} %add_convert_fusion.6), channel_id=1, source_target_pairs={{0,8},{2,10},{4,12},{6,14},{8,0},{10,2},{12,4},{14,6},{1,9},{3,11}... | collective-permute-start | bytes 147464 | tf_op jit(solution)/shard_map/ppermute | solution.py:535
  98.8 2.1 %collective-permute-start.18 = (bf16[96,1536]{1,0:T(8,128)(2,1)S(1)}, bf16[96,1536]{1,0:T(8,128)(2,1)S(1)}, u32[]{:S(2)}, u32[]{:S(2)}) collective-permute-start(bf16[96,1536]{1,0:T(8,128)(2,1)S(1)} %add_convert_fusion.3), channel_id=1, source_target_pairs={{0,2},{2,4},{4,6},{6,8},{8,10},{10,12},{12,14},{14,0},{1,3},{3,5},... | collective-permute-start | bytes 884744 | tf_op jit(solution)/shard_map/ppermute | solution.py:422
  101.4 2.5 %collective-permute-start.13 = (bf16[1,128,1536]{2,1,0:T(8,128)(2,1)S(1)}, bf16[1,128,1536]{2,1,0:T(8,128)(2,1)S(1)}, u32[]{:S(2)}, u32[]{:S(2)}) collective-permute-start(bf16[1,128,1536]{2,1,0:T(8,128)(2,1)S(1)} %fusion.2), channel_id=1, source_target_pairs={{0,16},{16,32},{32,48},{48,64},{64,80},{80,96},{96,112},{112,128},... | collective-permute-start | bytes 1179656 | tf_op jit(solution)/shard_map/ppermute | solution.py:42
  103.9 4.5 %collective-permute-done.21 = bf16[96,1536]{1,0:T(8,128)(2,1)S(1)} collective-permute-done((bf16[96,1536]{1,0:T(8,128)(2,1)S(1)}, bf16[96,1536]{1,0:T(8,128)(2,1)S(1)}, u32[]{:S(2)}, u32[]{:S(2)}) %collective-permute-start.21) | collective-permute-done | bytes 294944 | tf_op jit(solution)/shard_map/ppermute | solution.py:422
  109.6 4.1 %collective-permute-done.26.got = bf16[32,768]{1,0:T(8,128)(2,1)S(1)} collective-permute-done((bf16[32,768]{1,0:T(8,128)(2,1)S(1)}, bf16[32,768]{1,0:T(8,128)(2,1)S(1)}, u32[]{:S(2)}, u32[]{:S(2)}) %collective-permute-start.26) | collective-permute-done | bytes 49184 | tf_op jit(solution)/shard_map/ppermute | solution.py:36
  115.3 2.4 %collective-permute-done.22.second = bf16[96,1536]{1,0:T(8,128)(2,1)S(1)} collective-permute-done((bf16[96,1536]{1,0:T(8,128)(2,1)S(1)}, bf16[96,1536]{1,0:T(8,128)(2,1)S(1)}, u32[]{:S(2)}, u32[]{:S(2)}) %collective-permute-start.22) | collective-permute-done | bytes 294944 | tf_op jit(solution)/shard_map/ppermute | solution.py:422
  (97 shorter events, 24.2 us)
Async XLA Ops:
  0.6 12.5 %collective-permute-start.6 = (bf16[96,1536]{1,0:T(8,128)(2,1)}, bf16[96,1536]{1,0:T(8,128)(2,1)S(1)}, u32[]{:S(2)}, u32[]{:S(2)}) collective-permute-start(bf16[96,1536]{1,0:T(8,128)(2,1)} %bitcast.25), channel_id=1, source_target_pairs={{2,0},{4,2},{6,4},{8,6},{10,8},{12,10},{14,12},{0,14},{3,1},{5,3},... | collective-permute-start | bytes 884744 | tf_op jit(solution)/shard_map/ppermute | solution.py:422
  6.6 10.2 %collective-permute-start.5 = (bf16[96,1536]{1,0:T(8,128)(2,1)}, bf16[96,1536]{1,0:T(8,128)(2,1)S(1)}, u32[]{:S(2)}, u32[]{:S(2)}) collective-permute-start(bf16[96,1536]{1,0:T(8,128)(2,1)} %bitcast.26), channel_id=1, source_target_pairs={{0,2},{2,4},{4,6},{6,8},{8,10},{10,12},{12,14},{14,0},{1,3},{3,5},... | collective-permute-start | bytes 884744 | tf_op jit(solution)/shard_map/ppermute | solution.py:422
  13.1 9.0 %collective-permute-start.8 = (bf16[96,1536]{1,0:T(8,128)(2,1)S(1)}, bf16[96,1536]{1,0:T(8,128)(2,1)S(1)}, u32[]{:S(2)}, u32[]{:S(2)}) collective-permute-start(bf16[96,1536]{1,0:T(8,128)(2,1)S(1)} %collective-permute-done.6.refs_2_), channel_id=1, source_target_pairs={{2,0},{4,2},{6,4},{8,6},{10,8},{12,10},{14,12},{0,14},{3,1},{5,3},... | collective-permute-start | bytes 884744 | tf_op jit(solution)/shard_map/ppermute | solution.py:422
  16.7 9.1 %collective-permute-start.7 = (bf16[96,1536]{1,0:T(8,128)(2,1)S(1)}, bf16[96,1536]{1,0:T(8,128)(2,1)S(1)}, u32[]{:S(2)}, u32[]{:S(2)}) collective-permute-start(bf16[96,1536]{1,0:T(8,128)(2,1)S(1)} %collective-permute-done.5.refs_1_), channel_id=1, source_target_pairs={{0,2},{2,4},{4,6},{6,8},{8,10},{10,12},{12,14},{14,0},{1,3},{3,5},... | collective-permute-start | bytes 884744 | tf_op jit(solution)/shard_map/ppermute | solution.py:422
  16.7 24.8 %collective-permute-start.4 = (bf16[128,1536]{1,0:T(8,128)(2,1)}, bf16[128,1536]{1,0:T(8,128)(2,1)S(1)}, u32[]{:S(2)}, u32[]{:S(2)}) collective-permute-start(bf16[128,1536]{1,0:T(8,128)(2,1)} %bitcast.18), channel_id=1, source_target_pairs={{0,1},{1,0},{2,3},{3,2},{4,5},{5,4},{6,7},{7,6},{8,9},{9,8},{10,11... | collective-permute-start | bytes 1179656 | tf_op jit(solution)/shard_map/ppermute | solution.py:36
  22.1 26.9 %collective-permute-start.10 = (bf16[96,1536]{1,0:T(8,128)(2,1)S(1)}, bf16[96,1536]{1,0:T(8,128)(2,1)S(1)}, u32[]{:S(2)}, u32[]{:S(2)}) collective-permute-start(bf16[96,1536]{1,0:T(8,128)(2,1)S(1)} %collective-permute-done.8.refs_4_), channel_id=1, source_target_pairs={{2,0},{4,2},{6,4},{8,6},{10,8},{12,10},{14,12},{0,14},{3,1},{5,3},... | collective-permute-start | bytes 884744 | tf_op jit(solution)/shard_map/ppermute | solution.py:422
  25.8 23.2 %collective-permute-start.9 = (bf16[96,1536]{1,0:T(8,128)(2,1)S(1)}, bf16[96,1536]{1,0:T(8,128)(2,1)S(1)}, u32[]{:S(2)}, u32[]{:S(2)}) collective-permute-start(bf16[96,1536]{1,0:T(8,128)(2,1)S(1)} %collective-permute-done.7.refs_3_), channel_id=1, source_target_pairs={{0,2},{2,4},{4,6},{6,8},{8,10},{10,12},{12,14},{14,0},{1,3},{3,5},... | collective-permute-start | bytes 884744 | tf_op jit(solution)/shard_map/ppermute | solution.py:422
  27.9 8.1 %collective-permute-start.1 = (bf16[80,768]{1,0:T(8,128)(2,1)}, bf16[80,768]{1,0:T(8,128)(2,1)S(1)}, u32[]{:S(2)}, u32[]{:S(2)}) collective-permute-start(bf16[80,768]{1,0:T(8,128)(2,1)} %get-tuple-element.43), channel_id=1, source_target_pairs={{1,2},{2,1},{3,4},{4,3},{5,6},{6,5},{7,8},{8,7},{9,10},{10,9},{11,... | collective-permute-start | bytes 368648 | tf_op jit(solution)/shard_map/ppermute | solution.py:442
  33.3 8.2 %collective-permute-start.3 = (bf16[128,768]{1,0:T(8,128)(2,1)}, bf16[128,768]{1,0:T(8,128)(2,1)S(1)}, u32[]{:S(2)}, u32[]{:S(2)}) collective-permute-start(bf16[128,768]{1,0:T(8,128)(2,1)} %get-tuple-element.47), channel_id=1, source_target_pairs={{0,1},{1,0},{2,3},{3,2},{4,5},{5,4},{6,7},{7,6},{8,9},{9,8},{10,11... | collective-permute-start | bytes 589832 | tf_op jit(solution)/shard_map/ppermute | solution.py:36
  49.1 14.9 %collective-permute-start.16 = (bf16[96,1536]{1,0:T(8,128)(2,1)}, bf16[96,1536]{1,0:T(8,128)(2,1)S(1)}, u32[]{:S(2)}, u32[]{:S(2)}) collective-permute-start(bf16[96,1536]{1,0:T(8,128)(2,1)} %get-tuple-element.64), channel_id=1, source_target_pairs={{0,2},{2,4},{4,6},{6,8},{8,10},{10,12},{12,14},{14,0},{1,3},{3,5},... | collective-permute-start | bytes 884744 | tf_op jit(solution)/shard_map/ppermute | solution.py:422
  51.5 5.9 %collective-permute-start = (bf16[128,768]{1,0:T(8,128)(2,1)}, bf16[128,768]{1,0:T(8,128)(2,1)S(1)}, u32[]{:S(2)}, u32[]{:S(2)}) collective-permute-start(bf16[128,768]{1,0:T(8,128)(2,1)} %get-tuple-element.41), channel_id=1, source_target_pairs={{0,1},{1,0},{2,3},{3,2},{4,5},{5,4},{6,7},{7,6},{8,9},{9,8},{10,11... | collective-permute-start | bytes 589832 | tf_op jit(solution)/shard_map/ppermute | solution.py:36
  61.9 17.4 %collective-permute-start.19 = (bf16[96,1536]{1,0:T(8,128)(2,1)}, bf16[96,1536]{1,0:T(8,128)(2,1)S(1)}, u32[]{:S(2)}, u32[]{:S(2)}) collective-permute-start(bf16[96,1536]{1,0:T(8,128)(2,1)} %get-tuple-element.67), channel_id=1, source_target_pairs={{2,0},{4,2},{6,4},{8,6},{10,8},{12,10},{14,12},{0,14},{3,1},{5,3},... | collective-permute-start | bytes 884744 | tf_op jit(solution)/shard_map/ppermute | solution.py:505
  62.9 8.0 %collective-permute-start.11 = (bf16[96,1536]{1,0:T(8,128)(2,1)S(1)}, bf16[96,1536]{1,0:T(8,128)(2,1)S(1)}, u32[]{:S(2)}, u32[]{:S(2)}) collective-permute-start(bf16[96,1536]{1,0:T(8,128)(2,1)S(1)} %collective-permute-done.9.refs_5_), channel_id=1, source_target_pairs={{0,2},{2,4},{4,6},{6,8},{8,10},{10,12},{12,14},{14,0},{1,3},{3,5},... | collective-permute-start | bytes 884744 | tf_op jit(solution)/shard_map/ppermute | solution.py:504
  65.1 33.6 %collective-permute-start.17 = (bf16[96,1536]{1,0:T(8,128)(2,1)S(1)}, bf16[96,1536]{1,0:T(8,128)(2,1)S(1)}, u32[]{:S(2)}, u32[]{:S(2)}) collective-permute-start(bf16[96,1536]{1,0:T(8,128)(2,1)S(1)} %add_convert_fusion.4), channel_id=1, source_target_pairs={{0,2},{2,4},{4,6},{6,8},{8,10},{10,12},{12,14},{14,0},{1,3},{3,5},... | collective-permute-start | bytes 884744 | tf_op jit(solution)/shard_map/ppermute | solution.py:422
  79.4 19.1 %collective-permute-start.20 = (bf16[96,1536]{1,0:T(8,128)(2,1)S(1)}, bf16[96,1536]{1,0:T(8,128)(2,1)S(1)}, u32[]{:S(2)}, u32[]{:S(2)}) collective-permute-start(bf16[96,1536]{1,0:T(8,128)(2,1)S(1)} %add_convert_fusion.2), channel_id=1, source_target_pairs={{2,0},{4,2},{6,4},{8,6},{10,8},{12,10},{14,12},{0,14},{3,1},{5,3},... | collective-permute-start | bytes 884744 | tf_op jit(solution)/shard_map/ppermute | solution.py:422
  81.5 14.6 %collective-permute-start.14 = (bf16[128,768]{1,0:T(8,128)(2,1)S(1)}, bf16[128,768]{1,0:T(8,128)(2,1)S(1)}, u32[]{:S(2)}, u32[]{:S(2)}) collective-permute-start(bf16[128,768]{1,0:T(8,128)(2,1)S(1)} %get-tuple-element.63), channel_id=1, source_target_pairs={{0,1},{1,0},{2,3},{3,2},{4,5},{5,4},{6,7},{7,6},{8,9},{9,8},{10,11... | collective-permute-start | bytes 589832 | tf_op jit(solution)/shard_map/ppermute | solution.py:36
  83.4 6.1 %collective-permute-start.24 = (bf16[32,768]{1,0:T(8,128)(2,1)S(1)}, bf16[32,768]{1,0:T(8,128)(2,1)S(1)}, u32[]{:S(2)}, u32[]{:S(2)}) collective-permute-start(bf16[32,768]{1,0:T(8,128)(2,1)S(1)} %add_convert_fusion.7), channel_id=1, source_target_pairs={{0,4},{2,6},{4,0},{6,2},{8,12},{10,14},{12,8},{14,10},{1,5},{3,7},... | collective-permute-start | bytes 147464 | tf_op jit(solution)/shard_map/ppermute | solution.py:535
  85.9 15.0 %collective-permute-start.12 = (bf16[128,1536]{1,0:T(8,128)(2,1)S(1)}, bf16[128,1536]{1,0:T(8,128)(2,1)S(1)}, u32[]{:S(2)}, u32[]{:S(2)}) collective-permute-start(bf16[128,1536]{1,0:T(8,128)(2,1)S(1)} %convolution_convert_fusion), channel_id=1, source_target_pairs={{0,1},{1,0},{2,3},{3,2},{4,5},{5,4},{6,7},{7,6},{8,9},{9,8},{10,11... | collective-permute-start | bytes 1179656 | tf_op jit(solution)/shard_map/ppermute | solution.py:36
  89.5 20.0 %collective-permute-start.25 = (bf16[32,768]{1,0:T(8,128)(2,1)S(1)}, bf16[32,768]{1,0:T(8,128)(2,1)S(1)}, u32[]{:S(2)}, u32[]{:S(2)}) collective-permute-start(bf16[32,768]{1,0:T(8,128)(2,1)S(1)} %add_convert_fusion.6), channel_id=1, source_target_pairs={{0,8},{2,10},{4,12},{6,14},{8,0},{10,2},{12,4},{14,6},{1,9},{3,11}... | collective-permute-start | bytes 147464 | tf_op jit(solution)/shard_map/ppermute | solution.py:535
  97.2 17.3 %collective-permute-start.15 = (bf16[1,128,1536]{2,1,0:T(8,128)(2,1)S(1)}, bf16[1,128,1536]{2,1,0:T(8,128)(2,1)S(1)}, u32[]{:S(2)}, u32[]{:S(2)}) collective-permute-start(bf16[1,128,1536]{2,1,0:T(8,128)(2,1)S(1)} %bitcast.24), channel_id=1, source_target_pairs={{16,0},{32,16},{48,32},{64,48},{80,64},{96,80},{112,96},{128,112},... | collective-permute-start | bytes 1179656 | tf_op jit(solution)/shard_map/ppermute | solution.py:42
  98.6 9.8 %collective-permute-start.21 = (bf16[96,1536]{1,0:T(8,128)(2,1)S(1)}, bf16[96,1536]{1,0:T(8,128)(2,1)S(1)}, u32[]{:S(2)}, u32[]{:S(2)}) collective-permute-start(bf16[96,1536]{1,0:T(8,128)(2,1)S(1)} %add_convert_fusion.1), channel_id=1, source_target_pairs={{2,0},{4,2},{6,4},{8,6},{10,8},{12,10},{14,12},{0,14},{3,1},{5,3},... | collective-permute-start | bytes 884744 | tf_op jit(solution)/shard_map/ppermute | solution.py:422
  98.8 16.5 %collective-permute-start.18 = (bf16[96,1536]{1,0:T(8,128)(2,1)S(1)}, bf16[96,1536]{1,0:T(8,128)(2,1)S(1)}, u32[]{:S(2)}, u32[]{:S(2)}) collective-permute-start(bf16[96,1536]{1,0:T(8,128)(2,1)S(1)} %add_convert_fusion.3), channel_id=1, source_target_pairs={{0,2},{2,4},{4,6},{6,8},{8,10},{10,12},{12,14},{14,0},{1,3},{3,5},... | collective-permute-start | bytes 884744 | tf_op jit(solution)/shard_map/ppermute | solution.py:422
  101.4 13.9 %collective-permute-start.13 = (bf16[1,128,1536]{2,1,0:T(8,128)(2,1)S(1)}, bf16[1,128,1536]{2,1,0:T(8,128)(2,1)S(1)}, u32[]{:S(2)}, u32[]{:S(2)}) collective-permute-start(bf16[1,128,1536]{2,1,0:T(8,128)(2,1)S(1)} %fusion.2), channel_id=1, source_target_pairs={{0,16},{16,32},{32,48},{48,64},{64,80},{80,96},{96,112},{112,128},... | collective-permute-start | bytes 1179656 | tf_op jit(solution)/shard_map/ppermute | solution.py:42
  108.5 9.3 %collective-permute-start.22 = (bf16[96,1536]{1,0:T(8,128)(2,1)S(1)}, bf16[96,1536]{1,0:T(8,128)(2,1)S(1)}, u32[]{:S(2)}, u32[]{:S(2)}) collective-permute-start(bf16[96,1536]{1,0:T(8,128)(2,1)S(1)} %add_convert_fusion), channel_id=1, source_target_pairs={{2,0},{4,2},{6,4},{8,6},{10,8},{12,10},{14,12},{0,14},{3,1},{5,3},... | collective-permute-start | bytes 884744 | tf_op jit(solution)/shard_map/ppermute | solution.py:422
  (26 other events, 367.4 us)
